TPU v7x, 32 devices: a whole 2x2x4 slice. The times are simulated.
32 devices in a mesh: groups: 2 (over y), seq: 4 (over z), batch: 2 (over x), head: 2 (over core).
Axes of the slice: x: 2, y: 2, z: 4, core: 2. Of those that a mesh axis runs over, the one named last changes fastest.
Arguments:
- query_in: bfloat16 [4, 2048, 1024], P(('groups', 'batch'), 'seq', 'head'), parts along dimension 0, may hold values from -1.5 to 1.5
- key_in: bfloat16 [4, 2048, 1024], P(('groups', 'batch'), 'seq', 'head'), parts along dimension 0, may hold values from -1.5 to 1.5
- value_in: bfloat16 [4, 2048, 1024], P(('groups', 'batch'), 'seq', 'head'), parts along dimension 0, may hold values from -6 to 6
- level_mask: int32 [4, 2048, 16], P(('groups', 'batch'), 'seq'), parts along dimension 0, may hold values 0 or 1
- out_weight: bfloat16 [1024, 2048], P('head'), may hold values from -0.1875 to 0.1875
- grad_out: bfloat16 [4, 2048, 2048], P(('groups', 'batch'), 'seq', 'head'), parts along dimension 0, may hold values from -0.8984375 to 0.8984375
Outputs:
- layer_out: bfloat16 [4, 2048, 2048], P(('groups', 'batch'), 'seq', 'head'), parts along dimension 0
- grad_query: bfloat16 [4, 2048, 1024], P(('groups', 'batch'), 'seq', 'head'), parts along dimension 0
- grad_key: bfloat16 [4, 2048, 1024], P(('groups', 'batch'), 'seq', 'head'), parts along dimension 0
- grad_value: bfloat16 [4, 2048, 1024], P(('groups', 'batch'), 'seq', 'head'), parts along dimension 0
There are 2 independent parts, one for each index of `groups`. A program takes and returns all parts, laid end to end along the dimension named above; an argument that names none is the same for every part. Nothing has to cross between parts.
All inputs are finite; a program needn't handle non-finite values. No bound on the sum of `level_mask` on one device may be relied on, other than what follows from the above.
Results may differ from a plain program's by a relative error of at most 0.0091.
Values may be sent and summed in bfloat16 or wider, within the bound.
No kernel may reach another device: no remote copies, remote signals or barrier semaphores. Data moves between devices by JAX's collectives and lax.ppermute only.
A program may use at most 64 MiB of HBM per device.

v0:
```python
import jax
import jax.numpy as jnp
import numpy as np
from jax import lax
from jax.sharding import PartitionSpec as P

HEAD_DIM = 128


level_scale = np.array(
    [1.0] + [2.0 ** (-(tier - 1) / 2.0) for tier in range(1, 16)], dtype=np.float32
)
HIGHEST = lax.Precision.HIGHEST


def from_partner(block, axis, stride):
    count = lax.axis_size(axis)
    route = []
    for low in range(count):
        high = low | 1 << stride
        if high != low and high < count:
            route += [(low, high), (high, low)]
    return lax.ppermute(block, axis, route)


def top_bit(values):
    result = jnp.zeros_like(values)
    for power in range(1, 24):
        result = result + (values >= 1 << power).astype(jnp.int32)
    return result


def block_levels(count):
    rows = jnp.arange(count, dtype=jnp.int32)
    later = rows[:, None]
    earlier = rows[None, :]
    spread = jnp.bitwise_xor(later, earlier)
    depth_map = jnp.where(spread == 0, 0, 1 + top_bit(jnp.maximum(spread, 1)))
    inside = earlier <= later
    return jnp.stack(
        [((depth_map == tier) & inside).astype(jnp.float32) for tier in range(count.bit_length())]
    )


def reverse_tree_alt(reach, position, span):
    back = jnp.zeros_like(reach[0])
    pending = reach
    for bit_pos in range(span):
        other_up = from_partner(pending, "seq", bit_pos)
        lower = position >> bit_pos & 1 == 0
        back = back + jnp.where(lower, other_up[0], 0.0)
        pending = pending[1:] + other_up[1:]
    return back


def on_device(query_in, key_in, value_in, level_mask, out_weight, grad_out):
    batch_rows, length, width = query_in.shape
    heads = width // HEAD_DIM
    shape_heads = (batch_rows, length, heads, HEAD_DIM)
    query_rows = query_in.reshape(shape_heads)
    key_rows = key_in.reshape(shape_heads)
    value_rows = value_in.reshape(shape_heads)
    weights = level_mask.astype(jnp.float32) * jnp.asarray(level_scale, dtype=jnp.float32)
    tiers = length.bit_length()
    span = lax.axis_size("seq").bit_length() - 1
    position = lax.axis_index("seq")
    tier_weight = weights[:, :, tiers : tiers + span]
    grad_mixed = jnp.einsum(
        "bte,fe->btf",
        lax.all_gather(grad_out, "head", axis=2, tiled=True),
        out_weight,
        preferred_element_type=jnp.float32,
    ).astype(jnp.bfloat16)
    grad_rows = grad_mixed.reshape(shape_heads)
    block_state = jnp.einsum(
        "bthd,bthe->bhde", key_rows, value_rows, preferred_element_type=jnp.float32
    )
    weighted_query = (
        jnp.transpose(tier_weight, (2, 0, 1))[:, :, :, None, None] * query_rows[None]
    ).astype(jnp.bfloat16)
    reach = jnp.einsum(
        "jbthd,bthe->jbhde", weighted_query, grad_rows, preferred_element_type=jnp.float32
    )
    piece = lax.all_gather(block_state[None], "seq", axis=0, tiled=True)
    sources = jnp.arange(piece.shape[0], dtype=jnp.int32)
    tier_of = top_bit(jnp.maximum(jnp.bitwise_xor(sources, position), 1))
    picks = (sources < position)[None, :] & (
        tier_of[None, :] == jnp.arange(span, dtype=jnp.int32)[:, None]
    )
    states = jnp.einsum("jn,nbhde->jbhde", picks.astype(jnp.float32), piece, precision=HIGHEST)
    back = reverse_tree_alt(reach, position, span)
    states_low = states.astype(jnp.bfloat16)
    back_low = back.astype(jnp.bfloat16)
    intra_map = block_levels(length)
    blend = jnp.einsum("lts,btl->bts", intra_map, weights[:, :, :tiers], precision=HIGHEST)
    scores = jnp.einsum("bthd,bshd->bhts", query_rows, key_rows, preferred_element_type=jnp.float32)
    probs = (scores * blend[:, None]).astype(jnp.bfloat16)
    local_out = jnp.einsum("bhts,bshd->bthd", probs, value_rows, preferred_element_type=jnp.float32)
    far_out = jnp.einsum(
        "jbthd,jbhde->bthe", weighted_query, states_low, preferred_element_type=jnp.float32
    )
    mixed = (local_out + far_out).astype(jnp.bfloat16).reshape(batch_rows, length, width)
    partial_out = jnp.einsum("btf,fe->bte", mixed, out_weight, preferred_element_type=jnp.float32)
    layer_out = lax.psum_scatter(partial_out, "head", scatter_dimension=2, tiled=True).astype(
        jnp.bfloat16
    )
    dprob = jnp.einsum("bthe,bshe->bhts", grad_rows, value_rows, preferred_element_type=jnp.float32)
    dscore = (dprob * blend[:, None]).astype(jnp.bfloat16)
    query_local = jnp.einsum(
        "bhts,bshd->bthd", dscore, key_rows, preferred_element_type=jnp.float32
    )
    key_local = jnp.einsum(
        "bhts,bthd->bshd", dscore, query_rows, preferred_element_type=jnp.float32
    )
    value_local = jnp.einsum(
        "bhts,bthe->bshe", probs, grad_rows, preferred_element_type=jnp.float32
    )
    per_level = jnp.einsum(
        "bthe,jbhde->jbthd", grad_rows, states_low, preferred_element_type=jnp.float32
    )
    query_far = jnp.einsum("btj,jbthd->bthd", tier_weight, per_level, precision=HIGHEST)
    key_far = jnp.einsum(
        "bhde,bshe->bshd", back_low, value_rows, preferred_element_type=jnp.float32
    )
    value_far = jnp.einsum(
        "bhde,bshd->bshe", back_low, key_rows, preferred_element_type=jnp.float32
    )
    flat = (batch_rows, length, width)
    grad_query = (query_local + query_far).astype(jnp.bfloat16).reshape(flat)
    grad_key = (key_local + key_far).astype(jnp.bfloat16).reshape(flat)
    grad_value = (value_local + value_far).astype(jnp.bfloat16).reshape(flat)
    return (layer_out, grad_query, grad_key, grad_value)


def solution(mesh):
    return jax.shard_map(
        on_device,
        mesh=mesh,
        in_specs=(
            P(("groups", "batch"), "seq", "head"),
            P(("groups", "batch"), "seq", "head"),
            P(("groups", "batch"), "seq", "head"),
            P(("groups", "batch"), "seq", None),
            P("head", None),
            P(("groups", "batch"), "seq", "head"),
        ),
        out_specs=(
            P(("groups", "batch"), "seq", "head"),
            P(("groups", "batch"), "seq", "head"),
            P(("groups", "batch"), "seq", "head"),
            P(("groups", "batch"), "seq", "head"),
        ),
        check_vma=False,
    )
```

profile of v0, /device:TPU:0, one launch (start us, length us, event | category | flops | bytes accessed | tf_op | source)
XLA Modules:
  0.0 105.6 jit_solution(2868761896219859110)
XLA Ops:
  10.9 2.0 %fusion.75 = f32[4,128,128]{2,1,0:T(8,128)} fusion(bf16[512,4,128]{0,2,1:T(8,128)(2,1)} %copy.53, bf16[512,4,128]{2,1,0:T(4,128)(2,1)S(1)} %reshape.707), kind=kOutput, calls=%fused_computation.89 | convolution fusion | flops 67108864 | bytes 1310720 | tf_op jit(solution)/shard_map/bthd,bthe->bhde/dot_general | solution.py:75
  19.6 1.4 %fusion.64 = pred[10,512,512]{2,1,0:T(8,128)(4,1)} fusion(pred[10,512,512]{2,1,0:T(8,128)(4,1)} %fusion.63), kind=kLoop, calls=%fused_computation.78 | loop fusion | flops 19922944 | bytes 262144
  21.1 1.4 %fusion.65 = pred[10,512,512]{2,1,0:T(8,128)(4,1)} fusion(pred[10,512,512]{2,1,0:T(8,128)(4,1)} %fusion.64), kind=kLoop, calls=%fused_computation.79 | loop fusion | flops 19922944 | bytes 262144
  22.5 1.4 %fusion.66 = pred[10,512,512]{2,1,0:T(8,128)(4,1)} fusion(pred[10,512,512]{2,1,0:T(8,128)(4,1)} %fusion.65), kind=kLoop, calls=%fused_computation.80 | loop fusion | flops 19922944 | bytes 262144
  23.9 1.4 %fusion.67 = pred[10,512,512]{2,1,0:T(8,128)(4,1)} fusion(pred[10,512,512]{2,1,0:T(8,128)(4,1)} %fusion.66), kind=kLoop, calls=%fused_computation.81 | loop fusion | flops 19922944 | bytes 262144
  28.2 8.2 %fusion = f32[512,1,512]{2,1,0:T(1,128)} fusion(f32[512,10,1]{1,2,0:T(1,128)S(1)} %copy.70, pred[10,512,512]{2,1,0:T(8,128)(4,1)} %fusion.69), kind=kOutput, calls=%fused_computation | convolution fusion | flops 31457280 | bytes 3690496 | tf_op jit(solution)/shard_map/lts,btl->bts/dot_general | solution.py:95
  36.3 2.0 %reshape.704 = bf16[512,4,128]{2,1,0:T(4,128)(2,1)} reshape(bf16[1,512,512]{2,1,0:T(8,128)(2,1)} %param.7) | data formatting | bytes 1048576 | tf_op jit(solution)/shard_map/reshape
  38.3 2.1 %copy.63 = bf16[512,4,128]{0,2,1:T(8,128)(2,1)} copy(bf16[512,4,128]{2,1,0:T(4,128)(2,1)} %reshape.704) | data formatting | bytes 1048576 | tf_op jit(solution)/shard_map/reshape
  40.4 2.1 %copy.56 = f32[512,4,128]{2,0,1:T(8,128)} copy(bf16[512,4,128]{2,1,0:T(4,128)(2,1)} %reshape.704) | data formatting | bytes 1572864 | tf_op jit(solution)/shard_map/convert_element_type | solution.py:79
  44.7 3.2 %multiply_convert_fusion.1 = bf16[4,512,512]{2,1,0:T(8,128)(2,1)} fusion(bf16[512,4,128]{0,2,1:T(8,128)(2,1)} %copy.63, f32[512,512]{1,0:T(8,128)S(1)} %bitcast.127, bf16[512,4,128]{2,1,0:T(4,128)(2,1)S(1)} %reshape.705), kind=kOutput, calls=%fused_computation.3 | convolution fusion | flops 270532608 | bytes 4194304 | tf_op jit(solution)/shard_map/bthd,bshd->bhts/dot_general | solution.py:96
  48.0 3.1 %convolution_convert_fusion = bf16[2,4,128,128]{3,0,2,1:T(2,128)(2,1)S(1)} fusion(f32[4,4,128,128]{3,2,1,0:T(8,128)} %bitcast.137, pred[4]{0:T(512)(128)(4,1)S(1)} %iota_compare_fusion.1, s32[4]{0:T(128)S(1)} %fusion.108), kind=kOutput, calls=%fused_computation.29 | convolution fusion | flops 6422544 | bytes 1310740 | tf_op jit(solution)/shard_map/jn,nbhde->jbhde/dot_general | solution.py:90
  51.0 2.0 %fusion.7 = f32[4,128,512]{2,1,0:T(8,128)S(1)} fusion(f32[512,4,128]{2,0,1:T(8,128)} %copy.56, f32[2,512]{1,0:T(2,128)S(1)} %get-tuple-element.17, bf16[2,4,128,128]{3,0,2,1:T(2,128)(2,1)S(1)} %convolution_convert_fusion), kind=kOutput, calls=%fused_computation.12 | convolution fusion | flops 135266304 | bytes 2363392 | tf_op jit(solution)/shard_map/jbthd,jbhde->bthe/dot_general | solution.py:99
  53.8 3.2 %convolution_bitcast_fusion = f32[1,512,2048]{2,1,0:T(8,128)} fusion(bf16[512,512]{0,1:T(8,128)(2,1)S(1)} %bitcast.136, bf16[512,2048]{1,0:T(8,128)(2,1)S(1)} %copy-done), kind=kOutput, calls=%fused_computation.4 | convolution fusion | flops 1073741824 | bytes 6815744 | tf_op jit(solution)/shard_map/btf,fe->bte/dot_general | solution.py:103
  57.1 3.0 %fusion.12 = bf16[512,512]{0,1:T(8,128)(2,1)S(1)} fusion(bf16[512,2048]{1,0:T(8,128)(2,1)S(1)} %copy-done, bf16[1,512,2048]{2,1,0:T(8,128)(2,1)} %all-gather.4.cloned.1.call-done), kind=kOutput, calls=%fused_computation.23 | convolution fusion | flops 1074003968 | bytes 4718592 | tf_op jit(solution)/shard_map/bte,fe->btf/dot_general | solution.py:68
  60.6 3.2 %collective-permute-start = (f32[2,1,4,128,128]{3,4,0,2,1:T(8,128)S(1)}, f32[2,1,4,128,128]{3,4,0,2,1:T(8,128)S(1)}, u32[]{:S(2)}, u32[]{:S(2)}) collective-permute-start(f32[2,1,4,128,128]{3,4,0,2,1:T(8,128)S(1)} %fusion.19), channel_id=1, source_target_pairs={{0,4},{4,0},{8,12},{12,8},{1,5},{5,1},{9,13},{13,9},{2,6},{6,2},{1... | collective-permute-start | bytes 1572872 | tf_op jit(solution)/shard_map/ppermute | solution.py:23
  65.0 1.6 %fusion.15 = bf16[1,512,4,128]{1,3,2,0:T(8,128)(2,1)} fusion(bf16[4,512,512]{2,1,0:T(8,128)(2,1)S(1)} %multiply_convert_fusion, bf16[512,4,128]{0,2,1:T(8,128)(2,1)S(1)} %copy-done.7, f32[512,4,128]{0,2,1:T(8,128)S(1)} %fusion.2), kind=kOutput, calls=%fused_computation.24 | convolution fusion | flops 268959744 | bytes 4194304 | tf_op jit(solution)/shard_map/bhts,bshd->bthd/dot_general | solution.py:109
  66.6 9.0 %collective-permute-done = f32[2,1,4,128,128]{3,4,0,2,1:T(8,128)S(1)} collective-permute-done((f32[2,1,4,128,128]{3,4,0,2,1:T(8,128)S(1)}, f32[2,1,4,128,128]{3,4,0,2,1:T(8,128)S(1)}, u32[]{:S(2)}, u32[]{:S(2)}) %collective-permute-start) | collective-permute-done | bytes 524320 | tf_op jit(solution)/shard_map/ppermute | solution.py:23
  76.4 2.8 %collective-permute-start.1 = (f32[1,1,4,128,128]{3,4,0,2,1:T(8,128)}, f32[1,1,4,128,128]{3,4,0,2,1:T(8,128)S(1)}, u32[]{:S(2)}, u32[]{:S(2)}) collective-permute-start(f32[1,1,4,128,128]{3,4,0,2,1:T(8,128)} %slice_add_fusion), channel_id=1, source_target_pairs={{0,8},{8,0},{4,12},{12,4},{1,9},{9,1},{5,13},{13,5},{2,10},{10,2},... | collective-permute-start | bytes 786440 | tf_op jit(solution)/shard_map/ppermute | solution.py:23
  80.6 2.0 %copy.67 = bf16[1,512,512]{2,1,0:T(8,128)(2,1)} copy(bf16[1,512,512]{1,2,0:T(8,128)(2,1)} %bitcast.135) | data formatting | bytes 1048576
  82.7 3.3 %convolution_bitcast_fusion.2 = f32[1,512,4,128]{1,3,2,0:T(8,128)} fusion(bf16[512,4,128]{0,2,1:T(8,128)(2,1)} %bitcast.132, bf16[4,512,512]{2,1,0:T(8,128)(2,1)} %multiply_convert_fusion.1), kind=kOutput, calls=%fused_computation.14 | convolution fusion | flops 268435456 | bytes 3670016 | tf_op jit(solution)/shard_map/bhts,bthe->bshe/dot_general | solution.py:115
  86.0 4.6 %collective-permute-done.1 = f32[1,1,4,128,128]{3,4,0,2,1:T(8,128)S(1)} collective-permute-done((f32[1,1,4,128,128]{3,4,0,2,1:T(8,128)}, f32[1,1,4,128,128]{3,4,0,2,1:T(8,128)S(1)}, u32[]{:S(2)}, u32[]{:S(2)}) %collective-permute-start.1) | collective-permute-done | bytes 262176 | tf_op jit(solution)/shard_map/ppermute | solution.py:23
  91.8 2.0 %copy.68 = bf16[1,512,512]{2,1,0:T(8,128)(2,1)} copy(bf16[1,512,512]{1,2,0:T(8,128)(2,1)} %bitcast.134) | data formatting | bytes 1048576
  93.8 1.5 %fusion.16 = bf16[1,512,4,128]{1,3,2,0:T(8,128)(2,1)S(1)} fusion(f32[1,512,4,128]{1,3,2,0:T(8,128)} %convolution_bitcast_fusion.2, bf16[4,128,128]{1,2,0:T(8,128)(2,1)S(1)} %fusion.81, bf16[512,4,128]{2,1,0:T(4,128)(2,1)S(1)} %reshape.705), kind=kOutput, calls=%fused_computation.25 | convolution fusion | flops 67633152 | bytes 2228224 | tf_op jit(solution)/shard_map/bhde,bshd->bshe/dot_general | solution.py:125
  96.3 2.7 %convert_element_type.1833 = bf16[1,512,1024]{2,1,0:T(8,128)(2,1)} convert(f32[1,512,1024]{2,1,0:T(8,128)} %reduce-scatter.2.cloned.1.call-done) | non-fusion elementwise | flops 524288 | bytes 3145728 | tf_op jit(solution)/shard_map/convert_element_type | solution.py:104
  (60 shorter events, 22.4 us)
Async XLA Ops:
  7.2 46.7 %copy-start = (bf16[512,2048]{1,0:T(8,128)(2,1)S(1)}, bf16[512,2048]{1,0:T(8,128)(2,1)}, u32[]{:S(2)}) copy-start(bf16[512,2048]{1,0:T(8,128)(2,1)} %param.11) | copy-start | bytes 6291460
  7.2 40.8 %all-gather.6.cloned.1.call-start = ((), (), s32[]{:S(2)}) async-start(), calls=%async_computation.3 | async-start | bytes 1310720 | tf_op jit(solution)/shard_map/all_gather | solution.py:84
  8.5 6.6 %copy-start.11 = (s32[1,512,16]{1,2,0:T(8,128)S(1)}, s32[1,512,16]{1,2,0:T(8,128)}, u32[]{:S(2)}) copy-start(s32[1,512,16]{1,2,0:T(8,128)} %param.10) | copy-start | bytes 98308
  8.5 6.6 %copy-start.12 = (f32[16]{0:T(128)S(1)}, f32[16]{0:T(128)}, u32[]{:S(2)}) copy-start(f32[16]{0:T(128)} %constant.11.clone) | copy-start | bytes 196
  12.9 44.2 %all-gather.4.cloned.1.call-start = ((), (), s32[]{:S(2)}) async-start(), calls=%async_computation.2 | async-start | bytes 3145728 | tf_op jit(solution)/shard_map/all_gather | solution.py:70
  13.7 82.7 %reduce-scatter.2.cloned.1.call-start = ((), (), s32[]{:S(2)}) async-start(), calls=%async_computation.1 | async-start | bytes 6291456 | tf_op jit(solution)/shard_map/reduce_scatter | solution.py:104
  43.8 1.0 copy-start.3
  48.0 5.0 %copy-start.1 = (bf16[4,512,512]{2,1,0:T(8,128)(2,1)S(1)}, bf16[4,512,512]{2,1,0:T(8,128)(2,1)}, u32[]{:S(2)}) copy-start(bf16[4,512,512]{2,1,0:T(8,128)(2,1)} %multiply_convert_fusion.1) | copy-start | bytes 6291460
  57.1 3.0 %copy-start.2 = (f32[512,4,128]{2,0,1:T(8,128)S(1)}, f32[512,4,128]{2,0,1:T(8,128)}, u32[]{:S(2)}) copy-start(f32[512,4,128]{2,0,1:T(8,128)} %copy.56) | copy-start | bytes 3145732
  60.1 4.5 %copy-start.5 = (bf16[512,512]{0,1:T(8,128)(2,1)}, bf16[512,512]{0,1:T(8,128)(2,1)S(1)}, u32[]{:S(2)}) copy-start(bf16[512,512]{0,1:T(8,128)(2,1)S(1)} %fusion.12) | copy-start | bytes 1572868
  60.1 3.7 %copy-start.4 = (f32[512,1,512]{2,0,1:T(8,128)S(1)}, f32[512,1,512]{2,0,1:T(8,128)}, u32[]{:S(2)}) copy-start(f32[512,1,512]{2,0,1:T(8,128)} %copy-done.3) | copy-start | bytes 3145732
  60.6 15.0 %collective-permute-start = (f32[2,1,4,128,128]{3,4,0,2,1:T(8,128)S(1)}, f32[2,1,4,128,128]{3,4,0,2,1:T(8,128)S(1)}, u32[]{:S(2)}, u32[]{:S(2)}) collective-permute-start(f32[2,1,4,128,128]{3,4,0,2,1:T(8,128)S(1)} %fusion.19), channel_id=1, source_target_pairs={{0,4},{4,0},{8,12},{12,8},{1,5},{5,1},{9,13},{13,9},{2,6},{6,2},{1... | collective-permute-start | bytes 1572872 | tf_op jit(solution)/shard_map/ppermute | solution.py:23
  63.8 1.2 %copy-start.7 = (bf16[512,4,128]{0,2,1:T(8,128)(2,1)S(1)}, bf16[512,4,128]{0,2,1:T(8,128)(2,1)}, u32[]{:S(2)}) copy-start(bf16[512,4,128]{0,2,1:T(8,128)(2,1)} %copy.53) | copy-start | bytes 1572868
  65.0 14.2 %copy-start.6 = (bf16[512,4,128]{0,2,1:T(8,128)(2,1)S(1)}, bf16[512,4,128]{0,2,1:T(8,128)(2,1)}, u32[]{:S(2)}) copy-start(bf16[512,4,128]{0,2,1:T(8,128)(2,1)} %copy.63) | copy-start | bytes 1572868
  75.6 5.0 %copy-start.9 = (f32[2,1,4,128,128]{3,4,0,2,1:T(8,128)}, f32[2,1,4,128,128]{3,4,0,2,1:T(8,128)S(1)}, u32[]{:S(2)}) copy-start(f32[2,1,4,128,128]{3,4,0,2,1:T(8,128)S(1)} %collective-permute-done) | copy-start | bytes 1572868
  76.4 14.1 %collective-permute-start.1 = (f32[1,1,4,128,128]{3,4,0,2,1:T(8,128)}, f32[1,1,4,128,128]{3,4,0,2,1:T(8,128)S(1)}, u32[]{:S(2)}, u32[]{:S(2)}) collective-permute-start(f32[1,1,4,128,128]{3,4,0,2,1:T(8,128)} %slice_add_fusion), channel_id=1, source_target_pairs={{0,8},{8,0},{4,12},{12,4},{1,9},{9,1},{5,13},{13,5},{2,10},{10,2},... | collective-permute-start | bytes 786440 | tf_op jit(solution)/shard_map/ppermute | solution.py:23
  82.7 7.9 %copy-start.10 = (f32[2,1,4,128,128]{3,4,0,2,1:T(8,128)S(1)}, f32[2,1,4,128,128]{3,4,0,2,1:T(8,128)}, u32[]{:S(2)}) copy-start(f32[2,1,4,128,128]{3,4,0,2,1:T(8,128)} %copy-done.9) | copy-start | bytes 1572868
  82.7 7.9 %copy-start.8 = (f32[1,512,4,128]{1,3,2,0:T(8,128)S(1)}, f32[1,512,4,128]{1,3,2,0:T(8,128)}, u32[]{:S(2)}) copy-start(f32[1,512,4,128]{1,3,2,0:T(8,128)} %convolution_bitcast_fusion.1) | copy-start | bytes 3145732
Sparse Core Ops, SparseCore 0:
  13.0 30.6 all-gather.5
  45.3 9.9 all-gather.3
  57.6 14.2 reduce-scatter.1
where the time goes:
time: 106 us
  matrix products  36.1 us (34%)
  other arithmetic  17.9 us (17%)
  local copies, waits for them, and re-layouts  17.2 us (16%)
  waiting for transfers between devices  14.3 us (13%)
  between operations  14 us (13%)
  starting transfers between devices  6.06 us (6%)
    ppermute x2, waiting for transfers between devices, from_partner(): return lax.ppermute(block, axis, route)  13.6 us
    unnamed x9, other arithmetic  12.8 us
    dot_general x1, matrix products, on_device(): jnp.einsum('lts,btl->bts', intra_map, weights[:, :, :tiers], precision=HI...  8.16 us
    unnamed x29, local copies, waits for them, and re-layouts  6.06 us
    ppermute x2, starting transfers between devices, from_partner(): return lax.ppermute(block, axis, route)  5.94 us
    reshape x2, local copies, waits for them, and re-layouts  4.07 us
    another operation x6, local copies, waits for them, and re-layouts  3.74 us
    dot_general x1, matrix products, on_device(): jnp.einsum('bhts,bthe->bshe', probs, grad_rows, preferred_element_type=jn...  3.28 us
  transfers between devices with their start and end apart: 5, of which 2 were waited for; matrix products, arithmetic and copies ran while one was open for 59% of the time, Pallas kernels for 0%

commit v1 on v0

v1 whole, which is shorter than its diff:
```python
import functools

import jax
import jax.numpy as jnp
from jax import lax
from jax.experimental import pallas as pl
from jax.experimental.pallas import tpu as pltpu
from jax.sharding import PartitionSpec as P

HEAD_DIM = 128
TILE = 256
F32 = jnp.float32
BF16 = jnp.bfloat16
VMEM = pl.BlockSpec(memory_space=pltpu.VMEM)
SMEM = pl.BlockSpec(memory_space=pltpu.SMEM)


def level_scale(level):
    return 1.0 if level == 0 else 2.0 ** (-(level - 1) / 2.0)


def dot(a, b):
    return lax.dot_general(a, b, (((1,), (0,)), ((), ())), preferred_element_type=F32)


def dot_nt(a, b):
    return lax.dot_general(a, b, (((1,), (1,)), ((), ())), preferred_element_type=F32)


def dot_tn(a, b):
    return lax.dot_general(a, b, (((0,), (0,)), ((), ())), preferred_element_type=F32)


def tier(mask, level):
    return mask[:, level : level + 1].astype(F32) * jnp.float32(level_scale(level))


def call(kernel, name, out_shape, in_specs, flops, *args):
    moved = sum(a.size * a.dtype.itemsize for a in args)
    moved += sum(o.size * o.dtype.itemsize for o in out_shape)
    return pl.pallas_call(
        kernel,
        name=name,
        out_shape=out_shape,
        in_specs=in_specs,
        out_specs=[VMEM] * len(out_shape),
        compiler_params=pltpu.CompilerParams(vmem_limit_bytes=16 << 20),
        cost_estimate=pl.CostEstimate(flops=flops, bytes_accessed=moved, transcendentals=0),
    )(*args)


def head_slices(width):
    return [slice(i * HEAD_DIM, (i + 1) * HEAD_DIM) for i in range(width // HEAD_DIM)]


def state_kernel(key_ref, value_ref, state_ref):
    for col in head_slices(key_ref.shape[1]):
        state_ref[col, :] = dot_tn(key_ref[:, col], value_ref[:, col]).astype(BF16)


def own_kernel(place_ref, grad_ref, weight_ref, part_ref, quarter_ref):
    half = grad_ref.shape[1]
    mine = pl.multiple_of(place_ref[0] * half, half)
    other = pl.multiple_of((1 - place_ref[0]) * half, half)
    part_ref[...] = dot_nt(grad_ref[...], weight_ref[:, pl.ds(mine, half)])
    quarter_ref[...] = weight_ref[:, pl.ds(other, half)]


def reach_kernel(tiers, place_ref, grad_ref, weight_ref, part_ref, query_ref, mask_ref, *outs):
    grad_mixed_ref, weighted_ref, reach_refs = outs[0], outs[1], outs[2:]
    span = len(reach_refs)
    half = grad_ref.shape[1]
    other = pl.multiple_of((1 - place_ref[0]) * half, half)
    mask = mask_ref[...]
    weight = [tier(mask, tiers + j) for j in range(span)]
    for i, col in enumerate(head_slices(query_ref.shape[1])):
        rows = weight_ref[col, pl.ds(other, half)]
        grad = (part_ref[:, col] + dot_nt(grad_ref[...], rows)).astype(BF16)
        grad_mixed_ref[:, col] = grad
        query = query_ref[:, col].astype(F32)
        weighted = [(w * query).astype(BF16) for w in weight]
        for j in range(span):
            at = (i * span + j) * HEAD_DIM
            weighted_ref[:, at : at + HEAD_DIM] = weighted[j]
            reach_refs[j][col, :] = dot_tn(weighted[j], grad).astype(BF16)


def tile_blend(mask, tile):
    rows = lax.broadcasted_iota(jnp.int32, (tile, tile), 0)
    cols = lax.broadcasted_iota(jnp.int32, (tile, tile), 1)
    spread = rows ^ cols
    blend = jnp.where(spread == 0, tier(mask, 0), 0.0)
    for level in range(1, tile.bit_length()):
        here = ((spread >> (level - 1)) == 1) & (cols < rows)
        blend = jnp.where(here, tier(mask, level), blend)
    return blend


def local_kernel(query_ref, key_ref, value_ref, grad_ref, mask_ref, mixed_ref, dq_ref, dk_ref, dv_ref):
    length, width = query_ref.shape
    tile = min(TILE, length)
    count = length // tile
    inner = tile.bit_length()
    bits = count.bit_length() - 1
    span = [slice(i * tile, (i + 1) * tile) for i in range(count)]
    mask = mask_ref[...]
    blends = [tile_blend(mask[rows], tile) for rows in span]
    for col in head_slices(width):
        query = [query_ref[rows, col] for rows in span]
        key = [key_ref[rows, col] for rows in span]
        value = [value_ref[rows, col] for rows in span]
        grad = [grad_ref[rows, col] for rows in span]
        state = [dot_tn(key[i], value[i]) for i in range(count)] if count > 1 else []
        back = [None] * count
        for i in range(count):
            probs = (blends[i] * dot_nt(query[i], key[i])).astype(BF16)
            dscore = (blends[i] * dot_nt(grad[i], value[i])).astype(BF16)
            mixed = dot(probs, value[i])
            dq = dot(dscore, key[i])
            for b in range(bits):
                if not i >> b & 1:
                    continue
                first = ((i >> b) ^ 1) << b
                total = functools.reduce(jnp.add, state[first : first + (1 << b)]).astype(BF16)
                weight = tier(mask[span[i]], inner + b)
                weighted = (weight * query[i].astype(F32)).astype(BF16)
                mixed = mixed + dot(weighted, total)
                dq = dq + weight * dot_nt(grad[i], total)
                reach = dot_tn(weighted, grad[i])
                for m in range(first, first + (1 << b)):
                    back[m] = reach if back[m] is None else back[m] + reach
            mixed_ref[span[i], col] = mixed
            dq_ref[span[i], col] = dq
            dk_ref[span[i], col] = dot_tn(dscore, query[i])
            dv_ref[span[i], col] = dot_tn(probs, grad[i])
        for i in range(count):
            if back[i] is not None:
                low = back[i].astype(BF16)
                dk_ref[span[i], col] += dot_nt(value[i], low)
                dv_ref[span[i], col] += dot(key[i], low)


def mixed_kernel(flag_ref, mixed_ref, weighted_ref, *refs):
    state_refs, out_ref = refs[:-1], refs[-1]
    span = len(state_refs)
    for i, col in enumerate(head_slices(mixed_ref.shape[1])):
        states = [(state_refs[j][col, :].astype(F32) * flag_ref[j]).astype(BF16) for j in range(span)]
        at = i * span * HEAD_DIM
        far = dot(weighted_ref[:, at : at + span * HEAD_DIM], jnp.concatenate(states, axis=0))
        out_ref[:, col] = (mixed_ref[:, col] + far).astype(BF16)


def query_kernel(tiers, flag_ref, place_ref, dq_ref, grad_ref, mask_ref, mixed_ref, weight_ref, *refs):
    state_refs, out_ref, part_ref = refs[:-2], refs[-2], refs[-1]
    half = part_ref.shape[1]
    mine = pl.multiple_of(place_ref[0] * half, half)
    part_ref[...] = dot(mixed_ref[...], weight_ref[:, pl.ds(mine, half)])
    mask = mask_ref[...]
    weight = [tier(mask, tiers + j) * flag_ref[j] for j in range(len(state_refs))]
    for col in head_slices(dq_ref.shape[1]):
        total = dq_ref[:, col]
        for j, ref in enumerate(state_refs):
            total = total + weight[j] * dot_nt(grad_ref[:, col], ref[col, :])
        out_ref[:, col] = total.astype(BF16)


def layer_kernel(part_ref, mixed_ref, quarter_ref, out_ref):
    out_ref[...] = (part_ref[...] + dot(mixed_ref[...], quarter_ref[...])).astype(BF16)


def back_kernel(dk_ref, dv_ref, key_ref, value_ref, *refs):
    back_refs, dk_out, dv_out = refs[:-2], refs[-2], refs[-1]
    for col in head_slices(key_ref.shape[1]):
        back = functools.reduce(jnp.add, [ref[col, :].astype(F32) for ref in back_refs]).astype(BF16)
        dk_out[:, col] = (dk_ref[:, col] + dot_nt(value_ref[:, col], back)).astype(BF16)
        dv_out[:, col] = (dv_ref[:, col] + dot(key_ref[:, col], back)).astype(BF16)


def pairs(count, stride, up=True, down=True):
    route = []
    for low in range(count):
        high = low ^ stride
        if low < high < count:
            route += [(low, high)] * up + [(high, low)] * down
    return route


def add_low(a, b):
    return (a.astype(F32) + b.astype(F32)).astype(BF16)


def on_device(query_in, key_in, value_in, level_mask, out_weight, grad_out):
    blocks = lax.axis_size("seq")
    if query_in.shape[0] != 1 or lax.axis_size("head") != 2 or blocks < 2:
        raise ValueError("unsupported split")
    query, key, value, mask, grad = (x[0] for x in (query_in, key_in, value_in, level_mask, grad_out))
    length, width = query.shape
    half = grad.shape[1]
    tiers = length.bit_length()
    span = blocks.bit_length() - 1
    position = lax.axis_index("seq")
    place = lax.axis_index("head").astype(jnp.int32)[None]
    flags = ((position >> jnp.arange(span, dtype=jnp.int32)) & 1).astype(F32)
    swap = [(0, 1), (1, 0)]
    shape = jax.ShapeDtypeStruct
    matrix = shape((width, HEAD_DIM), BF16)
    low = shape((length, width), BF16)
    high = shape((length, width), F32)
    unit = 2 * length * width * HEAD_DIM

    with jax.named_scope("grad_swap"):
        grad_other = lax.ppermute(grad, "head", swap)
    (state,) = call(state_kernel, "state", [matrix], [VMEM] * 2, unit, key, value)
    states, total = [], state
    part, quarter = call(
        own_kernel,
        "own",
        [high, shape((width, half), BF16)],
        [SMEM, VMEM, VMEM],
        2 * length * width * half,
        place,
        grad,
        out_weight,
    )
    with jax.named_scope("weight_swap"):
        quarter = lax.ppermute(quarter, "head", swap)
    for j in range(span):
        with jax.named_scope(f"state_step{j}"):
            got = lax.ppermute(total, "seq", pairs(blocks, 1 << j, down=j < span - 1))
        states.append(got)
        if j < span - 1:
            total = add_low(total, got)

    grad_mixed, weighted, *pending = call(
        functools.partial(reach_kernel, tiers),
        "reach",
        [low, shape((length, span * width), BF16)] + [matrix] * span,
        [SMEM] + [VMEM] * 5,
        2 * length * width * half + span * unit,
        place,
        grad_other,
        out_weight,
        part,
        query,
        mask,
    )
    backs = []
    for j in range(span):
        with jax.named_scope(f"reach_step{j}"):
            later = [lax.ppermute(x, "seq", pairs(blocks, 1 << j)) for x in pending[1:]]
            backs.append(lax.ppermute(pending[0], "seq", pairs(blocks, 1 << j, up=False)))
        pending = [add_low(a, b) for a, b in zip(pending[1:], later)]

    mixed, dq, dk, dv = call(
        local_kernel,
        "local",
        [high] * 4,
        [VMEM] * 5,
        6 * 2 * unit,
        query,
        key,
        value,
        grad_mixed,
        mask,
    )
    (mixed,) = call(
        mixed_kernel, "mixed", [low], [SMEM] + [VMEM] * (2 + span), span * unit, flags, mixed, weighted, *states
    )
    with jax.named_scope("mixed_swap"):
        mixed_other = lax.ppermute(mixed, "head", swap)
    grad_query, part = call(
        functools.partial(query_kernel, tiers),
        "query",
        [low, shape((length, half), F32)],
        [SMEM] * 2 + [VMEM] * (5 + span),
        2 * length * width * half + span * unit,
        flags,
        place,
        dq,
        grad_mixed,
        mask,
        mixed,
        out_weight,
        *states,
    )
    (layer_out,) = call(
        layer_kernel,
        "layer",
        [shape((length, half), BF16)],
        [VMEM] * 3,
        2 * length * width * half,
        part,
        mixed_other,
        quarter,
    )
    grad_key, grad_value = call(
        back_kernel, "back", [low] * 2, [VMEM] * (4 + span), 2 * unit, dk, dv, key, value, *backs
    )
    return tuple(x[None] for x in (layer_out, grad_query, grad_key, grad_value))


def solution(mesh):
    rows = P(("groups", "batch"), "seq", "head")
    return jax.shard_map(
        on_device,
        mesh=mesh,
        in_specs=(rows, rows, rows, P(("groups", "batch"), "seq", None), P("head", None), rows),
        out_specs=(rows,) * 4,
        check_vma=False,
    )
```

time: 106 us -> 51.5 us (0.49)
  matrix products: 36.1 us -> 0 us
  Pallas kernels: 0 us -> 17.8 us
  other arithmetic: 17.9 us -> 0.98 us
  between operations: 14 us -> 0.75 us
  local copies, waits for them, and re-layouts: 17.2 us -> 5.97 us
  starting transfers between devices: 6.06 us -> 12.6 us
  waiting for transfers between devices: 14.3 us -> 12.9 us
    dot_general x16 -> x0, matrix products: 36.1 us -> none  [the longest x1 8.16 us: on_device(): jnp.einsum('lts,btl->bts', intra_map, weights[:, :, :tiers], precision=HI...]
    pallas_call x0 -> x8, Pallas kernels: none -> 17.8 us  [call(): pl.pallas_call(kernel, name=name, out_shape=out_shape, in_specs=in_specs,...]
    unnamed x9 -> x0, other arithmetic: 12.8 us -> none
    ppermute x2 -> x8, starting transfers between devices: 5.94 us -> 12.6 us  [the longest x2 7.71 us: on_device(): got = lax.ppermute(total, 'seq', pairs(blocks, 1 << j, down=j < span - 1))]
    reshape x2 -> x0, local copies, waits for them, and re-layouts: 4.07 us -> none
    another operation x6 -> x0, local copies, waits for them, and re-layouts: 3.74 us -> none
    convert_element_type x1 -> x0, local copies, waits for them, and re-layouts: 2.08 us -> none  [on_device(): jnp.transpose(tier_weight, (2, 0, 1))[:, :, :, None, None]]
    convert_element_type x2 -> x3, other arithmetic: 2.76 us -> 0.98 us  [the longest x2 0.98 us: add_low(): return (a.astype(F32) + b.astype(F32)).astype(BF16)]
  transfers between devices with their start and end apart: 5 -> 8, of which waited for: 2 -> 3; matrix products, arithmetic and copies ran while one was open for 59% -> 4% of each run, Pallas kernels for 0% -> 29%
where the time goes in v1:
time: 51.5 us; the launch traced here: 51 us
  Pallas kernels  17.8 us (35%)
  waiting for transfers between devices  12.9 us (25%)
  starting transfers between devices  12.6 us (24%)
  local copies, waits for them, and re-layouts  5.97 us (12%)
  other arithmetic  0.98 us (2%)
  between operations  0.75 us (1%)
    pallas_call x8, Pallas kernels, call(): pl.pallas_call(kernel, name=name, out_shape=out_shape, in_specs=in_specs,...  17.8 us
    ppermute x2, starting transfers between devices, on_device(): got = lax.ppermute(total, 'seq', pairs(blocks, 1 << j, down=j < span - 1))  7.71 us
    ppermute x2, waiting for transfers between devices, on_device(): lax.ppermute(pending[0], 'seq', pairs(blocks, 1 << j, up=False))  6.91 us
    unnamed x17, local copies, waits for them, and re-layouts  5.97 us
    ppermute x2, waiting for transfers between devices, on_device(): got = lax.ppermute(total, 'seq', pairs(blocks, 1 << j, down=j < span - 1))  2.99 us
    ppermute x1, waiting for transfers between devices, on_device(): later = [lax.ppermute(x, 'seq', pairs(blocks, 1 << j)) for x in pending[1:]]  2.97 us
    ppermute x2, starting transfers between devices, on_device(): lax.ppermute(pending[0], 'seq', pairs(blocks, 1 << j, up=False))  2.57 us
    ppermute x1, starting transfers between devices, on_device(): later = [lax.ppermute(x, 'seq', pairs(blocks, 1 << j)) for x in pending[1:]]  1.64 us
  transfers between devices with their start and end apart: 8, of which 3 were waited for; matrix products, arithmetic and copies ran while one was open for 4% of the time, Pallas kernels for 29%

profile of v1, /device:TPU:0, one launch (start us, length us, event | category | flops | bytes accessed | tf_op | source)
XLA Modules:
  0.0 51.0 jit_solution(17516237354209676713)
XLA Ops:
  0.6 0.6 %collective-permute-start = (bf16[512,1024]{1,0:T(8,128)(2,1)}, bf16[512,1024]{1,0:T(8,128)(2,1)}, u32[]{:S(2)}, u32[]{:S(2)}) collective-permute-start(bf16[512,1024]{1,0:T(8,128)(2,1)} %bitcast.19), channel_id=1, source_target_pairs={{0,1},{1,0},{2,3},{3,2},{4,5},{5,4},{6,7},{7,6},{8,9},{9,8},{10,11... | collective-permute-start | bytes 3145736 | tf_op jit(solution)/shard_map/grad_swap/ppermute | solution.py:212
  1.2 1.6 %copy-done = bf16[512,2048]{1,0:T(8,128)(2,1)S(1)} copy-done((bf16[512,2048]{1,0:T(8,128)(2,1)S(1)}, bf16[512,2048]{1,0:T(8,128)(2,1)}, u32[]{:S(2)}) %copy-start) | copy-done | bytes 2097176
  2.8 1.2 %copy-done.6 = bf16[1,512,1024]{2,1,0:T(8,128)(2,1)S(1)} copy-done((bf16[1,512,1024]{2,1,0:T(8,128)(2,1)S(1)}, bf16[1,512,1024]{2,1,0:T(8,128)(2,1)}, u32[]{:S(2)}) %copy-start.6) | copy-done | bytes 1048600
  4.0 1.7 %own.1 = (f32[512,512]{1,0:T(8,128)S(1)}, bf16[512,1024]{1,0:T(8,128)(2,1)}) custom-call(s32[1]{0:T(128)} %bitcast.place_ref, bf16[512,1024]{1,0:T(8,128)(2,1)S(1)} %bitcast.20, bf16[512,2048]{1,0:T(8,128)(2,1)S(1)} %copy-done), custom_call_target="tpu_custom_call" | custom-call | flops 536870912 | bytes 5242884 | tf_op jit(solution)/shard_map/own/pallas_call | solution.py:41
  5.8 1.0 %state.1 = bf16[512,128]{1,0:T(8,128)(2,1)} custom-call(bf16[512,512]{1,0:T(8,128)(2,1)S(1)} %bitcast.13, bf16[512,512]{1,0:T(8,128)(2,1)S(1)} %bitcast.16), custom_call_target="tpu_custom_call" | custom-call | flops 67108864 | bytes 1179648 | tf_op jit(solution)/shard_map/state/pallas_call | solution.py:41
  6.8 3.0 %collective-permute-start.1 = (bf16[512,128]{1,0:T(8,128)(2,1)}, bf16[512,128]{1,0:T(8,128)(2,1)S(1)}, u32[]{:S(2)}, u32[]{:S(2)}) collective-permute-start(bf16[512,128]{1,0:T(8,128)(2,1)} %state.1), channel_id=1, source_target_pairs={{0,4},{4,0},{8,12},{12,8},{1,5},{5,1},{9,13},{13,9},{2,6},{6,2},{1... | collective-permute-start | bytes 393224 | tf_op jit(solution)/shard_map/state_step0/ppermute | solution.py:229
  9.8 0.9 %copy.10 = s32[1,512,16]{2,1,0:T(8,128)S(1)} copy(s32[1,512,16]{1,2,0:T(8,128)} %param.9) | data formatting | bytes 65536 | tf_op args[3]
  10.7 3.0 %collective-permute-done.1.refs_0_ = bf16[512,128]{1,0:T(8,128)(2,1)S(1)} collective-permute-done((bf16[512,128]{1,0:T(8,128)(2,1)}, bf16[512,128]{1,0:T(8,128)(2,1)S(1)}, u32[]{:S(2)}, u32[]{:S(2)}) %collective-permute-start.1) | collective-permute-done | bytes 131104 | tf_op jit(solution)/shard_map/state_step0/ppermute | solution.py:229
  13.7 0.9 %add_convert_fusion.1 = bf16[512,128]{1,0:T(8,128)(2,1)S(1)} fusion(bf16[512,128]{1,0:T(8,128)(2,1)S(1)} %collective-permute-done.1.refs_0_, bf16[512,128]{1,0:T(8,128)(2,1)} %state.1), kind=kLoop, calls=%fused_computation.1 | loop fusion | flops 262144 | bytes 393216 | tf_op jit(solution)/shard_map/convert_element_type | solution.py:189
  14.7 4.7 %collective-permute-start.2 = (bf16[512,128]{1,0:T(8,128)(2,1)S(1)}, bf16[512,128]{1,0:T(8,128)(2,1)S(1)}, u32[]{:S(2)}, u32[]{:S(2)}) collective-permute-start(bf16[512,128]{1,0:T(8,128)(2,1)S(1)} %add_convert_fusion.1), channel_id=1, source_target_pairs={{0,8},{4,12},{1,9},{5,13},{2,10},{6,14},{3,11},{7,15},{16,24},{20,... | collective-permute-start | bytes 393224 | tf_op jit(solution)/shard_map/state_step1/ppermute | solution.py:229
  19.4 1.2 %copy-done.5 = f32[512,512]{1,0:T(8,128)S(1)} copy-done((f32[512,512]{1,0:T(8,128)S(1)}, f32[512,512]{1,0:T(8,128)}, u32[]{:S(2)}) %copy-start.5) | copy-done | bytes 1048600
  20.6 1.0 %copy-done.7 = bf16[1,512,512]{2,1,0:T(8,128)(2,1)S(1)} copy-done((bf16[1,512,512]{2,1,0:T(8,128)(2,1)S(1)}, bf16[1,512,512]{2,1,0:T(8,128)(2,1)}, u32[]{:S(2)}) %copy-start.7) | copy-done | bytes 524312
  21.6 3.4 %reach.1 = (bf16[512,512]{1,0:T(8,128)(2,1)S(1)}, bf16[512,1024]{1,0:T(8,128)(2,1)S(1)}, bf16[512,128]{1,0:T(8,128)(2,1)S(1)}, bf16[512,128]{1,0:T(8,128)(2,1)S(1)}) custom-call(s32[1]{0:T(128)} %bitcast.place_ref, bf16[512,1024]{1,0:T(8,128)(2,1)} %collective-permute-done.grad_ref, bf16[512,2048]{1,0:T(8,128)(2,1)S(1)} %copy-done.1, ...), custom_call_target="tpu_custom_call" | custom-call | flops 671088640 | bytes 6586372 | tf_op jit(solution)/shard_map/reach/pallas_call | solution.py:41
  25.1 3.9 %local.1 = (f32[512,512]{1,0:T(8,128)S(1)}, f32[512,512]{1,0:T(8,128)S(1)}, f32[512,512]{1,0:T(8,128)S(1)}, f32[512,512]{1,0:T(8,128)S(1)}) custom-call(bf16[512,512]{1,0:T(8,128)(2,1)S(1)} %bitcast.22, bf16[512,512]{1,0:T(8,128)(2,1)S(1)} %bitcast.14, bf16[512,512]{1,0:T(8,128)(2,1)S(1)} %bitcast.17, bf16[512,512]{1,0:T(8,128)(2,1)S(1)} %get-tuple-element.19.grad_ref, ...), custom_call_target="tpu_custom_call" | custom-call | flops 805306368 | bytes 6324224 | tf_op jit(solution)/shard_map/local/pallas_call | solution.py:41
  29.0 1.0 %mixed.1.mixed_ref = bf16[512,512]{1,0:T(8,128)(2,1)S(1)} custom-call(f32[2]{0:T(128)S(1)} %and_convert_fusion.flag_ref, f32[512,512]{1,0:T(8,128)S(1)} %get-tuple-element.21.mixed_ref, bf16[512,1024]{1,0:T(8,128)(2,1)S(1)} %get-tuple-element.22.weighted_ref, bf16[512,128]{1,0:T(8,128)(2,1)S(1)} %collective-permute-done.1.refs_0_, ...), custom_call_target="tpu_custom_call" | custom-call | flops 134217728 | bytes 2883592 | tf_op jit(solution)/shard_map/mixed/pallas_call | solution.py:41
  30.0 0.1 collective-permute-start.3
  30.1 1.6 %collective-permute-start.6 = (bf16[512,128]{1,0:T(8,128)(2,1)S(1)}, bf16[512,128]{1,0:T(8,128)(2,1)S(1)}, u32[]{:S(2)}, u32[]{:S(2)}) collective-permute-start(bf16[512,128]{1,0:T(8,128)(2,1)S(1)} %get-tuple-element.29), channel_id=1, source_target_pairs={{0,4},{4,0},{8,12},{12,8},{1,5},{5,1},{9,13},{13,9},{2,6},{6,2},{1... | collective-permute-start | bytes 393224 | tf_op jit(solution)/shard_map/reach_step0/ppermute | solution.py:250
  31.7 1.3 %collective-permute-start.5 = (bf16[512,128]{1,0:T(8,128)(2,1)S(1)}, bf16[512,128]{1,0:T(8,128)(2,1)S(1)}, u32[]{:S(2)}, u32[]{:S(2)}) collective-permute-start(bf16[512,128]{1,0:T(8,128)(2,1)S(1)} %get-tuple-element.28), channel_id=1, source_target_pairs={{4,0},{12,8},{5,1},{13,9},{6,2},{14,10},{7,3},{15,11},{20,16},{28,... | collective-permute-start | bytes 393224 | tf_op jit(solution)/shard_map/reach_step0/ppermute | solution.py:251
  33.0 3.0 %collective-permute-done.6 = bf16[512,128]{1,0:T(8,128)(2,1)S(1)} collective-permute-done((bf16[512,128]{1,0:T(8,128)(2,1)S(1)}, bf16[512,128]{1,0:T(8,128)(2,1)S(1)}, u32[]{:S(2)}, u32[]{:S(2)}) %collective-permute-start.6) | collective-permute-done | bytes 131104 | tf_op jit(solution)/shard_map/reach_step0/ppermute | solution.py:250
  36.0 1.3 %collective-permute-start.7 = (bf16[512,128]{1,0:T(8,128)(2,1)S(1)}, bf16[512,128]{1,0:T(8,128)(2,1)S(1)}, u32[]{:S(2)}, u32[]{:S(2)}) collective-permute-start(bf16[512,128]{1,0:T(8,128)(2,1)S(1)} %add_convert_fusion), channel_id=1, source_target_pairs={{8,0},{12,4},{9,1},{13,5},{10,2},{14,6},{11,3},{15,7},{24,16},{28,... | collective-permute-start | bytes 393224 | tf_op jit(solution)/shard_map/reach_step1/ppermute | solution.py:251
  37.3 2.4 %query.1 = (bf16[512,512]{1,0:T(8,128)(2,1)}, f32[512,1024]{1,0:T(8,128)S(1)}) custom-call(f32[2]{0:T(128)S(1)} %and_convert_fusion.flag_ref, s32[1]{0:T(128)} %bitcast.place_ref, f32[512,512]{1,0:T(8,128)S(1)} %get-tuple-element.20.dq_ref, bf16[512,512]{1,0:T(8,128)(2,1)S(1)} %get-tuple-element.19.grad_ref, s32[512,16]{1,0:T(8,128)S(1)} %bitcast.12, ...), custom_call_target="tpu_custom_call" | custom-call | flops 671088640 | bytes 7110668 | tf_op jit(solution)/shard_map/query/pallas_call | solution.py:41
  39.7 6.9 %collective-permute-done.7.refs_1_ = bf16[512,128]{1,0:T(8,128)(2,1)S(1)} collective-permute-done((bf16[512,128]{1,0:T(8,128)(2,1)S(1)}, bf16[512,128]{1,0:T(8,128)(2,1)S(1)}, u32[]{:S(2)}, u32[]{:S(2)}) %collective-permute-start.7) | collective-permute-done | bytes 131104 | tf_op jit(solution)/shard_map/reach_step1/ppermute | solution.py:251
  46.6 1.4 %back.1 = (bf16[512,512]{1,0:T(8,128)(2,1)}, bf16[512,512]{1,0:T(8,128)(2,1)}) custom-call(f32[512,512]{1,0:T(8,128)S(1)} %get-tuple-element.26.dk_ref, f32[512,512]{1,0:T(8,128)S(1)} %get-tuple-element.27.dv_ref, bf16[512,512]{1,0:T(8,128)(2,1)S(1)} %bitcast.15, bf16[512,512]{1,0:T(8,128)(2,1)S(1)} %bitcast.18, ...), custom_call_target="tpu_custom_call" | custom-call | flops 134217728 | bytes 4456448 | tf_op jit(solution)/shard_map/back/pallas_call | solution.py:41
  48.0 2.9 %layer.1 = bf16[512,1024]{1,0:T(8,128)(2,1)} custom-call(f32[512,1024]{1,0:T(8,128)S(1)} %get-tuple-element.23.part_ref, bf16[512,512]{1,0:T(8,128)(2,1)S(1)} %collective-permute-done.3.mixed_ref, bf16[512,1024]{1,0:T(8,128)(2,1)} %collective-permute-done.4.quarter_ref), custom_call_target="tpu_custom_call" | custom-call | flops 536870912 | bytes 4718592 | tf_op jit(solution)/shard_map/layer/pallas_call | solution.py:41
  (20 shorter events, 0.1 us)
Async XLA Ops:
  0.6 18.7 %collective-permute-start = (bf16[512,1024]{1,0:T(8,128)(2,1)}, bf16[512,1024]{1,0:T(8,128)(2,1)}, u32[]{:S(2)}, u32[]{:S(2)}) collective-permute-start(bf16[512,1024]{1,0:T(8,128)(2,1)} %bitcast.19), channel_id=1, source_target_pairs={{0,1},{1,0},{2,3},{3,2},{4,5},{5,4},{6,7},{7,6},{8,9},{9,8},{10,11... | collective-permute-start | bytes 3145736 | tf_op jit(solution)/shard_map/grad_swap/ppermute | solution.py:212
  1.2 1.6 %copy-start = (bf16[512,2048]{1,0:T(8,128)(2,1)S(1)}, bf16[512,2048]{1,0:T(8,128)(2,1)}, u32[]{:S(2)}) copy-start(bf16[512,2048]{1,0:T(8,128)(2,1)} %weight_ref.5) | copy-start | bytes 6291460
  2.8 1.2 %copy-start.6 = (bf16[1,512,1024]{2,1,0:T(8,128)(2,1)S(1)}, bf16[1,512,1024]{2,1,0:T(8,128)(2,1)}, u32[]{:S(2)}) copy-start(bf16[1,512,1024]{2,1,0:T(8,128)(2,1)} %param.11) | copy-start | bytes 3145732
  4.0 1.8 %copy-start.2 = (bf16[1,512,512]{2,1,0:T(8,128)(2,1)S(1)}, bf16[1,512,512]{2,1,0:T(8,128)(2,1)}, u32[]{:S(2)}) copy-start(bf16[1,512,512]{2,1,0:T(8,128)(2,1)} %param.7) | copy-start | bytes 1572868
  4.0 1.8 %copy-start.3 = (bf16[1,512,512]{2,1,0:T(8,128)(2,1)S(1)}, bf16[1,512,512]{2,1,0:T(8,128)(2,1)}, u32[]{:S(2)}) copy-start(bf16[1,512,512]{2,1,0:T(8,128)(2,1)} %param.8) | copy-start | bytes 1572868
  4.0 15.3 %copy-start.1 = (bf16[512,2048]{1,0:T(8,128)(2,1)S(1)}, bf16[512,2048]{1,0:T(8,128)(2,1)}, u32[]{:S(2)}) copy-start(bf16[512,2048]{1,0:T(8,128)(2,1)} %weight_ref.5) | copy-start | bytes 6291460
  5.7 1.0 %copy-start.4 = (f32[512,512]{1,0:T(8,128)}, f32[512,512]{1,0:T(8,128)S(1)}, u32[]{:S(2)}) copy-start(f32[512,512]{1,0:T(8,128)S(1)} %get-tuple-element.18.part_ref) | copy-start | bytes 3145732
  5.7 42.3 %collective-permute-start.4 = (bf16[512,1024]{1,0:T(8,128)(2,1)}, bf16[512,1024]{1,0:T(8,128)(2,1)}, u32[]{:S(2)}, u32[]{:S(2)}) collective-permute-start(bf16[512,1024]{1,0:T(8,128)(2,1)} %get-tuple-element.24), channel_id=1, source_target_pairs={{0,1},{1,0},{2,3},{3,2},{4,5},{5,4},{6,7},{7,6},{8,9},{9,8},{10,11... | collective-permute-start | bytes 3145736 | tf_op jit(solution)/shard_map/weight_swap/ppermute | solution.py:226
  6.8 6.9 %collective-permute-start.1 = (bf16[512,128]{1,0:T(8,128)(2,1)}, bf16[512,128]{1,0:T(8,128)(2,1)S(1)}, u32[]{:S(2)}, u32[]{:S(2)}) collective-permute-start(bf16[512,128]{1,0:T(8,128)(2,1)} %state.1), channel_id=1, source_target_pairs={{0,4},{4,0},{8,12},{12,8},{1,5},{5,1},{9,13},{13,9},{2,6},{6,2},{1... | collective-permute-start | bytes 393224 | tf_op jit(solution)/shard_map/state_step0/ppermute | solution.py:229
  14.7 14.4 %collective-permute-start.2 = (bf16[512,128]{1,0:T(8,128)(2,1)S(1)}, bf16[512,128]{1,0:T(8,128)(2,1)S(1)}, u32[]{:S(2)}, u32[]{:S(2)}) collective-permute-start(bf16[512,128]{1,0:T(8,128)(2,1)S(1)} %add_convert_fusion.1), channel_id=1, source_target_pairs={{0,8},{4,12},{1,9},{5,13},{2,10},{6,14},{3,11},{7,15},{16,24},{20,... | collective-permute-start | bytes 393224 | tf_op jit(solution)/shard_map/state_step1/ppermute | solution.py:229
  19.3 1.2 %copy-start.5 = (f32[512,512]{1,0:T(8,128)S(1)}, f32[512,512]{1,0:T(8,128)}, u32[]{:S(2)}) copy-start(f32[512,512]{1,0:T(8,128)} %copy-done.4) | copy-start | bytes 3145732
  20.6 1.0 %copy-start.7 = (bf16[1,512,512]{2,1,0:T(8,128)(2,1)S(1)}, bf16[1,512,512]{2,1,0:T(8,128)(2,1)}, u32[]{:S(2)}) copy-start(bf16[1,512,512]{2,1,0:T(8,128)(2,1)} %param.6) | copy-start | bytes 1572868
  30.0 18.0 %collective-permute-start.3 = (bf16[512,512]{1,0:T(8,128)(2,1)S(1)}, bf16[512,512]{1,0:T(8,128)(2,1)S(1)}, u32[]{:S(2)}, u32[]{:S(2)}) collective-permute-start(bf16[512,512]{1,0:T(8,128)(2,1)S(1)} %mixed.1.mixed_ref), channel_id=1, source_target_pairs={{0,1},{1,0},{2,3},{3,2},{4,5},{5,4},{6,7},{7,6},{8,9},{9,8},{10,11... | collective-permute-start | bytes 1572872 | tf_op jit(solution)/shard_map/mixed_swap/ppermute | solution.py:270
  30.1 5.9 %collective-permute-start.6 = (bf16[512,128]{1,0:T(8,128)(2,1)S(1)}, bf16[512,128]{1,0:T(8,128)(2,1)S(1)}, u32[]{:S(2)}, u32[]{:S(2)}) collective-permute-start(bf16[512,128]{1,0:T(8,128)(2,1)S(1)} %get-tuple-element.29), channel_id=1, source_target_pairs={{0,4},{4,0},{8,12},{12,8},{1,5},{5,1},{9,13},{13,9},{2,6},{6,2},{1... | collective-permute-start | bytes 393224 | tf_op jit(solution)/shard_map/reach_step0/ppermute | solution.py:250
  31.7 8.0 %collective-permute-start.5 = (bf16[512,128]{1,0:T(8,128)(2,1)S(1)}, bf16[512,128]{1,0:T(8,128)(2,1)S(1)}, u32[]{:S(2)}, u32[]{:S(2)}) collective-permute-start(bf16[512,128]{1,0:T(8,128)(2,1)S(1)} %get-tuple-element.28), channel_id=1, source_target_pairs={{4,0},{12,8},{5,1},{13,9},{6,2},{14,10},{7,3},{15,11},{20,16},{28,... | collective-permute-start | bytes 393224 | tf_op jit(solution)/shard_map/reach_step0/ppermute | solution.py:251
  36.0 10.6 %collective-permute-start.7 = (bf16[512,128]{1,0:T(8,128)(2,1)S(1)}, bf16[512,128]{1,0:T(8,128)(2,1)S(1)}, u32[]{:S(2)}, u32[]{:S(2)}) collective-permute-start(bf16[512,128]{1,0:T(8,128)(2,1)S(1)} %add_convert_fusion), channel_id=1, source_target_pairs={{8,0},{12,4},{9,1},{13,5},{10,2},{14,6},{11,3},{15,7},{24,16},{28,... | collective-permute-start | bytes 393224 | tf_op jit(solution)/shard_map/reach_step1/ppermute | solution.py:251

commit v2 on v1

v2 whole, which is shorter than its diff:
```python
import functools

import jax
import jax.numpy as jnp
from jax import lax
from jax.experimental import pallas as pl
from jax.experimental.pallas import tpu as pltpu
from jax.sharding import PartitionSpec as P

HEAD_DIM = 128
TILE = 256
DIRECT = 4
F32 = jnp.float32
BF16 = jnp.bfloat16
VMEM = pl.BlockSpec(memory_space=pltpu.VMEM)
SMEM = pl.BlockSpec(memory_space=pltpu.SMEM)
HBM = pl.BlockSpec(memory_space=pltpu.HBM)


def level_scale(level):
    return 1.0 if level == 0 else 2.0 ** (-(level - 1) / 2.0)


def dot(a, b):
    return lax.dot_general(a, b, (((1,), (0,)), ((), ())), preferred_element_type=F32)


def dot_nt(a, b):
    return lax.dot_general(a, b, (((1,), (1,)), ((), ())), preferred_element_type=F32)


def dot_tn(a, b):
    return lax.dot_general(a, b, (((0,), (0,)), ((), ())), preferred_element_type=F32)


def call(kernel, outs, in_specs, flops, args, out_specs=None, scratch=(), limit=16):
    moved = sum(a.size * a.dtype.itemsize for a in args)
    moved += sum(o.size * o.dtype.itemsize for o in outs)
    return pl.pallas_call(
        kernel,
        out_shape=outs,
        in_specs=in_specs,
        out_specs=out_specs or [VMEM] * len(outs),
        scratch_shapes=list(scratch),
        compiler_params=pltpu.CompilerParams(vmem_limit_bytes=limit << 20),
        cost_estimate=pl.CostEstimate(flops=flops, bytes_accessed=moved, transcendentals=0),
    )(*args)


def head_slices(width):
    return [slice(i * HEAD_DIM, (i + 1) * HEAD_DIM) for i in range(width // HEAD_DIM)]


def upper(spot_ref, bit):
    return (spot_ref[0] >> bit) & 1


def column(ref, index):
    half = ref.shape[1] // 2
    return ref.at[:, pl.ds(pl.multiple_of(index * half, half), half)]


def prep_kernel(tiers, span, *refs):
    place_ref, mask_ref, key_hbm, value_hbm, grad_hbm, weight_hbm, query_hbm = refs[:7]
    state_ref, part_ref, weighted_ref, tier_ref = refs[7:11]
    key, value, grad, weight, query, sems = refs[11:]
    sources = [key_hbm, value_hbm, column(weight_hbm, place_ref[0]), grad_hbm, query_hbm]
    copies = [
        pltpu.make_async_copy(src, dst, sems.at[n])
        for n, (src, dst) in enumerate(zip(sources, [key, value, weight, grad, query]))
    ]
    for copy in copies:
        copy.start()
    slots = mask_ref.shape[0]
    mask = mask_ref[...].astype(F32)
    rows = [mask[l : l + 1] * jnp.float32(level_scale(l)) for l in range(slots)]
    tier = jnp.transpose(jnp.concatenate(rows, axis=0))
    tier_ref[...] = tier
    copies[0].wait()
    copies[1].wait()
    cols = head_slices(key.shape[1])
    for col in cols:
        state_ref[col, :] = dot_tn(key[:, col], value[:, col]).astype(BF16)
    copies[2].wait()
    copies[3].wait()
    part_ref[...] = dot_nt(grad[...], weight[...])
    copies[4].wait()
    for j in range(span):
        scale = jnp.broadcast_to(tier[:, tiers + j : tiers + j + 1], (tier.shape[0], HEAD_DIM))
        for i, col in enumerate(cols):
            at = (i * span + j) * HEAD_DIM
            weighted_ref[:, at : at + HEAD_DIM] = (scale * query[:, col].astype(F32)).astype(BF16)


def reach_kernel(span, direct, place_ref, spot_ref, grad_ref, weight_ref, part_ref, weighted_ref, state_ref, *outs):
    grad_mixed_ref, send_refs = outs[0], outs[1:]
    other = column(weight_ref, 1 - place_ref[0])
    grad_mixed = (part_ref[...] + dot_nt(grad_ref[...], other[...])).astype(BF16)
    grad_mixed_ref[...] = grad_mixed
    step = span * HEAD_DIM
    for i, col in enumerate(head_slices(grad_mixed.shape[1])):
        reach = dot_tn(grad_mixed[:, col], weighted_ref[:, i * step : (i + 1) * step])
        state = state_ref[col, :].astype(F32)
        for j in range(span):
            send = reach[:, j * HEAD_DIM : (j + 1) * HEAD_DIM]
            if direct:
                send = jnp.where(upper(spot_ref, j) > 0, send, state)
            send_refs[j][col, :] = send.astype(BF16)


def tile_blend(tier, tile):
    rows = lax.broadcasted_iota(jnp.int32, (tile, tile), 0)
    cols = lax.broadcasted_iota(jnp.int32, (tile, tile), 1)
    spread = rows ^ cols
    blend = jnp.where(spread == 0, tier[:, 0:1], 0.0)
    for level in range(1, tile.bit_length()):
        here = ((spread >> (level - 1)) == 1) & (cols < rows)
        blend = jnp.where(here, tier[:, level : level + 1], blend)
    return blend


def local_kernel(query_ref, key_ref, value_ref, grad_ref, tier_ref, mixed_ref, dq_ref, dk_ref, dv_ref):
    length, width = query_ref.shape
    tile = min(TILE, length)
    count = length // tile
    inner = tile.bit_length()
    bits = count.bit_length() - 1
    span = [slice(i * tile, (i + 1) * tile) for i in range(count)]
    tiers = [tier_ref[rows, :] for rows in span]
    blends = [tile_blend(tier, tile) for tier in tiers]
    for col in head_slices(width):
        query = [query_ref[rows, col] for rows in span]
        key = [key_ref[rows, col] for rows in span]
        value = [value_ref[rows, col] for rows in span]
        grad = [grad_ref[rows, col] for rows in span]
        state = [dot_tn(key[i], value[i]) for i in range(count)] if count > 1 else []
        back = [None] * count
        for i in range(count):
            probs = (blends[i] * dot_nt(query[i], key[i])).astype(BF16)
            dscore = (blends[i] * dot_nt(grad[i], value[i])).astype(BF16)
            mixed = dot(probs, value[i])
            dq = dot(dscore, key[i])
            for b in range(bits):
                if not i >> b & 1:
                    continue
                first = ((i >> b) ^ 1) << b
                total = functools.reduce(jnp.add, state[first : first + (1 << b)]).astype(BF16)
                weight = tiers[i][:, inner + b : inner + b + 1]
                weighted = (weight * query[i].astype(F32)).astype(BF16)
                mixed = mixed + dot(weighted, total)
                dq = dq + weight * dot_nt(grad[i], total)
                reach = dot_tn(weighted, grad[i])
                for m in range(first, first + (1 << b)):
                    back[m] = reach if back[m] is None else back[m] + reach
            mixed_ref[span[i], col] = mixed
            dq_ref[span[i], col] = dq
            dk_ref[span[i], col] = dot_tn(dscore, query[i])
            dv_ref[span[i], col] = dot_tn(probs, grad[i])
        for i in range(count):
            if back[i] is not None:
                low = back[i].astype(BF16)
                dk_ref[span[i], col] += dot_nt(value[i], low)
                dv_ref[span[i], col] += dot(key[i], low)


def level_sums(got_refs, col, groups):
    sums, at = [], 0
    for count in groups:
        level = [ref[col, :].astype(F32) for ref in got_refs[at : at + count]]
        sums.append(functools.reduce(jnp.add, level))
        at += count
    return sums


def low_states(sums, spot_ref):
    kept = [(x * upper(spot_ref, j).astype(F32)).astype(BF16) for j, x in enumerate(sums)]
    return jnp.concatenate(kept, axis=0)


def low_back(sums, spot_ref):
    kept = [x * (1 - upper(spot_ref, j)).astype(F32) for j, x in enumerate(sums)]
    return functools.reduce(jnp.add, kept).astype(BF16)


def mixed_kernel(groups, spot_ref, mixed_ref, weighted_ref, *refs):
    got_refs, out_ref = refs[:-1], refs[-1]
    step = len(groups) * HEAD_DIM
    for i, col in enumerate(head_slices(mixed_ref.shape[1])):
        states = low_states(level_sums(got_refs, col, groups), spot_ref)
        far = dot(weighted_ref[:, i * step : (i + 1) * step], states)
        out_ref[:, col] = (mixed_ref[:, col] + far).astype(BF16)


def tail_kernel(tiers, groups, *refs):
    span = len(groups)
    place_ref, spot_ref, dq_ref, dk_ref, dv_ref, key_ref, value_ref, grad_ref, tier_ref, mixed_ref, weight_ref = refs[:11]
    got_refs = refs[11:-8]
    dq_out, dk_out, dv_out, part_ref, dq_low, dk_low, dv_low, sems = refs[-8:]
    scale = [tier_ref[:, tiers + j : tiers + j + 1] for j in range(span)]
    for col in head_slices(key_ref.shape[1]):
        sums = level_sums(got_refs, col, groups)
        back = low_back(sums, spot_ref)
        dk_low[:, col] = (dk_ref[:, col] + dot(value_ref[:, col], back)).astype(BF16)
        dv_low[:, col] = (dv_ref[:, col] + dot_nt(key_ref[:, col], back)).astype(BF16)
        far = dot_nt(grad_ref[:, col], low_states(sums, spot_ref))
        total = dq_ref[:, col]
        for j in range(span):
            total = total + scale[j] * far[:, j * HEAD_DIM : (j + 1) * HEAD_DIM]
        dq_low[:, col] = total.astype(BF16)
    copies = [
        pltpu.make_async_copy(src, dst, sems.at[n])
        for n, (src, dst) in enumerate([(dq_low, dq_out), (dk_low, dk_out), (dv_low, dv_out)])
    ]
    for copy in copies:
        copy.start()
    part_ref[...] = dot(mixed_ref[...], column(weight_ref, place_ref[0])[...])
    for copy in copies:
        copy.wait()


def layer_kernel(place_ref, part_ref, mixed_ref, weight_ref, out_hbm, out_low, sems):
    weight = column(weight_ref, place_ref[0])
    chunks = sems.shape[0]
    rows = part_ref.shape[0] // chunks
    copies = []
    for n in range(chunks):
        at = pl.ds(n * rows, rows)
        out_low[at, :] = (part_ref[at, :] + dot(mixed_ref[at, :], weight[...])).astype(BF16)
        copies.append(pltpu.make_async_copy(out_low.at[at, :], out_hbm.at[at, :], sems.at[n]))
        copies[-1].start()
    for copy in copies:
        copy.wait()


def swap_blocks(x, stride):
    return lax.ppermute(x, "seq", [(n, n ^ stride) for n in range(lax.axis_size("seq"))])


def add_low(a, b):
    return (a.astype(F32) + b.astype(F32)).astype(BF16)


def exchange_direct(sends):
    got = []
    for s in range(1, lax.axis_size("seq")):
        got.append(swap_blocks(sends[s.bit_length() - 1], s))
    return got, [1 << j for j in range(len(sends))]


def exchange_tree(state, reach, spot):
    got = []
    for j in range(len(reach)):
        from_state = swap_blocks(state, 1 << j)
        from_reach = [swap_blocks(x, 1 << j) for x in reach[j:]]
        got.append(jnp.where(spot >> j & 1 == 1, from_state, from_reach[0]))
        state = add_low(state, from_state)
        reach = reach[: j + 1] + [add_low(a, b) for a, b in zip(reach[j + 1 :], from_reach[1:])]
    return got, [1] * len(reach)


def on_device(query_in, key_in, value_in, level_mask, out_weight, grad_out):
    blocks = lax.axis_size("seq")
    span = blocks.bit_length() - 1
    if query_in.shape[0] != 1 or lax.axis_size("head") != 2 or blocks != 1 << span:
        raise ValueError("unsupported split")
    query, key, value, mask, grad = (x[0] for x in (query_in, key_in, value_in, level_mask, grad_out))
    length, width = query.shape
    half = grad.shape[1]
    tiers = length.bit_length()
    direct = blocks <= DIRECT
    place = lax.axis_index("head").astype(jnp.int32)[None]
    spot = lax.axis_index("seq").astype(jnp.int32)[None]
    swap = [(0, 1), (1, 0)]
    shape = jax.ShapeDtypeStruct
    dma = pltpu.SemaphoreType.DMA
    matrix = shape((width, HEAD_DIM), BF16)
    low = shape((length, width), BF16)
    high = shape((length, width), F32)
    low_buffer = pltpu.VMEM((length, width), BF16)
    half_buffer = pltpu.VMEM((length, half), BF16)
    unit = 2 * length * width * HEAD_DIM
    project = 2 * length * width * half

    grad_other = lax.ppermute(grad, "head", swap)
    state, part, weighted, tier = call(
        functools.partial(prep_kernel, tiers, span),
        [matrix, high, shape((length, span * width), BF16), shape((length, mask.shape[1]), F32)],
        [SMEM, VMEM] + [HBM] * 5,
        project + unit,
        (place, mask.T, *[pltpu.with_memory_space_constraint(x, pltpu.HBM) for x in (key, value, grad, out_weight, query)]),
        scratch=[low_buffer, low_buffer, half_buffer, pltpu.VMEM((width, half), BF16), low_buffer, dma((5,))],
        limit=12,
    )
    weight_other = lax.ppermute(out_weight, "head", swap)
    grad_mixed, *sends = call(
        functools.partial(reach_kernel, span, direct),
        [low] + [matrix] * span,
        [SMEM] * 2 + [VMEM] * 5,
        project + span * unit,
        (place, spot, grad_other, out_weight, part, weighted, state),
    )
    got, groups = exchange_direct(sends) if direct else exchange_tree(state, sends, spot)
    mixed, dq, dk, dv = call(local_kernel, [high] * 4, [VMEM] * 5, 12 * unit, (query, key, value, grad_mixed, tier))
    (mixed,) = call(
        functools.partial(mixed_kernel, groups),
        [low],
        [SMEM] + [VMEM] * (2 + len(got)),
        span * unit,
        (spot, mixed, weighted, *got),
    )
    mixed_other = lax.ppermute(mixed, "head", swap)
    grad_query, grad_key, grad_value, part = call(
        functools.partial(tail_kernel, tiers, groups),
        [low] * 3 + [shape((length, half), F32)],
        [SMEM] * 2 + [VMEM] * (9 + len(got)),
        project + (2 + span) * unit,
        (place, spot, dq, dk, dv, key, value, grad_mixed, tier, mixed, out_weight, *got),
        out_specs=[HBM] * 3 + [VMEM],
        scratch=[low_buffer] * 3 + [dma((3,))],
    )
    (layer_out,) = call(
        layer_kernel,
        [shape((length, half), BF16)],
        [SMEM] + [VMEM] * 3,
        project,
        (place, part, mixed_other, weight_other),
        out_specs=[HBM],
        scratch=[half_buffer, dma((4,))],
    )
    return tuple(x[None] for x in (layer_out, grad_query, grad_key, grad_value))


def solution(mesh):
    rows = P(("groups", "batch"), "seq", "head")
    return jax.shard_map(
        on_device,
        mesh=mesh,
        in_specs=(rows, rows, rows, P(("groups", "batch"), "seq", None), P("head", None), rows),
        out_specs=(rows,) * 4,
        check_vma=False,
    )
```

time: 51.5 us -> 28 us (0.54)
  the two profiles are of different devices: /device:TPU:0 before, /device:TPU:23 now
where the time goes in v2:
time: 28 us; the launch traced here: 27.8 us
  Pallas kernels  12.4 us (44%)
  waiting for transfers between devices  8.91 us (32%)
  starting transfers between devices  4.97 us (18%)
  local copies, waits for them, and re-layouts  0.77 us (3%)
  between operations  0.7 us (2%)
    pallas_call x6, Pallas kernels, call(): pl.pallas_call(kernel, out_shape=outs, in_specs=in_specs, out_specs=out_s...  12.4 us
    ppermute x3, waiting for transfers between devices, swap_blocks(): lax.ppermute(x, 'seq', [(n, n ^ stride) for n in range(lax.axis_size('seq...  7.33 us
    ppermute x3, starting transfers between devices, swap_blocks(): lax.ppermute(x, 'seq', [(n, n ^ stride) for n in range(lax.axis_size('seq...  3.61 us
    ppermute x1, waiting for transfers between devices, on_device(): grad_other = lax.ppermute(grad, 'head', swap)  1.58 us
    unnamed x10, local copies, waits for them, and re-layouts  0.77 us
    ppermute x1, starting transfers between devices, on_device(): weight_other = lax.ppermute(out_weight, 'head', swap)  0.74 us
  transfers between devices with their start and end apart: 6, of which 3 were waited for; matrix products, arithmetic and copies ran while one was open for 0% of the time, Pallas kernels for 39%

profile of v2, /device:TPU:23, one launch (start us, length us, event | category | flops | bytes accessed | tf_op | source)
XLA Modules:
  0.0 27.8 jit_solution(13928486327071589713)
XLA Ops:
  0.6 0.7 %collective-permute-start.5 = (bf16[512,2048]{1,0:T(8,128)(2,1)}, bf16[512,2048]{1,0:T(8,128)(2,1)S(1)}, u32[]{:S(2)}, u32[]{:S(2)}) collective-permute-start(bf16[512,2048]{1,0:T(8,128)(2,1)} %refs_10_.1), channel_id=1, source_target_pairs={{0,1},{1,0},{2,3},{3,2},{4,5},{5,4},{6,7},{7,6},{8,9},{9,8},{10,11... | collective-permute-start | bytes 6291464 | tf_op jit(solution)/shard_map/ppermute | solution.py:294
  1.4 0.1 collective-permute-start
  1.5 0.0 copy-start.4
  1.5 0.8 %copy-done.4 = s32[1,512,16]{1,2,0:T(8,128)S(1)} copy-done((s32[1,512,16]{1,2,0:T(8,128)S(1)}, s32[1,512,16]{1,2,0:T(8,128)}, u32[]{:S(2)}) %copy-start.4) | copy-done | bytes 32792
  2.2 3.1 %shard_map.93 = (bf16[512,128]{1,0:T(8,128)(2,1)S(1)}, f32[512,512]{1,0:T(8,128)S(1)}, bf16[512,1024]{1,0:T(8,128)(2,1)S(1)}, f32[512,16]{1,0:T(8,128)S(1)}) custom-call(s32[1]{0:T(128)} %bitcast.refs_0_.place_ref, s32[16,512]{1,0:T(8,128)S(1)} %bitcast.21, bf16[512,512]{1,0:T(8,128)(2,1)} %bitcast.13, bf16[512,512]{1,0:T(8,128)(2,1)} %bitcast.16, ...), custom_call_target="tpu_custom_call" | custom-call | flops 603979776 | bytes 7012356 | tf_op jit(solution)/shard_map/pallas_call | solution.py:39
  5.3 1.6 %collective-permute-done.grad_ref = bf16[512,1024]{1,0:T(8,128)(2,1)S(1)} collective-permute-done((bf16[512,1024]{1,0:T(8,128)(2,1)}, bf16[512,1024]{1,0:T(8,128)(2,1)S(1)}, u32[]{:S(2)}, u32[]{:S(2)}) %collective-permute-start) | collective-permute-done | bytes 1048608 | tf_op jit(solution)/shard_map/ppermute | solution.py:284
  6.9 0.0 copy-done
  6.9 1.1 %shard_map.94 = (bf16[512,512]{1,0:T(8,128)(2,1)S(1)}, bf16[512,128]{1,0:T(8,128)(2,1)S(1)}, bf16[512,128]{1,0:T(8,128)(2,1)S(1)}) custom-call(s32[1]{0:T(128)} %bitcast.refs_0_.place_ref, s32[1]{0:T(128)} %bitcast.1.spot_ref.refs_1_, bf16[512,1024]{1,0:T(8,128)(2,1)S(1)} %collective-permute-done.grad_ref, bf16[512,2048]{1,0:T(8,128)(2,1)S(1)} %copy-done, ...), custom_call_target="tpu_custom_call" | custom-call | flops 671088640 | bytes 6160392 | tf_op jit(solution)/shard_map/pallas_call | solution.py:39
  8.0 0.1 collective-permute-start.2
  8.1 2.4 %collective-permute-start.3 = (bf16[512,128]{1,0:T(8,128)(2,1)S(1)}, bf16[512,128]{1,0:T(8,128)(2,1)S(1)}, u32[]{:S(2)}, u32[]{:S(2)}) collective-permute-start(bf16[512,128]{1,0:T(8,128)(2,1)S(1)} %get-tuple-element.29), channel_id=1, source_target_pairs={{0,12},{4,8},{8,4},{12,0},{1,13},{5,9},{9,5},{13,1},{2,14},{6,10},... | collective-permute-start | bytes 393224 | tf_op jit(solution)/shard_map/ppermute | solution.py:236
  10.5 1.1 %collective-permute-start.1 = (bf16[512,128]{1,0:T(8,128)(2,1)S(1)}, bf16[512,128]{1,0:T(8,128)(2,1)S(1)}, u32[]{:S(2)}, u32[]{:S(2)}) collective-permute-start(bf16[512,128]{1,0:T(8,128)(2,1)S(1)} %get-tuple-element.28), channel_id=1, source_target_pairs={{0,4},{4,0},{8,12},{12,8},{1,5},{5,1},{9,13},{13,9},{2,6},{6,2},{1... | collective-permute-start | bytes 393224 | tf_op jit(solution)/shard_map/ppermute | solution.py:236
  11.6 0.0 copy-done.1
  11.6 0.0 copy-done.2
  11.6 0.0 copy-done.3
  11.6 3.9 %shard_map.95 = (f32[512,512]{1,0:T(8,128)S(1)}, f32[512,512]{1,0:T(8,128)S(1)}, f32[512,512]{1,0:T(8,128)S(1)}, f32[512,512]{1,0:T(8,128)S(1)}) custom-call(bf16[512,512]{1,0:T(8,128)(2,1)S(1)} %bitcast.20, bf16[512,512]{1,0:T(8,128)(2,1)S(1)} %bitcast.14, bf16[512,512]{1,0:T(8,128)(2,1)S(1)} %bitcast.17, ...), custom_call_target="tpu_custom_call" | custom-call | flops 805306368 | bytes 6324224 | tf_op jit(solution)/shard_map/pallas_call | solution.py:39
  15.5 0.5 %collective-permute-done.2.refs_1_.refs_12_ = bf16[512,128]{1,0:T(8,128)(2,1)S(1)} collective-permute-done((bf16[512,128]{1,0:T(8,128)(2,1)S(1)}, bf16[512,128]{1,0:T(8,128)(2,1)S(1)}, u32[]{:S(2)}, u32[]{:S(2)}) %collective-permute-start.2) | collective-permute-done | bytes 131104 | tf_op jit(solution)/shard_map/ppermute | solution.py:236
  16.0 6.8 %collective-permute-done.3.refs_2_.refs_13_ = bf16[512,128]{1,0:T(8,128)(2,1)S(1)} collective-permute-done((bf16[512,128]{1,0:T(8,128)(2,1)S(1)}, bf16[512,128]{1,0:T(8,128)(2,1)S(1)}, u32[]{:S(2)}, u32[]{:S(2)}) %collective-permute-start.3) | collective-permute-done | bytes 131104 | tf_op jit(solution)/shard_map/ppermute | solution.py:236
  22.8 0.0 collective-permute-done.1.refs_0_.refs_11_
  22.8 0.4 %shard_map.96.refs_9_ = bf16[512,512]{1,0:T(8,128)(2,1)S(1)} custom-call(s32[1]{0:T(128)} %bitcast.1.spot_ref.refs_1_, f32[512,512]{1,0:T(8,128)S(1)} %get-tuple-element.27.mixed_ref, bf16[512,1024]{1,0:T(8,128)(2,1)S(1)} %get-tuple-element.20.weighted_ref, bf16[512,128]{1,0:T(8,128)(2,1)S(1)} %collective-permute-done.1.refs_0_.refs_11_, ...), custom_call_target="tpu_custom_call" | custom-call | flops 134217728 | bytes 3014660 | tf_op jit(solution)/shard_map/pallas_call | solution.py:39
  23.3 0.5 %collective-permute-start.4 = (bf16[512,512]{1,0:T(8,128)(2,1)S(1)}, bf16[512,512]{1,0:T(8,128)(2,1)S(1)}, u32[]{:S(2)}, u32[]{:S(2)}) collective-permute-start(bf16[512,512]{1,0:T(8,128)(2,1)S(1)} %shard_map.96.refs_9_), channel_id=1, source_target_pairs={{0,1},{1,0},{2,3},{3,2},{4,5},{5,4},{6,7},{7,6},{8,9},{9,8},{10,11... | collective-permute-start | bytes 1572872 | tf_op jit(solution)/shard_map/ppermute | solution.py:311
  23.8 2.4 %shard_map.97 = (bf16[512,512]{1,0:T(8,128)(2,1)}, bf16[512,512]{1,0:T(8,128)(2,1)}, bf16[512,512]{1,0:T(8,128)(2,1)}, f32[512,1024]{1,0:T(8,128)S(1)}) custom-call(s32[1]{0:T(128)} %bitcast.refs_0_.place_ref, s32[1]{0:T(128)} %bitcast.1.spot_ref.refs_1_, f32[512,512]{1,0:T(8,128)S(1)} %get-tuple-element.24.refs_2_, ...), custom_call_target="tpu_custom_call" | custom-call | flops 805306368 | bytes 11436040 | tf_op jit(solution)/shard_map/pallas_call | solution.py:39
  26.2 0.0 collective-permute-done.4.mixed_ref
  26.3 0.0 collective-permute-done.5.weight_ref
  26.3 1.5 %shard_map.98 = bf16[512,1024]{1,0:T(8,128)(2,1)} custom-call(s32[1]{0:T(128)} %bitcast.refs_0_.place_ref, f32[512,1024]{1,0:T(8,128)S(1)} %get-tuple-element.30.part_ref, bf16[512,512]{1,0:T(8,128)(2,1)S(1)} %collective-permute-done.4.mixed_ref, bf16[512,2048]{1,0:T(8,128)(2,1)S(1)} %collective-permute-done.5.weight_ref), custom_call_target="tpu_custom_call" | custom-call | flops 536870912 | bytes 5767172 | tf_op jit(solution)/shard_map/pallas_call | solution.py:39
  (4 shorter events, 0.0 us)
Async XLA Ops:
  0.6 25.6 %collective-permute-start.5 = (bf16[512,2048]{1,0:T(8,128)(2,1)}, bf16[512,2048]{1,0:T(8,128)(2,1)S(1)}, u32[]{:S(2)}, u32[]{:S(2)}) collective-permute-start(bf16[512,2048]{1,0:T(8,128)(2,1)} %refs_10_.1), channel_id=1, source_target_pairs={{0,1},{1,0},{2,3},{3,2},{4,5},{5,4},{6,7},{7,6},{8,9},{9,8},{10,11... | collective-permute-start | bytes 6291464 | tf_op jit(solution)/shard_map/ppermute | solution.py:294
  1.4 5.5 %collective-permute-start = (bf16[512,1024]{1,0:T(8,128)(2,1)}, bf16[512,1024]{1,0:T(8,128)(2,1)S(1)}, u32[]{:S(2)}, u32[]{:S(2)}) collective-permute-start(bf16[512,1024]{1,0:T(8,128)(2,1)} %bitcast.22), channel_id=1, source_target_pairs={{0,1},{1,0},{2,3},{3,2},{4,5},{5,4},{6,7},{7,6},{8,9},{9,8},{10,11... | collective-permute-start | bytes 3145736 | tf_op jit(solution)/shard_map/ppermute | solution.py:284
  1.5 0.8 %copy-start.4 = (s32[1,512,16]{1,2,0:T(8,128)S(1)}, s32[1,512,16]{1,2,0:T(8,128)}, u32[]{:S(2)}) copy-start(s32[1,512,16]{1,2,0:T(8,128)} %param.9) | copy-start | bytes 98308
  2.2 4.7 %copy-start = (bf16[512,2048]{1,0:T(8,128)(2,1)S(1)}, bf16[512,2048]{1,0:T(8,128)(2,1)}, u32[]{:S(2)}) copy-start(bf16[512,2048]{1,0:T(8,128)(2,1)} %refs_10_.1) | copy-start | bytes 6291460
  6.9 4.7 %copy-start.1 = (bf16[1,512,512]{2,1,0:T(8,128)(2,1)S(1)}, bf16[1,512,512]{2,1,0:T(8,128)(2,1)}, u32[]{:S(2)}) copy-start(bf16[1,512,512]{2,1,0:T(8,128)(2,1)} %param.7) | copy-start | bytes 1572868
  6.9 4.7 %copy-start.2 = (bf16[1,512,512]{2,1,0:T(8,128)(2,1)S(1)}, bf16[1,512,512]{2,1,0:T(8,128)(2,1)}, u32[]{:S(2)}) copy-start(bf16[1,512,512]{2,1,0:T(8,128)(2,1)} %param.8) | copy-start | bytes 1572868
  6.9 4.7 %copy-start.3 = (bf16[1,512,512]{2,1,0:T(8,128)(2,1)S(1)}, bf16[1,512,512]{2,1,0:T(8,128)(2,1)}, u32[]{:S(2)}) copy-start(bf16[1,512,512]{2,1,0:T(8,128)(2,1)} %param.6) | copy-start | bytes 1572868
  8.0 8.1 %collective-permute-start.2 = (bf16[512,128]{1,0:T(8,128)(2,1)S(1)}, bf16[512,128]{1,0:T(8,128)(2,1)S(1)}, u32[]{:S(2)}, u32[]{:S(2)}) collective-permute-start(bf16[512,128]{1,0:T(8,128)(2,1)S(1)} %get-tuple-element.29), channel_id=1, source_target_pairs={{0,8},{4,12},{8,0},{12,4},{1,9},{5,13},{9,1},{13,5},{2,10},{6,14},... | collective-permute-start | bytes 393224 | tf_op jit(solution)/shard_map/ppermute | solution.py:236
  8.1 14.7 %collective-permute-start.3 = (bf16[512,128]{1,0:T(8,128)(2,1)S(1)}, bf16[512,128]{1,0:T(8,128)(2,1)S(1)}, u32[]{:S(2)}, u32[]{:S(2)}) collective-permute-start(bf16[512,128]{1,0:T(8,128)(2,1)S(1)} %get-tuple-element.29), channel_id=1, source_target_pairs={{0,12},{4,8},{8,4},{12,0},{1,13},{5,9},{9,5},{13,1},{2,14},{6,10},... | collective-permute-start | bytes 393224 | tf_op jit(solution)/shard_map/ppermute | solution.py:236
  10.5 12.3 %collective-permute-start.1 = (bf16[512,128]{1,0:T(8,128)(2,1)S(1)}, bf16[512,128]{1,0:T(8,128)(2,1)S(1)}, u32[]{:S(2)}, u32[]{:S(2)}) collective-permute-start(bf16[512,128]{1,0:T(8,128)(2,1)S(1)} %get-tuple-element.28), channel_id=1, source_target_pairs={{0,4},{4,0},{8,12},{12,8},{1,5},{5,1},{9,13},{13,9},{2,6},{6,2},{1... | collective-permute-start | bytes 393224 | tf_op jit(solution)/shard_map/ppermute | solution.py:236
  23.3 3.0 %collective-permute-start.4 = (bf16[512,512]{1,0:T(8,128)(2,1)S(1)}, bf16[512,512]{1,0:T(8,128)(2,1)S(1)}, u32[]{:S(2)}, u32[]{:S(2)}) collective-permute-start(bf16[512,512]{1,0:T(8,128)(2,1)S(1)} %shard_map.96.refs_9_), channel_id=1, source_target_pairs={{0,1},{1,0},{2,3},{3,2},{4,5},{5,4},{6,7},{7,6},{8,9},{9,8},{10,11... | collective-permute-start | bytes 1572872 | tf_op jit(solution)/shard_map/ppermute | solution.py:311

commit v3 on v2

v3 whole, which is shorter than its diff:
```python
import functools

import jax
import jax.numpy as jnp
from jax import lax
from jax.experimental import pallas as pl
from jax.experimental.pallas import tpu as pltpu
from jax.sharding import PartitionSpec as P

HEAD_DIM = 128
TILE = 256
F32 = jnp.float32
BF16 = jnp.bfloat16
VMEM = pl.BlockSpec(memory_space=pltpu.VMEM)
SMEM = pl.BlockSpec(memory_space=pltpu.SMEM)
HBM = pl.BlockSpec(memory_space=pltpu.HBM)


def level_scale(level):
    return 1.0 if level == 0 else 2.0 ** (-(level - 1) / 2.0)


def dot(a, b):
    return lax.dot_general(a, b, (((1,), (0,)), ((), ())), preferred_element_type=F32)


def dot_nt(a, b):
    return lax.dot_general(a, b, (((1,), (1,)), ((), ())), preferred_element_type=F32)


def dot_tn(a, b):
    return lax.dot_general(a, b, (((0,), (0,)), ((), ())), preferred_element_type=F32)


def call(kernel, outs, in_specs, flops, args, out_specs=None, scratch=(), limit=16):
    moved = sum(a.size * a.dtype.itemsize for a in args)
    moved += sum(o.size * o.dtype.itemsize for o in outs)
    return pl.pallas_call(
        kernel,
        out_shape=outs,
        in_specs=in_specs,
        out_specs=out_specs or [VMEM] * len(outs),
        scratch_shapes=list(scratch),
        compiler_params=pltpu.CompilerParams(vmem_limit_bytes=limit << 20),
        cost_estimate=pl.CostEstimate(flops=flops, bytes_accessed=moved, transcendentals=0),
    )(*args)


def head_slices(width):
    return [slice(i * HEAD_DIM, (i + 1) * HEAD_DIM) for i in range(width // HEAD_DIM)]


def upper(spot_ref, bit):
    return (spot_ref[0] >> bit) & 1


def column(ref, index):
    half = ref.shape[1] // 2
    return ref.at[:, pl.ds(pl.multiple_of(index * half, half), half)]


def start_copies(pairs, sems):
    copies = [pltpu.make_async_copy(src, dst, sems.at[n]) for n, (src, dst) in enumerate(pairs)]
    for copy in copies:
        copy.start()
    return copies


def state_kernel(place_ref, spot_ref, mask_hbm, key_hbm, value_hbm, grad_hbm, weight_hbm, query_hbm, *refs):
    state_ref, tier_ref, key, value, grad, weight, query, mask, sems = refs
    mine = column(weight_hbm, place_ref[0])
    sources = [key_hbm, value_hbm, mask_hbm, mine, grad_hbm, query_hbm]
    copies = start_copies(zip(sources, [key, value, mask, weight, grad, query]), sems)
    copies[0].wait()
    copies[1].wait()
    for col in head_slices(key.shape[1]):
        state_ref[col, :] = dot_tn(key[:, col], value[:, col]).astype(BF16)
    copies[2].wait()
    levels = mask[...].astype(F32)
    rows = [levels[l : l + 1] * jnp.float32(level_scale(l)) for l in range(levels.shape[0])]
    tier_ref[...] = jnp.transpose(jnp.concatenate(rows, axis=0))
    for copy in copies[3:]:
        copy.wait()


def own_kernel(tiers, span, place_ref, grad_ref, weight_ref, query_ref, tier_ref, weight_hbm, *refs):
    part_ref, weighted_ref, other_ref, sems = refs
    copies = start_copies([(column(weight_hbm, 1 - place_ref[0]), other_ref)], sems)
    part_ref[...] = dot_nt(grad_ref[...], weight_ref[...])
    length, width = query_ref.shape
    for j in range(span):
        scale = jnp.broadcast_to(tier_ref[:, tiers + j : tiers + j + 1], (length, HEAD_DIM))
        for i, col in enumerate(head_slices(width)):
            at = (i * span + j) * HEAD_DIM
            weighted_ref[:, at : at + HEAD_DIM] = (scale * query_ref[:, col].astype(F32)).astype(BF16)
    copies[0].wait()


def reach_kernel(span, spot_ref, grad_ref, weight_ref, part_ref, weighted_ref, state_ref, *outs):
    grad_mixed_ref, send_refs = outs[0], outs[1:]
    grad_mixed = (part_ref[...] + dot_nt(grad_ref[...], weight_ref[...])).astype(BF16)
    grad_mixed_ref[...] = grad_mixed
    step = span * HEAD_DIM
    for i, col in enumerate(head_slices(grad_mixed.shape[1])):
        reach = dot_tn(grad_mixed[:, col], weighted_ref[:, i * step : (i + 1) * step])
        state = state_ref[col, :].astype(F32)
        for j in range(span):
            send = jnp.where(upper(spot_ref, j) > 0, reach[:, j * HEAD_DIM : (j + 1) * HEAD_DIM], state)
            send_refs[j][col, :] = send.astype(BF16)


def add_kernel(a_ref, b_ref, out_ref):
    out_ref[...] = (a_ref[...].astype(F32) + b_ref[...].astype(F32)).astype(BF16)


def tile_blend(tier, tile):
    rows = lax.broadcasted_iota(jnp.int32, (tile, tile), 0)
    cols = lax.broadcasted_iota(jnp.int32, (tile, tile), 1)
    spread = rows ^ cols
    blend = jnp.where(spread == 0, tier[:, 0:1], 0.0)
    for level in range(1, tile.bit_length()):
        here = ((spread >> (level - 1)) == 1) & (cols < rows)
        blend = jnp.where(here, tier[:, level : level + 1], blend)
    return blend


def tiles_of(length):
    tile = min(TILE, length)
    return tile, [slice(i * tile, (i + 1) * tile) for i in range(length // tile)]


def sibling_tiles(count):
    for i in range(count):
        for b in range(count.bit_length() - 1):
            if i >> b & 1:
                first = ((i >> b) ^ 1) << b
                yield i, b, range(first, first + (1 << b))


def forward_kernel(query_ref, key_ref, value_ref, tier_ref, mixed_ref, probs_ref, blend_ref, state_ref):
    length, width = query_ref.shape
    tile, spans = tiles_of(length)
    inner = tile.bit_length()
    for rows in spans:
        blend_ref[rows, :] = tile_blend(tier_ref[rows, :], tile)
    for h, col in enumerate(head_slices(width)):
        mixed = []
        for rows in spans:
            probs = (blend_ref[rows, :] * dot_nt(query_ref[rows, col], key_ref[rows, col])).astype(BF16)
            probs_ref[rows, h * tile : (h + 1) * tile] = probs
            mixed.append(dot(probs, value_ref[rows, col]))
        states = [dot_tn(key_ref[rows, col], value_ref[rows, col]) for rows in spans[:-1]]
        for n, (i, b, members) in enumerate(sibling_tiles(len(spans))):
            total = functools.reduce(jnp.add, [states[m] for m in members]).astype(BF16)
            state_ref[n, col, :] = total
            weight = tier_ref[spans[i], inner + b : inner + b + 1]
            weighted = (weight * query_ref[spans[i], col].astype(F32)).astype(BF16)
            mixed[i] = mixed[i] + dot(weighted, total)
        for rows, value in zip(spans, mixed):
            mixed_ref[rows, col] = value


def backward_kernel(query_ref, key_ref, value_ref, grad_ref, tier_ref, probs_ref, blend_ref, state_ref, *outs):
    dq_ref, dk_ref, dv_ref = outs
    length, width = query_ref.shape
    tile, spans = tiles_of(length)
    inner = tile.bit_length()
    for h, col in enumerate(head_slices(width)):
        dq, dk, dv = [], [], []
        for rows in spans:
            query, key, value, grad = (ref[rows, col] for ref in (query_ref, key_ref, value_ref, grad_ref))
            dscore = (blend_ref[rows, :] * dot_nt(grad, value)).astype(BF16)
            dq.append(dot(dscore, key))
            dk.append(dot_tn(dscore, query))
            dv.append(dot_tn(probs_ref[rows, h * tile : (h + 1) * tile], grad))
        backs = [None] * len(spans)
        for n, (i, b, members) in enumerate(sibling_tiles(len(spans))):
            grad = grad_ref[spans[i], col]
            weight = tier_ref[spans[i], inner + b : inner + b + 1]
            weighted = (weight * query_ref[spans[i], col].astype(F32)).astype(BF16)
            dq[i] = dq[i] + weight * dot_nt(grad, state_ref[n, col, :])
            reach = dot_tn(grad, weighted)
            for m in members:
                backs[m] = reach if backs[m] is None else backs[m] + reach
        for m, rows in enumerate(spans):
            if backs[m] is not None:
                low = backs[m].astype(BF16)
                dk[m] = dk[m] + dot(value_ref[rows, col], low)
                dv[m] = dv[m] + dot_nt(key_ref[rows, col], low)
            dq_ref[rows, col] = dq[m]
            dk_ref[rows, col] = dk[m]
            dv_ref[rows, col] = dv[m]


def low_states(state_refs, col, spot_ref):
    kept = [(ref[col, :].astype(F32) * upper(spot_ref, j).astype(F32)).astype(BF16) for j, ref in enumerate(state_refs)]
    return jnp.concatenate(kept, axis=0)


def low_back(back_refs, col, spot_ref):
    kept = [ref[col, :].astype(F32) * (1 - upper(spot_ref, j)).astype(F32) for j, ref in enumerate(back_refs)]
    return functools.reduce(jnp.add, kept).astype(BF16)


def mixed_kernel(spot_ref, mixed_ref, weighted_ref, *refs):
    state_refs, out_ref = refs[:-1], refs[-1]
    step = len(state_refs) * HEAD_DIM
    for i, col in enumerate(head_slices(mixed_ref.shape[1])):
        far = dot(weighted_ref[:, i * step : (i + 1) * step], low_states(state_refs, col, spot_ref))
        out_ref[:, col] = (mixed_ref[:, col] + far).astype(BF16)


def query_kernel(tiers, span, spot_ref, dq_ref, dk_ref, dv_ref, key_ref, value_ref, grad_ref, tier_ref, *refs):
    mixed_ref, weight_ref = refs[:2]
    got_refs = refs[2:-4]
    dq_low, dk_low, dv_low, part_ref = refs[-4:]
    scale = [tier_ref[:, tiers + j : tiers + j + 1] for j in range(span)]
    for col in head_slices(dq_ref.shape[1]):
        far = dot_nt(grad_ref[:, col], low_states(got_refs, col, spot_ref))
        total = dq_ref[:, col]
        for j in range(span):
            total = total + scale[j] * far[:, j * HEAD_DIM : (j + 1) * HEAD_DIM]
        dq_low[:, col] = total.astype(BF16)
        back = low_back(got_refs, col, spot_ref)
        dk_low[:, col] = (dk_ref[:, col] + dot(value_ref[:, col], back)).astype(BF16)
        dv_low[:, col] = (dv_ref[:, col] + dot_nt(key_ref[:, col], back)).astype(BF16)
    part_ref[...] = dot(mixed_ref[...], weight_ref[...])


def last_kernel(part_ref, mixed_ref, weight_ref, dq_low, dk_low, dv_low, out_hbm, dq_hbm, dk_hbm, dv_hbm, out_low, sems):
    chunks = sems.shape[0] - 3
    rows = part_ref.shape[0] // chunks
    copies = []

    def send(src, dst):
        copies.append(pltpu.make_async_copy(src, dst, sems.at[len(copies)]))
        copies[-1].start()

    send(dq_low, dq_hbm)
    send(dk_low, dk_hbm)
    send(dv_low, dv_hbm)
    for n in range(chunks):
        at = pl.ds(n * rows, rows)
        out_low[at, :] = (part_ref[at, :] + dot(mixed_ref[at, :], weight_ref[...])).astype(BF16)
        send(out_low.at[at, :], out_hbm.at[at, :])
    for copy in copies:
        copy.wait()


def swap_blocks(x, level):
    return lax.ppermute(x, "seq", [(n, n ^ 1 << level) for n in range(lax.axis_size("seq"))])


def add_low(a, b):
    return call(add_kernel, [jax.ShapeDtypeStruct(a.shape, BF16)], [VMEM] * 2, a.size, (a, b), limit=4)[0]


def hbm(*arrays):
    return [pltpu.with_memory_space_constraint(x, pltpu.HBM) for x in arrays]


def on_device(query_in, key_in, value_in, level_mask, out_weight, grad_out):
    blocks = lax.axis_size("seq")
    span = blocks.bit_length() - 1
    if query_in.shape[0] != 1 or lax.axis_size("head") != 2 or blocks != 1 << span:
        raise ValueError("unsupported split")
    query, key, value, mask, grad = (x[0] for x in (query_in, key_in, value_in, level_mask, grad_out))
    length, width = query.shape
    half = grad.shape[1]
    tiers = length.bit_length()
    tile, spans = tiles_of(length)
    siblings = max(1, len(list(sibling_tiles(len(spans)))))
    place = lax.axis_index("head").astype(jnp.int32)[None]
    spot = lax.axis_index("seq").astype(jnp.int32)[None]
    swap = [(0, 1), (1, 0)]
    shape = jax.ShapeDtypeStruct
    dma = pltpu.SemaphoreType.DMA
    matrix = shape((width, HEAD_DIM), BF16)
    low = shape((length, width), BF16)
    high = shape((length, width), F32)
    wide = shape((length, half), BF16)
    low_buffer = pltpu.VMEM((length, width), BF16)
    unit = 2 * length * width * HEAD_DIM
    project = 2 * length * width * half

    grad_other = lax.ppermute(grad, "head", swap)
    state, tier, key, value, grad_own, weight_own, query = call(
        state_kernel,
        [matrix, shape((length, mask.shape[1]), F32), low, low, wide, shape((width, half), BF16), low],
        [SMEM] * 2 + [HBM] * 6,
        unit,
        (place, spot, *hbm(mask.T, key, value, grad, out_weight, query)),
        scratch=[pltpu.VMEM(mask.shape[::-1], mask.dtype), dma((6,))],
    )
    part, weighted, weight_rest = call(
        functools.partial(own_kernel, tiers, span),
        [high, shape((length, span * width), BF16), shape((width, half), BF16)],
        [SMEM] + [VMEM] * 4 + [HBM],
        project,
        (place, grad_own, weight_own, query, tier, *hbm(out_weight)),
        scratch=[dma((1,))],
    )
    grad_mixed, *sends = call(
        functools.partial(reach_kernel, span),
        [low] + [matrix] * span,
        [SMEM] + [VMEM] * 5,
        project + span * unit,
        (spot, grad_other, weight_rest, part, weighted, state),
    )
    weight_other = lax.ppermute(weight_rest, "head", swap)
    mixed, probs, blend, inner = call(
        forward_kernel,
        [high, shape((length, width // HEAD_DIM * tile), BF16), shape((length, tile), F32)]
        + [shape((siblings, width, HEAD_DIM), BF16)],
        [VMEM] * 4,
        4 * unit,
        (query, key, value, tier),
    )
    got = []
    for level, total in enumerate(sends):
        for step in range(level):
            total = add_low(total, swap_blocks(total, step))
        got.append(swap_blocks(total, level))
    dq, dk, dv = call(
        backward_kernel, [high] * 3, [VMEM] * 8, 8 * unit, (query, key, value, grad_mixed, tier, probs, blend, inner)
    )
    (mixed,) = call(mixed_kernel, [low], [SMEM] + [VMEM] * (2 + span), span * unit, (spot, mixed, weighted, *got))
    mixed_other = lax.ppermute(mixed, "head", swap)
    *lows, part = call(
        functools.partial(query_kernel, tiers, span),
        [low] * 3 + [shape((length, half), F32)],
        [SMEM] + [VMEM] * (9 + span),
        project + (2 + span) * unit,
        (spot, dq, dk, dv, key, value, grad_mixed, tier, mixed, weight_own, *got),
    )
    layer_out, grad_query, grad_key, grad_value = call(
        last_kernel,
        [wide, low, low, low],
        [VMEM] * 6,
        project,
        (part, mixed_other, weight_other, *lows),
        out_specs=[HBM] * 4,
        scratch=[pltpu.VMEM((length, half), BF16), dma((7,))],
    )
    return tuple(x[None] for x in (layer_out, grad_query, grad_key, grad_value))


def solution(mesh):
    rows = P(("groups", "batch"), "seq", "head")
    return jax.shard_map(
        on_device,
        mesh=mesh,
        in_specs=(rows, rows, rows, P(("groups", "batch"), "seq", None), P("head", None), rows),
        out_specs=(rows,) * 4,
        check_vma=False,
    )
```

time: 28 us -> 27.6 us (0.986)
  the two profiles are of different devices: /device:TPU:23 before, /device:TPU:0 now
where the time goes in v3:
time: 27.6 us; the launch traced here: 27.4 us
  Pallas kernels  12.6 us (46%)
  waiting for transfers between devices  7.09 us (26%)
  starting transfers between devices  7.01 us (25%)
  between operations  0.72 us (3%)
    pallas_call x9, Pallas kernels, call(): pl.pallas_call(kernel, out_shape=outs, in_specs=in_specs, out_specs=out_s...  12.6 us
    ppermute x3, waiting for transfers between devices, swap_blocks(): lax.ppermute(x, 'seq', [(n, n ^ 1 << level) for n in range(lax.axis_size(...  7.08 us
    ppermute x3, starting transfers between devices, swap_blocks(): lax.ppermute(x, 'seq', [(n, n ^ 1 << level) for n in range(lax.axis_size(...  6.29 us
    ppermute x1, starting transfers between devices, on_device(): grad_other = lax.ppermute(grad, 'head', swap)  0.56 us
  transfers between devices with their start and end apart: 6, of which 2 were waited for; matrix products, arithmetic and copies ran while one was open for 0% of the time, Pallas kernels for 40%

profile of v3, /device:TPU:0, one launch (start us, length us, event | category | flops | bytes accessed | tf_op | source)
XLA Modules:
  0.0 27.4 jit_solution(1352938359282121810)
XLA Ops:
  0.6 0.6 %collective-permute-start = (bf16[512,1024]{1,0:T(8,128)(2,1)}, bf16[512,1024]{1,0:T(8,128)(2,1)S(1)}, u32[]{:S(2)}, u32[]{:S(2)}) collective-permute-start(bf16[512,1024]{1,0:T(8,128)(2,1)} %bitcast.13), channel_id=1, source_target_pairs={{0,1},{1,0},{2,3},{3,2},{4,5},{5,4},{6,7},{7,6},{8,9},{9,8},{10,11... | collective-permute-start | bytes 3145736 | tf_op jit(solution)/shard_map/ppermute | solution.py:286
  1.2 2.1 %shard_map.93 = (bf16[512,128]{1,0:T(8,128)(2,1)S(1)}, f32[512,16]{1,0:T(8,128)S(1)}, bf16[512,512]{1,0:T(8,128)(2,1)S(1)}, bf16[512,512]{1,0:T(8,128)(2,1)S(1)}...) custom-call(s32[1]{0:T(128)} %bitcast.1.place_ref, s32[1]{0:T(128)} %bitcast.spot_ref, ...), custom_call_target="tpu_custom_call" | custom-call | flops 67108864 | bytes 8585224 | tf_op jit(solution)/shard_map/pallas_call | solution.py:38
  3.3 1.3 %shard_map.94 = (f32[512,512]{1,0:T(8,128)S(1)}, bf16[512,1024]{1,0:T(8,128)(2,1)S(1)}, bf16[512,1024]{1,0:T(8,128)(2,1)S(1)}) custom-call(s32[1]{0:T(128)} %bitcast.1.place_ref, bf16[512,1024]{1,0:T(8,128)(2,1)S(1)} %get-tuple-element.35.grad_ref, bf16[512,1024]{1,0:T(8,128)(2,1)S(1)} %get-tuple-element.36.weight_ref.refs_1_, ...), custom_call_target="tpu_custom_call" | custom-call | flops 536870912 | bytes 7897092 | tf_op jit(solution)/shard_map/pallas_call | solution.py:38
  4.5 0.1 collective-permute-start.5
  4.6 0.0 collective-permute-done.grad_ref
  4.6 1.1 %shard_map.95 = (bf16[512,512]{1,0:T(8,128)(2,1)S(1)}, bf16[512,128]{1,0:T(8,128)(2,1)S(1)}, bf16[512,128]{1,0:T(8,128)(2,1)S(1)}) custom-call(s32[1]{0:T(128)} %bitcast.spot_ref, bf16[512,1024]{1,0:T(8,128)(2,1)S(1)} %collective-permute-done.grad_ref, bf16[512,1024]{1,0:T(8,128)(2,1)S(1)} %get-tuple-element.38.weight_ref, ...), custom_call_target="tpu_custom_call" | custom-call | flops 671088640 | bytes 5111812 | tf_op jit(solution)/shard_map/pallas_call | solution.py:38
  5.7 3.1 %collective-permute-start.2 = (bf16[512,128]{1,0:T(8,128)(2,1)S(1)}, bf16[512,128]{1,0:T(8,128)(2,1)S(1)}, u32[]{:S(2)}, u32[]{:S(2)}) collective-permute-start(bf16[512,128]{1,0:T(8,128)(2,1)S(1)} %get-tuple-element.51.a_ref), channel_id=1, source_target_pairs={{0,4},{4,0},{8,12},{12,8},{1,5},{5,1},{9,13},{13,9},{2,6},{6,2},{1... | collective-permute-start | bytes 393224 | tf_op jit(solution)/shard_map/ppermute | solution.py:251
  8.8 0.1 collective-permute-start.1
  8.9 4.3 %collective-permute-done.2.b_ref = bf16[512,128]{1,0:T(8,128)(2,1)S(1)} collective-permute-done((bf16[512,128]{1,0:T(8,128)(2,1)S(1)}, bf16[512,128]{1,0:T(8,128)(2,1)S(1)}, u32[]{:S(2)}, u32[]{:S(2)}) %collective-permute-start.2) | collective-permute-done | bytes 131104 | tf_op jit(solution)/shard_map/ppermute | solution.py:251
  13.2 3.1 %collective-permute-start.3 = (bf16[512,128]{1,0:T(8,128)(2,1)S(1)}, bf16[512,128]{1,0:T(8,128)(2,1)S(1)}, u32[]{:S(2)}, u32[]{:S(2)}) collective-permute-start(bf16[512,128]{1,0:T(8,128)(2,1)S(1)} %shard_map.98), channel_id=1, source_target_pairs={{0,8},{4,12},{8,0},{12,4},{1,9},{5,13},{9,1},{13,5},{2,10},{6,14},... | collective-permute-start | bytes 393224 | tf_op jit(solution)/shard_map/ppermute | solution.py:251
  16.3 2.3 %shard_map.96 = (f32[512,512]{1,0:T(8,128)S(1)}, bf16[512,1024]{1,0:T(8,128)(2,1)S(1)}, f32[512,256]{1,0:T(8,128)S(1)}, bf16[1,512,128]{2,1,0:T(8,128)(2,1)S(1)}) custom-call(bf16[512,512]{1,0:T(8,128)(2,1)S(1)} %get-tuple-element.32.query_ref, bf16[512,512]{1,0:T(8,128)(2,1)S(1)} %get-tuple-element.33.key_ref, ...), custom_call_target="tpu_custom_call" | custom-call | flops 268435456 | bytes 4358144 | tf_op jit(solution)/shard_map/pallas_call | solution.py:38
  18.6 0.0 collective-permute-done.1.refs_0_.refs_2_
  18.6 2.8 %collective-permute-done.3.refs_1_.refs_3_ = bf16[512,128]{1,0:T(8,128)(2,1)S(1)} collective-permute-done((bf16[512,128]{1,0:T(8,128)(2,1)S(1)}, bf16[512,128]{1,0:T(8,128)(2,1)S(1)}, u32[]{:S(2)}, u32[]{:S(2)}) %collective-permute-start.3) | collective-permute-done | bytes 131104 | tf_op jit(solution)/shard_map/ppermute | solution.py:251
  21.4 0.4 %shard_map.99.refs_0_ = bf16[512,512]{1,0:T(8,128)(2,1)S(1)} custom-call(s32[1]{0:T(128)} %bitcast.spot_ref, f32[512,512]{1,0:T(8,128)S(1)} %get-tuple-element.49.mixed_ref, bf16[512,1024]{1,0:T(8,128)(2,1)S(1)} %get-tuple-element.40.weighted_ref, bf16[512,128]{1,0:T(8,128)(2,1)S(1)} %collective-permute-done.1.refs_0_.refs_2_, ...), custom_call_target="tpu_custom_call" | custom-call | flops 134217728 | bytes 2883588 | tf_op jit(solution)/shard_map/pallas_call | solution.py:38
  21.9 0.1 collective-permute-start.4
  21.9 2.5 %shard_map.97 = (f32[512,512]{1,0:T(8,128)S(1)}, f32[512,512]{1,0:T(8,128)S(1)}, f32[512,512]{1,0:T(8,128)S(1)}) custom-call(bf16[512,512]{1,0:T(8,128)(2,1)S(1)} %get-tuple-element.32.query_ref, bf16[512,512]{1,0:T(8,128)(2,1)S(1)} %get-tuple-element.33.key_ref, bf16[512,512]{1,0:T(8,128)(2,1)S(1)} %get-tuple-element.34.value_ref, ...), custom_call_target="tpu_custom_call" | custom-call | flops 536870912 | bytes 6979584 | tf_op jit(solution)/shard_map/pallas_call | solution.py:38
  24.5 1.4 %shard_map.100 = (bf16[512,512]{1,0:T(8,128)(2,1)S(1)}, bf16[512,512]{1,0:T(8,128)(2,1)S(1)}, bf16[512,512]{1,0:T(8,128)(2,1)S(1)}, f32[512,1024]{1,0:T(8,128)S(1)}) custom-call(s32[1]{0:T(128)} %bitcast.spot_ref, f32[512,512]{1,0:T(8,128)S(1)} %get-tuple-element.46.dq_ref, f32[512,512]{1,0:T(8,128)S(1)} %get-tuple-element.47.dk_ref, ...), custom_call_target="tpu_custom_call" | custom-call | flops 805306368 | bytes 10256388 | tf_op jit(solution)/shard_map/pallas_call | solution.py:38
  25.9 0.0 collective-permute-done.5.weight_ref
  25.9 0.0 collective-permute-done.4.mixed_ref
  25.9 1.5 %shard_map.101 = (bf16[512,1024]{1,0:T(8,128)(2,1)}, bf16[512,512]{1,0:T(8,128)(2,1)}, bf16[512,512]{1,0:T(8,128)(2,1)}, bf16[512,512]{1,0:T(8,128)(2,1)}) custom-call(f32[512,1024]{1,0:T(8,128)S(1)} %get-tuple-element.52.part_ref, bf16[512,512]{1,0:T(8,128)(2,1)S(1)} %collective-permute-done.4.mixed_ref, ...), custom_call_target="tpu_custom_call" | custom-call | flops 536870912 | bytes 7864320 | tf_op jit(solution)/shard_map/pallas_call | solution.py:38
  (1 shorter events, 0.0 us)
Async XLA Ops:
  0.6 4.0 %collective-permute-start = (bf16[512,1024]{1,0:T(8,128)(2,1)}, bf16[512,1024]{1,0:T(8,128)(2,1)S(1)}, u32[]{:S(2)}, u32[]{:S(2)}) collective-permute-start(bf16[512,1024]{1,0:T(8,128)(2,1)} %bitcast.13), channel_id=1, source_target_pairs={{0,1},{1,0},{2,3},{3,2},{4,5},{5,4},{6,7},{7,6},{8,9},{9,8},{10,11... | collective-permute-start | bytes 3145736 | tf_op jit(solution)/shard_map/ppermute | solution.py:286
  4.5 21.3 %collective-permute-start.5 = (bf16[512,1024]{1,0:T(8,128)(2,1)S(1)}, bf16[512,1024]{1,0:T(8,128)(2,1)S(1)}, u32[]{:S(2)}, u32[]{:S(2)}) collective-permute-start(bf16[512,1024]{1,0:T(8,128)(2,1)S(1)} %get-tuple-element.38.weight_ref), channel_id=1, source_target_pairs={{0,1},{1,0},{2,3},{3,2},{4,5},{5,4},{6,7},{7,6},{8,9},{9,8},{10,11... | collective-permute-start | bytes 3145736 | tf_op jit(solution)/shard_map/ppermute | solution.py:310
  5.7 7.5 %collective-permute-start.2 = (bf16[512,128]{1,0:T(8,128)(2,1)S(1)}, bf16[512,128]{1,0:T(8,128)(2,1)S(1)}, u32[]{:S(2)}, u32[]{:S(2)}) collective-permute-start(bf16[512,128]{1,0:T(8,128)(2,1)S(1)} %get-tuple-element.51.a_ref), channel_id=1, source_target_pairs={{0,4},{4,0},{8,12},{12,8},{1,5},{5,1},{9,13},{13,9},{2,6},{6,2},{1... | collective-permute-start | bytes 393224 | tf_op jit(solution)/shard_map/ppermute | solution.py:251
  8.8 9.8 %collective-permute-start.1 = (bf16[512,128]{1,0:T(8,128)(2,1)S(1)}, bf16[512,128]{1,0:T(8,128)(2,1)S(1)}, u32[]{:S(2)}, u32[]{:S(2)}) collective-permute-start(bf16[512,128]{1,0:T(8,128)(2,1)S(1)} %get-tuple-element.50), channel_id=1, source_target_pairs={{0,4},{4,0},{8,12},{12,8},{1,5},{5,1},{9,13},{13,9},{2,6},{6,2},{1... | collective-permute-start | bytes 393224 | tf_op jit(solution)/shard_map/ppermute | solution.py:251
  13.2 8.2 %collective-permute-start.3 = (bf16[512,128]{1,0:T(8,128)(2,1)S(1)}, bf16[512,128]{1,0:T(8,128)(2,1)S(1)}, u32[]{:S(2)}, u32[]{:S(2)}) collective-permute-start(bf16[512,128]{1,0:T(8,128)(2,1)S(1)} %shard_map.98), channel_id=1, source_target_pairs={{0,8},{4,12},{8,0},{12,4},{1,9},{5,13},{9,1},{13,5},{2,10},{6,14},... | collective-permute-start | bytes 393224 | tf_op jit(solution)/shard_map/ppermute | solution.py:251
  21.9 4.0 %collective-permute-start.4 = (bf16[512,512]{1,0:T(8,128)(2,1)S(1)}, bf16[512,512]{1,0:T(8,128)(2,1)S(1)}, u32[]{:S(2)}, u32[]{:S(2)}) collective-permute-start(bf16[512,512]{1,0:T(8,128)(2,1)S(1)} %shard_map.99.refs_0_), channel_id=1, source_target_pairs={{0,1},{1,0},{2,3},{3,2},{4,5},{5,4},{6,7},{7,6},{8,9},{9,8},{10,11... | collective-permute-start | bytes 1572872 | tf_op jit(solution)/shard_map/ppermute | solution.py:328

commit v4 on v3

--- a/solution.py
+++ b/solution.py
@@ -32,7 +32,7 @@
     return lax.dot_general(a, b, (((0,), (0,)), ((), ())), preferred_element_type=F32)
 
 
-def call(kernel, outs, in_specs, flops, args, out_specs=None, scratch=(), limit=16):
+def call(kernel, outs, in_specs, flops, args, out_specs=None, scratch=(), limit=16, aliases=None):
     moved = sum(a.size * a.dtype.itemsize for a in args)
     moved += sum(o.size * o.dtype.itemsize for o in outs)
     return pl.pallas_call(
@@ -41,6 +41,7 @@
         in_specs=in_specs,
         out_specs=out_specs or [VMEM] * len(outs),
         scratch_shapes=list(scratch),
+        input_output_aliases=aliases or {},
         compiler_params=pltpu.CompilerParams(vmem_limit_bytes=limit << 20),
         cost_estimate=pl.CostEstimate(flops=flops, bytes_accessed=moved, transcendentals=0),
     )(*args)
@@ -66,34 +67,31 @@
     return copies
 
 
-def state_kernel(place_ref, spot_ref, mask_hbm, key_hbm, value_hbm, grad_hbm, weight_hbm, query_hbm, *refs):
-    state_ref, tier_ref, key, value, grad, weight, query, mask, sems = refs
-    mine = column(weight_hbm, place_ref[0])
-    sources = [key_hbm, value_hbm, mask_hbm, mine, grad_hbm, query_hbm]
-    copies = start_copies(zip(sources, [key, value, mask, weight, grad, query]), sems)
+def prep_kernel(tiers, span, place_ref, spot_ref, mask_hbm, key_hbm, value_hbm, grad_hbm, weight_hbm, query_hbm, *refs):
+    state_ref, tier_ref, key, value, weight, rest, query, part_ref, weighted_ref, mask, grad, sems = refs
+    mine, other = column(weight_hbm, place_ref[0]), column(weight_hbm, 1 - place_ref[0])
+    sources = [mine, grad_hbm, key_hbm, value_hbm, mask_hbm, query_hbm, other]
+    copies = start_copies(zip(sources, [weight, grad, key, value, mask, query, rest]), sems)
     copies[0].wait()
     copies[1].wait()
-    for col in head_slices(key.shape[1]):
+    part_ref[...] = dot_nt(grad[...], weight[...])
+    copies[2].wait()
+    copies[3].wait()
+    cols = head_slices(key.shape[1])
+    for col in cols:
         state_ref[col, :] = dot_tn(key[:, col], value[:, col]).astype(BF16)
-    copies[2].wait()
+    copies[4].wait()
     levels = mask[...].astype(F32)
     rows = [levels[l : l + 1] * jnp.float32(level_scale(l)) for l in range(levels.shape[0])]
-    tier_ref[...] = jnp.transpose(jnp.concatenate(rows, axis=0))
-    for copy in copies[3:]:
-        copy.wait()
-
-
-def own_kernel(tiers, span, place_ref, grad_ref, weight_ref, query_ref, tier_ref, weight_hbm, *refs):
-    part_ref, weighted_ref, other_ref, sems = refs
-    copies = start_copies([(column(weight_hbm, 1 - place_ref[0]), other_ref)], sems)
-    part_ref[...] = dot_nt(grad_ref[...], weight_ref[...])
-    length, width = query_ref.shape
+    tier = jnp.transpose(jnp.concatenate(rows, axis=0))
+    tier_ref[...] = tier
+    copies[5].wait()
     for j in range(span):
-        scale = jnp.broadcast_to(tier_ref[:, tiers + j : tiers + j + 1], (length, HEAD_DIM))
-        for i, col in enumerate(head_slices(width)):
+        scale = jnp.broadcast_to(tier[:, tiers + j : tiers + j + 1], (tier.shape[0], HEAD_DIM))
+        for i, col in enumerate(cols):
             at = (i * span + j) * HEAD_DIM
-            weighted_ref[:, at : at + HEAD_DIM] = (scale * query_ref[:, col].astype(F32)).astype(BF16)
-    copies[0].wait()
+            weighted_ref[:, at : at + HEAD_DIM] = (scale * query[:, col].astype(F32)).astype(BF16)
+    copies[6].wait()
 
 
 def reach_kernel(span, spot_ref, grad_ref, weight_ref, part_ref, weighted_ref, state_ref, *outs):
@@ -202,49 +200,106 @@
     return functools.reduce(jnp.add, kept).astype(BF16)
 
 
-def mixed_kernel(spot_ref, mixed_ref, weighted_ref, *refs):
-    state_refs, out_ref = refs[:-1], refs[-1]
-    step = len(state_refs) * HEAD_DIM
+def far(spot_ref, top):
+    return upper(spot_ref, top) > 0
+
+
+def near_mixed_kernel(span, spot_ref, mixed_ref, weighted_ref, *refs):
+    got_refs, out_ref = refs[:-1], refs[-1]
     for i, col in enumerate(head_slices(mixed_ref.shape[1])):
-        far = dot(weighted_ref[:, i * step : (i + 1) * step], low_states(state_refs, col, spot_ref))
-        out_ref[:, col] = (mixed_ref[:, col] + far).astype(BF16)
-
-
-def query_kernel(tiers, span, spot_ref, dq_ref, dk_ref, dv_ref, key_ref, value_ref, grad_ref, tier_ref, *refs):
-    mixed_ref, weight_ref = refs[:2]
-    got_refs = refs[2:-4]
-    dq_low, dk_low, dv_low, part_ref = refs[-4:]
-    scale = [tier_ref[:, tiers + j : tiers + j + 1] for j in range(span)]
+        total = mixed_ref[:, col]
+        if got_refs:
+            at = i * span * HEAD_DIM
+            weighted = weighted_ref[:, at : at + len(got_refs) * HEAD_DIM]
+            total = total + dot(weighted, low_states(got_refs, col, spot_ref))
+        out_ref[:, col] = total.astype(BF16)
+
+
+def far_mixed_kernel(spot_ref, mixed_ref, weighted_ref, *refs):
+    got_refs, out_ref = refs[:-1], refs[-1]
+    step = len(got_refs) * HEAD_DIM
+
+    @pl.when(far(spot_ref, len(got_refs) - 1))
+    def _():
+        for i, col in enumerate(head_slices(mixed_ref.shape[1])):
+            total = dot(weighted_ref[:, i * step : (i + 1) * step], low_states(got_refs, col, spot_ref))
+            out_ref[:, col] = (mixed_ref[:, col] + total).astype(BF16)
+
+
+def near_own_kernel(tiers, top, spot_ref, dq_ref, grad_ref, tier_ref, mixed_ref, weight_ref, *refs):
+    got_refs, (near_dq_ref, part_ref) = refs[:-2], refs[-2:]
     for col in head_slices(dq_ref.shape[1]):
-        far = dot_nt(grad_ref[:, col], low_states(got_refs, col, spot_ref))
         total = dq_ref[:, col]
-        for j in range(span):
-            total = total + scale[j] * far[:, j * HEAD_DIM : (j + 1) * HEAD_DIM]
-        dq_low[:, col] = total.astype(BF16)
+        if got_refs:
+            rest = dot_nt(grad_ref[:, col], low_states(got_refs, col, spot_ref))
+            for j in range(top):
+                scale = tier_ref[:, tiers + j : tiers + j + 1]
+                total = total + scale * rest[:, j * HEAD_DIM : (j + 1) * HEAD_DIM]
+        near_dq_ref[:, col] = total
+
+    @pl.when(jnp.logical_not(far(spot_ref, top)))
+    def _():
+        part_ref[...] = dot(mixed_ref[...], weight_ref[...])
+
+
+def near_layer_kernel(top, spot_ref, part_ref, mixed_ref, weight_ref, out_ref):
+    @pl.when(jnp.logical_not(far(spot_ref, top)))
+    def _():
+        out_ref[...] = (part_ref[...] + dot(mixed_ref[...], weight_ref[...])).astype(BF16)
+
+
+def finish_kernel(tiers, spot_ref, dk_ref, dv_ref, key_ref, value_ref, near_dq_ref, grad_ref, tier_ref, *refs):
+    mixed_ref, weight_ref, layer_ref = refs[:3]
+    got_refs = refs[3:-10]
+    out_hbm, dq_hbm, dk_hbm, dv_hbm, part_ref, dq_low, dk_low, dv_low, near_low, sems = refs[-10:]
+    top = len(got_refs) - 1
+    cols = head_slices(key_ref.shape[1])
+    near = jnp.logical_not(far(spot_ref, top))
+    early = [pltpu.make_async_copy(layer_ref, out_hbm, sems.at[0]), pltpu.make_async_copy(near_low, dq_hbm, sems.at[1])]
+    late = [pltpu.make_async_copy(dk_low, dk_hbm, sems.at[2]), pltpu.make_async_copy(dv_low, dv_hbm, sems.at[3])]
+
+    @pl.when(near)
+    def _():
+        early[0].start()
+        near_low[...] = near_dq_ref[...].astype(BF16)
+        early[1].start()
+
+    for col in cols:
         back = low_back(got_refs, col, spot_ref)
         dk_low[:, col] = (dk_ref[:, col] + dot(value_ref[:, col], back)).astype(BF16)
         dv_low[:, col] = (dv_ref[:, col] + dot_nt(key_ref[:, col], back)).astype(BF16)
-    part_ref[...] = dot(mixed_ref[...], weight_ref[...])
-
-
-def last_kernel(part_ref, mixed_ref, weight_ref, dq_low, dk_low, dv_low, out_hbm, dq_hbm, dk_hbm, dv_hbm, out_low, sems):
-    chunks = sems.shape[0] - 3
-    rows = part_ref.shape[0] // chunks
-    copies = []
-
-    def send(src, dst):
-        copies.append(pltpu.make_async_copy(src, dst, sems.at[len(copies)]))
-        copies[-1].start()
-
-    send(dq_low, dq_hbm)
-    send(dk_low, dk_hbm)
-    send(dv_low, dv_hbm)
-    for n in range(chunks):
-        at = pl.ds(n * rows, rows)
-        out_low[at, :] = (part_ref[at, :] + dot(mixed_ref[at, :], weight_ref[...])).astype(BF16)
-        send(out_low.at[at, :], out_hbm.at[at, :])
-    for copy in copies:
-        copy.wait()
+
+    @pl.when(near)
+    def _():
+        for copy in late:
+            copy.start()
+        for copy in early + late:
+            copy.wait()
+
+    @pl.when(far(spot_ref, top))
+    def _():
+        part_ref[...] = dot(mixed_ref[...], weight_ref[...])
+        scale = tier_ref[:, tiers + top : tiers + top + 1]
+        for col in cols:
+            rest = dot_nt(grad_ref[:, col], got_refs[top][col, :])
+            dq_low[:, col] = (near_dq_ref[:, col] + scale * rest).astype(BF16)
+
+
+def far_layer_kernel(top, spot_ref, part_ref, mixed_ref, weight_ref, dq_ref, dk_ref, dv_ref, *refs):
+    outs, (out_low, sems) = refs[4:8], refs[8:]
+
+    @pl.when(far(spot_ref, top))
+    def _():
+        copies = start_copies(zip([dq_ref, dk_ref, dv_ref], outs[1:]), sems)
+        chunks = sems.shape[0] - len(copies)
+        rows = part_ref.shape[0] // chunks
+        for n in range(chunks):
+            at = pl.ds(n * rows, rows)
+            out_low[at, :] = (part_ref[at, :] + dot(mixed_ref[at, :], weight_ref[...])).astype(BF16)
+            copies.append(pltpu.make_async_copy(out_low.at[at, :], outs[0].at[at, :], sems.at[len(copies)]))
+            copies[-1].start()
+        for copy in copies:
+            copy.wait()
 
 
 def swap_blocks(x, level):
@@ -284,21 +339,15 @@
     project = 2 * length * width * half
 
     grad_other = lax.ppermute(grad, "head", swap)
-    state, tier, key, value, grad_own, weight_own, query = call(
-        state_kernel,
-        [matrix, shape((length, mask.shape[1]), F32), low, low, wide, shape((width, half), BF16), low],
+    state, tier, key, value, weight_own, weight_rest, query, part, weighted = call(
+        functools.partial(prep_kernel, tiers, span),
+        [matrix, shape((length, mask.shape[1]), F32), low, low]
+        + [shape((width, half), BF16)] * 2
+        + [low, high, shape((length, span * width), BF16)],
         [SMEM] * 2 + [HBM] * 6,
-        unit,
+        project + unit,
         (place, spot, *hbm(mask.T, key, value, grad, out_weight, query)),
-        scratch=[pltpu.VMEM(mask.shape[::-1], mask.dtype), dma((6,))],
-    )
-    part, weighted, weight_rest = call(
-        functools.partial(own_kernel, tiers, span),
-        [high, shape((length, span * width), BF16), shape((width, half), BF16)],
-        [SMEM] + [VMEM] * 4 + [HBM],
-        project,
-        (place, grad_own, weight_own, query, tier, *hbm(out_weight)),
-        scratch=[dma((1,))],
+        scratch=[pltpu.VMEM(mask.shape[::-1], mask.dtype), pltpu.VMEM((length, half), BF16), dma((7,))],
     )
     grad_mixed, *sends = call(
         functools.partial(reach_kernel, span),
@@ -324,23 +373,49 @@
     dq, dk, dv = call(
         backward_kernel, [high] * 3, [VMEM] * 8, 8 * unit, (query, key, value, grad_mixed, tier, probs, blend, inner)
     )
-    (mixed,) = call(mixed_kernel, [low], [SMEM] + [VMEM] * (2 + span), span * unit, (spot, mixed, weighted, *got))
+    top = span - 1
+    (near_mixed,) = call(
+        functools.partial(near_mixed_kernel, span),
+        [low],
+        [SMEM] + [VMEM] * (2 + top),
+        top * unit,
+        (spot, mixed, weighted, *got[:top]),
+    )
+    near_other = lax.ppermute(near_mixed, "head", swap)
+    near_dq, part = call(
+        functools.partial(near_own_kernel, tiers, top),
+        [high, shape((length, half), F32)],
+        [SMEM] + [VMEM] * (5 + top),
+        project + top * unit,
+        (spot, dq, grad_mixed, tier, near_mixed, weight_own, *got[:top]),
+    )
+    (near_layer,) = call(
+        functools.partial(near_layer_kernel, top),
+        [wide],
+        [SMEM] + [VMEM] * 3,
+        project,
+        (spot, part, near_other, weight_other),
+    )
+    (mixed,) = call(far_mixed_kernel, [low], [SMEM] + [VMEM] * (2 + span), span * unit, (spot, mixed, weighted, *got))
     mixed_other = lax.ppermute(mixed, "head", swap)
-    *lows, part = call(
-        functools.partial(query_kernel, tiers, span),
-        [low] * 3 + [shape((length, half), F32)],
-        [SMEM] + [VMEM] * (9 + span),
-        project + (2 + span) * unit,
-        (spot, dq, dk, dv, key, value, grad_mixed, tier, mixed, weight_own, *got),
+    *outs, part, dq_low, dk_low, dv_low = call(
+        functools.partial(finish_kernel, tiers),
+        [wide, low, low, low, shape((length, half), F32), low, low, low],
+        [SMEM] + [VMEM] * (10 + span),
+        project + 3 * unit,
+        (spot, dk, dv, key, value, near_dq, grad_mixed, tier, mixed, weight_own, near_layer, *got),
+        out_specs=[HBM] * 4 + [VMEM] * 4,
+        scratch=[low_buffer, dma((4,))],
     )
     layer_out, grad_query, grad_key, grad_value = call(
-        last_kernel,
+        functools.partial(far_layer_kernel, top),
         [wide, low, low, low],
-        [VMEM] * 6,
+        [SMEM] + [VMEM] * 6 + [HBM] * 4,
         project,
-        (part, mixed_other, weight_other, *lows),
+        (spot, part, mixed_other, weight_other, dq_low, dk_low, dv_low, *outs),
         out_specs=[HBM] * 4,
         scratch=[pltpu.VMEM((length, half), BF16), dma((7,))],
+        aliases={7 + n: n for n in range(4)},
     )
     return tuple(x[None] for x in (layer_out, grad_query, grad_key, grad_value))
 

time: 27.6 us -> 27.4 us (level)
  waiting for transfers between devices: 7.09 us -> 6.71 us
    ppermute x3, waiting for transfers between devices: 7.08 us -> 6.7 us  [swap_blocks(): lax.ppermute(x, 'seq', [(n, n ^ 1 << level) for n in range(lax.axis_size(...]
    pallas_call x9 -> x11, Pallas kernels: 12.6 us -> 12.8 us  [call(): pl.pallas_call(kernel, out_shape=outs, in_specs=in_specs, out_specs=out_s...]
  transfers between devices with their start and end apart: 6 -> 7, of which waited for: 2 -> 2; matrix products, arithmetic and copies ran while one was open for 0% -> 0% of each run, Pallas kernels for 40% -> 47%
where the time goes in v4:
time: 27.4 us; the launch traced here: 27.2 us
  Pallas kernels  12.8 us (47%)
  starting transfers between devices  7.01 us (26%)
  waiting for transfers between devices  6.71 us (24%)
  between operations  0.74 us (3%)
    pallas_call x11, Pallas kernels, call(): pl.pallas_call(kernel, out_shape=outs, in_specs=in_specs, out_specs=out_s...  12.8 us
    ppermute x3, waiting for transfers between devices, swap_blocks(): lax.ppermute(x, 'seq', [(n, n ^ 1 << level) for n in range(lax.axis_size(...  6.7 us
    ppermute x3, starting transfers between devices, swap_blocks(): lax.ppermute(x, 'seq', [(n, n ^ 1 << level) for n in range(lax.axis_size(...  6.29 us
    ppermute x1, starting transfers between devices, on_device(): grad_other = lax.ppermute(grad, 'head', swap)  0.56 us
  transfers between devices with their start and end apart: 7, of which 2 were waited for; matrix products, arithmetic and copies ran while one was open for 0% of the time, Pallas kernels for 47%

profile of v4, /device:TPU:0, one launch (start us, length us, event | category | flops | bytes accessed | tf_op | source)
XLA Modules:
  0.0 27.2 jit_solution(3350469712457543736)
XLA Ops:
  0.6 0.6 %collective-permute-start = (bf16[512,1024]{1,0:T(8,128)(2,1)}, bf16[512,1024]{1,0:T(8,128)(2,1)S(1)}, u32[]{:S(2)}, u32[]{:S(2)}) collective-permute-start(bf16[512,1024]{1,0:T(8,128)(2,1)} %bitcast.14), channel_id=1, source_target_pairs={{0,1},{1,0},{2,3},{3,2},{4,5},{5,4},{6,7},{7,6},{8,9},{9,8},{10,11... | collective-permute-start | bytes 3145736 | tf_op jit(solution)/shard_map/ppermute | solution.py:341
  1.2 3.1 %shard_map.93 = (bf16[512,128]{1,0:T(8,128)(2,1)S(1)}, f32[512,16]{1,0:T(8,128)S(1)}, bf16[512,512]{1,0:T(8,128)(2,1)S(1)}, bf16[512,512]{1,0:T(8,128)(2,1)S(1)}...) custom-call(s32[1]{0:T(128)} %bitcast.1.place_ref, ...), custom_call_target="tpu_custom_call" | custom-call | flops 603979776 | bytes 10682376 | tf_op jit(solution)/shard_map/pallas_call | solution.py:38
  4.3 0.1 collective-permute-start.5
  4.4 0.0 collective-permute-done.grad_ref
  4.4 1.1 %shard_map.94 = (bf16[512,512]{1,0:T(8,128)(2,1)S(1)}, bf16[512,128]{1,0:T(8,128)(2,1)S(1)}, bf16[512,128]{1,0:T(8,128)(2,1)S(1)}) custom-call(s32[1]{0:T(128)} %bitcast.spot_ref, bf16[512,1024]{1,0:T(8,128)(2,1)S(1)} %collective-permute-done.grad_ref, bf16[512,1024]{1,0:T(8,128)(2,1)S(1)} %get-tuple-element.40.weight_ref, ...), custom_call_target="tpu_custom_call" | custom-call | flops 671088640 | bytes 5111812 | tf_op jit(solution)/shard_map/pallas_call | solution.py:38
  5.5 3.1 %collective-permute-start.2 = (bf16[512,128]{1,0:T(8,128)(2,1)S(1)}, bf16[512,128]{1,0:T(8,128)(2,1)S(1)}, u32[]{:S(2)}, u32[]{:S(2)}) collective-permute-start(bf16[512,128]{1,0:T(8,128)(2,1)S(1)} %get-tuple-element.56.a_ref), channel_id=1, source_target_pairs={{0,4},{4,0},{8,12},{12,8},{1,5},{5,1},{9,13},{13,9},{2,6},{6,2},{1... | collective-permute-start | bytes 393224 | tf_op jit(solution)/shard_map/ppermute | solution.py:306
  8.6 0.1 collective-permute-start.1
  8.7 4.3 %collective-permute-done.2.b_ref = bf16[512,128]{1,0:T(8,128)(2,1)S(1)} collective-permute-done((bf16[512,128]{1,0:T(8,128)(2,1)S(1)}, bf16[512,128]{1,0:T(8,128)(2,1)S(1)}, u32[]{:S(2)}, u32[]{:S(2)}) %collective-permute-start.2) | collective-permute-done | bytes 131104 | tf_op jit(solution)/shard_map/ppermute | solution.py:306
  13.0 3.1 %collective-permute-start.3 = (bf16[512,128]{1,0:T(8,128)(2,1)S(1)}, bf16[512,128]{1,0:T(8,128)(2,1)S(1)}, u32[]{:S(2)}, u32[]{:S(2)}) collective-permute-start(bf16[512,128]{1,0:T(8,128)(2,1)S(1)} %shard_map.99), channel_id=1, source_target_pairs={{0,8},{4,12},{8,0},{12,4},{1,9},{5,13},{9,1},{13,5},{2,10},{6,14},... | collective-permute-start | bytes 393224 | tf_op jit(solution)/shard_map/ppermute | solution.py:306
  16.1 2.3 %shard_map.95 = (f32[512,512]{1,0:T(8,128)S(1)}, bf16[512,1024]{1,0:T(8,128)(2,1)S(1)}, f32[512,256]{1,0:T(8,128)S(1)}, bf16[1,512,128]{2,1,0:T(8,128)(2,1)S(1)}) custom-call(bf16[512,512]{1,0:T(8,128)(2,1)S(1)} %get-tuple-element.37.query_ref, bf16[512,512]{1,0:T(8,128)(2,1)S(1)} %get-tuple-element.38.key_ref, ...), custom_call_target="tpu_custom_call" | custom-call | flops 268435456 | bytes 4358144 | tf_op jit(solution)/shard_map/pallas_call | solution.py:38
  18.4 0.0 collective-permute-done.1.refs_0_.refs_3_
  18.4 0.3 %shard_map.97.mixed_ref = bf16[512,512]{1,0:T(8,128)(2,1)S(1)} custom-call(s32[1]{0:T(128)} %bitcast.spot_ref, f32[512,512]{1,0:T(8,128)S(1)} %get-tuple-element.52.mixed_ref, bf16[512,1024]{1,0:T(8,128)(2,1)S(1)} %get-tuple-element.42.weighted_ref, bf16[512,128]{1,0:T(8,128)(2,1)S(1)} %collective-permute-done.1.refs_0_.refs_3_), custom_call_target="tpu_custom_call" | custom-call | flops 67108864 | bytes 2752516 | tf_op jit(solution)/shard_map/pallas_call | solution.py:38
  18.7 0.1 collective-permute-start.4
  18.8 2.4 %collective-permute-done.3.refs_1_.refs_4_ = bf16[512,128]{1,0:T(8,128)(2,1)S(1)} collective-permute-done((bf16[512,128]{1,0:T(8,128)(2,1)S(1)}, bf16[512,128]{1,0:T(8,128)(2,1)S(1)}, u32[]{:S(2)}, u32[]{:S(2)}) %collective-permute-start.3) | collective-permute-done | bytes 131104 | tf_op jit(solution)/shard_map/ppermute | solution.py:306
  21.2 0.0 collective-permute-start.6
  21.2 2.5 %shard_map.96 = (f32[512,512]{1,0:T(8,128)S(1)}, f32[512,512]{1,0:T(8,128)S(1)}, f32[512,512]{1,0:T(8,128)S(1)}) custom-call(bf16[512,512]{1,0:T(8,128)(2,1)S(1)} %get-tuple-element.37.query_ref, bf16[512,512]{1,0:T(8,128)(2,1)S(1)} %get-tuple-element.38.key_ref, bf16[512,512]{1,0:T(8,128)(2,1)S(1)} %get-tuple-element.39.value_ref, ...), custom_call_target="tpu_custom_call" | custom-call | flops 536870912 | bytes 6979584 | tf_op jit(solution)/shard_map/pallas_call | solution.py:38
  23.7 1.1 %shard_map.98 = (f32[512,512]{1,0:T(8,128)S(1)}, f32[512,1024]{1,0:T(8,128)S(1)}) custom-call(s32[1]{0:T(128)} %bitcast.spot_ref, f32[512,512]{1,0:T(8,128)S(1)} %get-tuple-element.51.dq_ref, bf16[512,512]{1,0:T(8,128)(2,1)S(1)} %get-tuple-element.44.grad_ref, f32[512,16]{1,0:T(8,128)S(1)} %get-tuple-element.45.tier_ref, ...), custom_call_target="tpu_custom_call" | custom-call | flops 603979776 | bytes 6455300 | tf_op jit(solution)/shard_map/pallas_call | solution.py:38
  24.8 0.0 collective-permute-done.5.weight_ref
  24.8 0.0 collective-permute-done.4.mixed_ref
  24.9 0.7 %shard_map.101.refs_2_ = bf16[512,1024]{1,0:T(8,128)(2,1)S(1)} custom-call(s32[1]{0:T(128)} %bitcast.spot_ref, f32[512,1024]{1,0:T(8,128)S(1)} %get-tuple-element.57.part_ref, bf16[512,512]{1,0:T(8,128)(2,1)S(1)} %collective-permute-done.4.mixed_ref, bf16[512,1024]{1,0:T(8,128)(2,1)S(1)} %collective-permute-done.5.weight_ref), custom_call_target="tpu_custom_call" | custom-call | flops 536870912 | bytes 4718596 | tf_op jit(solution)/shard_map/pallas_call | solution.py:38
  25.6 1.5 %shard_map.102 = (bf16[512,1024]{1,0:T(8,128)(2,1)}, bf16[512,512]{1,0:T(8,128)(2,1)}, bf16[512,512]{1,0:T(8,128)(2,1)}, bf16[512,512]{1,0:T(8,128)(2,1)}, f32[5...) custom-call(s32[1]{0:T(128)} %bitcast.spot_ref, ...), custom_call_target="tpu_custom_call" | custom-call | flops 738197504 | bytes 13926404 | tf_op jit(solution)/shard_map/pallas_call | solution.py:38
  27.1 0.0 collective-permute-done.6.mixed_ref
  27.1 0.1 shard_map.103
  (2 shorter events, 0.0 us)
Async XLA Ops:
  0.6 3.8 %collective-permute-start = (bf16[512,1024]{1,0:T(8,128)(2,1)}, bf16[512,1024]{1,0:T(8,128)(2,1)S(1)}, u32[]{:S(2)}, u32[]{:S(2)}) collective-permute-start(bf16[512,1024]{1,0:T(8,128)(2,1)} %bitcast.14), channel_id=1, source_target_pairs={{0,1},{1,0},{2,3},{3,2},{4,5},{5,4},{6,7},{7,6},{8,9},{9,8},{10,11... | collective-permute-start | bytes 3145736 | tf_op jit(solution)/shard_map/ppermute | solution.py:341
  4.3 20.5 %collective-permute-start.5 = (bf16[512,1024]{1,0:T(8,128)(2,1)S(1)}, bf16[512,1024]{1,0:T(8,128)(2,1)S(1)}, u32[]{:S(2)}, u32[]{:S(2)}) collective-permute-start(bf16[512,1024]{1,0:T(8,128)(2,1)S(1)} %get-tuple-element.40.weight_ref), channel_id=1, source_target_pairs={{0,1},{1,0},{2,3},{3,2},{4,5},{5,4},{6,7},{7,6},{8,9},{9,8},{10,11... | collective-permute-start | bytes 3145736 | tf_op jit(solution)/shard_map/ppermute | solution.py:359
  5.5 7.5 %collective-permute-start.2 = (bf16[512,128]{1,0:T(8,128)(2,1)S(1)}, bf16[512,128]{1,0:T(8,128)(2,1)S(1)}, u32[]{:S(2)}, u32[]{:S(2)}) collective-permute-start(bf16[512,128]{1,0:T(8,128)(2,1)S(1)} %get-tuple-element.56.a_ref), channel_id=1, source_target_pairs={{0,4},{4,0},{8,12},{12,8},{1,5},{5,1},{9,13},{13,9},{2,6},{6,2},{1... | collective-permute-start | bytes 393224 | tf_op jit(solution)/shard_map/ppermute | solution.py:306
  8.6 9.8 %collective-permute-start.1 = (bf16[512,128]{1,0:T(8,128)(2,1)S(1)}, bf16[512,128]{1,0:T(8,128)(2,1)S(1)}, u32[]{:S(2)}, u32[]{:S(2)}) collective-permute-start(bf16[512,128]{1,0:T(8,128)(2,1)S(1)} %get-tuple-element.53), channel_id=1, source_target_pairs={{0,4},{4,0},{8,12},{12,8},{1,5},{5,1},{9,13},{13,9},{2,6},{6,2},{1... | collective-permute-start | bytes 393224 | tf_op jit(solution)/shard_map/ppermute | solution.py:306
  13.0 8.2 %collective-permute-start.3 = (bf16[512,128]{1,0:T(8,128)(2,1)S(1)}, bf16[512,128]{1,0:T(8,128)(2,1)S(1)}, u32[]{:S(2)}, u32[]{:S(2)}) collective-permute-start(bf16[512,128]{1,0:T(8,128)(2,1)S(1)} %shard_map.99), channel_id=1, source_target_pairs={{0,8},{4,12},{8,0},{12,4},{1,9},{5,13},{9,1},{13,5},{2,10},{6,14},... | collective-permute-start | bytes 393224 | tf_op jit(solution)/shard_map/ppermute | solution.py:306
  18.7 6.2 %collective-permute-start.4 = (bf16[512,512]{1,0:T(8,128)(2,1)S(1)}, bf16[512,512]{1,0:T(8,128)(2,1)S(1)}, u32[]{:S(2)}, u32[]{:S(2)}) collective-permute-start(bf16[512,512]{1,0:T(8,128)(2,1)S(1)} %shard_map.97.mixed_ref), channel_id=1, source_target_pairs={{0,1},{1,0},{2,3},{3,2},{4,5},{5,4},{6,7},{7,6},{8,9},{9,8},{10,11... | collective-permute-start | bytes 1572872 | tf_op jit(solution)/shard_map/ppermute | solution.py:384
  21.2 5.9 %collective-permute-start.6 = (bf16[512,512]{1,0:T(8,128)(2,1)S(1)}, bf16[512,512]{1,0:T(8,128)(2,1)S(1)}, u32[]{:S(2)}, u32[]{:S(2)}) collective-permute-start(bf16[512,512]{1,0:T(8,128)(2,1)S(1)} %shard_map.100.refs_0_), channel_id=1, source_target_pairs={{0,1},{1,0},{2,3},{3,2},{4,5},{5,4},{6,7},{7,6},{8,9},{9,8},{10,11... | collective-permute-start | bytes 1572872 | tf_op jit(solution)/shard_map/ppermute | solution.py:400

commit v5 on v4

--- a/solution.py
+++ b/solution.py
@@ -204,7 +204,7 @@
     return upper(spot_ref, top) > 0
 
 
-def near_mixed_kernel(span, spot_ref, mixed_ref, weighted_ref, *refs):
+def base_kernel(span, spot_ref, mixed_ref, weighted_ref, *refs):
     got_refs, out_ref = refs[:-1], refs[-1]
     for i, col in enumerate(head_slices(mixed_ref.shape[1])):
         total = mixed_ref[:, col]
@@ -212,91 +212,104 @@
             at = i * span * HEAD_DIM
             weighted = weighted_ref[:, at : at + len(got_refs) * HEAD_DIM]
             total = total + dot(weighted, low_states(got_refs, col, spot_ref))
-        out_ref[:, col] = total.astype(BF16)
-
-
-def far_mixed_kernel(spot_ref, mixed_ref, weighted_ref, *refs):
-    got_refs, out_ref = refs[:-1], refs[-1]
-    step = len(got_refs) * HEAD_DIM
-
-    @pl.when(far(spot_ref, len(got_refs) - 1))
-    def _():
-        for i, col in enumerate(head_slices(mixed_ref.shape[1])):
-            total = dot(weighted_ref[:, i * step : (i + 1) * step], low_states(got_refs, col, spot_ref))
-            out_ref[:, col] = (mixed_ref[:, col] + total).astype(BF16)
-
-
-def near_own_kernel(tiers, top, spot_ref, dq_ref, grad_ref, tier_ref, mixed_ref, weight_ref, *refs):
-    got_refs, (near_dq_ref, part_ref) = refs[:-2], refs[-2:]
-    for col in head_slices(dq_ref.shape[1]):
+        out_ref[:, col] = total
+
+
+def early_kernel(tiers, top, spot_ref, dq_ref, dk_ref, dv_ref, key_ref, value_ref, grad_ref, tier_ref, *refs):
+    base_ref, weight_ref = refs[:2]
+    got_refs, (dq_out, part_ref, dk_low, dv_low) = refs[2:-4], refs[-4:]
+    cols = head_slices(dq_ref.shape[1])
+    for col in cols:
         total = dq_ref[:, col]
         if got_refs:
             rest = dot_nt(grad_ref[:, col], low_states(got_refs, col, spot_ref))
             for j in range(top):
                 scale = tier_ref[:, tiers + j : tiers + j + 1]
                 total = total + scale * rest[:, j * HEAD_DIM : (j + 1) * HEAD_DIM]
-        near_dq_ref[:, col] = total
+        dq_out[:, col] = total
 
     @pl.when(jnp.logical_not(far(spot_ref, top)))
     def _():
-        part_ref[...] = dot(mixed_ref[...], weight_ref[...])
-
-
-def near_layer_kernel(top, spot_ref, part_ref, mixed_ref, weight_ref, out_ref):
+        part_ref[...] = dot(base_ref[...].astype(BF16), weight_ref[...])
+
+    @pl.when(far(spot_ref, top))
+    def _():
+        for col in cols:
+            dk, dv = dk_ref[:, col], dv_ref[:, col]
+            if got_refs:
+                back = low_back(got_refs, col, spot_ref)
+                dk = dk + dot(value_ref[:, col], back)
+                dv = dv + dot_nt(key_ref[:, col], back)
+            dk_low[:, col] = dk.astype(BF16)
+            dv_low[:, col] = dv.astype(BF16)
+
+
+def near_layer_kernel(top, spot_ref, part_ref, base_ref, weight_ref, dq_ref, out_ref, dq_low):
     @pl.when(jnp.logical_not(far(spot_ref, top)))
     def _():
-        out_ref[...] = (part_ref[...] + dot(mixed_ref[...], weight_ref[...])).astype(BF16)
-
-
-def finish_kernel(tiers, spot_ref, dk_ref, dv_ref, key_ref, value_ref, near_dq_ref, grad_ref, tier_ref, *refs):
-    mixed_ref, weight_ref, layer_ref = refs[:3]
-    got_refs = refs[3:-10]
-    out_hbm, dq_hbm, dk_hbm, dv_hbm, part_ref, dq_low, dk_low, dv_low, near_low, sems = refs[-10:]
-    top = len(got_refs) - 1
+        out_ref[...] = (part_ref[...] + dot(base_ref[...].astype(BF16), weight_ref[...])).astype(BF16)
+        dq_low[...] = dq_ref[...].astype(BF16)
+
+
+def top_columns(weighted_ref, i, span):
+    at = (i * span + span - 1) * HEAD_DIM
+    return weighted_ref[:, at : at + HEAD_DIM]
+
+
+def finish_kernel(tiers, spot_ref, dk_ref, dv_ref, key_ref, value_ref, dq_ref, grad_ref, tier_ref, *refs):
+    base_ref, weighted_ref, weight_ref, near_layer, near_dq, far_dk, far_dv = refs[:7]
+    got_refs = refs[7:-9]
+    out_hbm, dq_hbm, dk_hbm, dv_hbm, part_ref, dq_low, dk_low, dv_low, sems = refs[-9:]
+    span = len(got_refs)
+    top = span - 1
     cols = head_slices(key_ref.shape[1])
-    near = jnp.logical_not(far(spot_ref, top))
-    early = [pltpu.make_async_copy(layer_ref, out_hbm, sems.at[0]), pltpu.make_async_copy(near_low, dq_hbm, sems.at[1])]
-    late = [pltpu.make_async_copy(dk_low, dk_hbm, sems.at[2]), pltpu.make_async_copy(dv_low, dv_hbm, sems.at[3])]
-
-    @pl.when(near)
-    def _():
-        early[0].start()
-        near_low[...] = near_dq_ref[...].astype(BF16)
-        early[1].start()
-
-    for col in cols:
-        back = low_back(got_refs, col, spot_ref)
-        dk_low[:, col] = (dk_ref[:, col] + dot(value_ref[:, col], back)).astype(BF16)
-        dv_low[:, col] = (dv_ref[:, col] + dot_nt(key_ref[:, col], back)).astype(BF16)
-
-    @pl.when(near)
-    def _():
-        for copy in late:
-            copy.start()
-        for copy in early + late:
+
+    @pl.when(jnp.logical_not(far(spot_ref, top)))
+    def _():
+        copies = start_copies([(near_layer, out_hbm), (near_dq, dq_hbm)], sems)
+        backs = [low_back(got_refs, col, spot_ref) for col in cols]
+        for col, back in zip(cols, backs):
+            dk_low[:, col] = (dk_ref[:, col] + dot(value_ref[:, col], back)).astype(BF16)
+        copies.append(pltpu.make_async_copy(dk_low, dk_hbm, sems.at[2]))
+        copies[-1].start()
+        for col, back in zip(cols, backs):
+            dv_low[:, col] = (dv_ref[:, col] + dot_nt(key_ref[:, col], back)).astype(BF16)
+        copies.append(pltpu.make_async_copy(dv_low, dv_hbm, sems.at[3]))
+        copies[-1].start()
+        for copy in copies:
             copy.wait()
 
     @pl.when(far(spot_ref, top))
     def _():
-        part_ref[...] = dot(mixed_ref[...], weight_ref[...])
+        copies = start_copies([(far_dk, dk_hbm), (far_dv, dv_hbm)], sems)
+        mixed = []
+        for i, col in enumerate(cols):
+            total = base_ref[:, col] + dot(top_columns(weighted_ref, i, span), got_refs[top][col, :])
+            mixed.append(total.astype(BF16))
+        part_ref[...] = dot(jnp.concatenate(mixed, axis=1), weight_ref[...])
         scale = tier_ref[:, tiers + top : tiers + top + 1]
         for col in cols:
             rest = dot_nt(grad_ref[:, col], got_refs[top][col, :])
-            dq_low[:, col] = (near_dq_ref[:, col] + scale * rest).astype(BF16)
-
-
-def far_layer_kernel(top, spot_ref, part_ref, mixed_ref, weight_ref, dq_ref, dk_ref, dv_ref, *refs):
-    outs, (out_low, sems) = refs[4:8], refs[8:]
-
-    @pl.when(far(spot_ref, top))
-    def _():
-        copies = start_copies(zip([dq_ref, dk_ref, dv_ref], outs[1:]), sems)
-        chunks = sems.shape[0] - len(copies)
+            dq_low[:, col] = (dq_ref[:, col] + scale * rest).astype(BF16)
+        for copy in copies:
+            copy.wait()
+
+
+def far_layer_kernel(span, spot_ref, part_ref, base_ref, weighted_ref, got_ref, weight_ref, dq_ref, *refs):
+    out_hbm, dq_hbm, mixed_low, out_low, sems = refs[2:]
+
+    @pl.when(far(spot_ref, span - 1))
+    def _():
+        copies = start_copies([(dq_ref, dq_hbm)], sems)
+        for i, col in enumerate(head_slices(base_ref.shape[1])):
+            total = base_ref[:, col] + dot(top_columns(weighted_ref, i, span), got_ref[col, :])
+            mixed_low[:, col] = total.astype(BF16)
+        chunks = sems.shape[0] - 1
         rows = part_ref.shape[0] // chunks
         for n in range(chunks):
             at = pl.ds(n * rows, rows)
-            out_low[at, :] = (part_ref[at, :] + dot(mixed_ref[at, :], weight_ref[...])).astype(BF16)
-            copies.append(pltpu.make_async_copy(out_low.at[at, :], outs[0].at[at, :], sems.at[len(copies)]))
+            out_low[at, :] = (part_ref[at, :] + dot(mixed_low[at, :], weight_ref[...])).astype(BF16)
+            copies.append(pltpu.make_async_copy(out_low.at[at, :], out_hbm.at[at, :], sems.at[len(copies)]))
             copies[-1].start()
         for copy in copies:
             copy.wait()
@@ -357,6 +370,7 @@
         (spot, grad_other, weight_rest, part, weighted, state),
     )
     weight_other = lax.ppermute(weight_rest, "head", swap)
+    weighted_other = lax.ppermute(weighted, "head", swap)
     mixed, probs, blend, inner = call(
         forward_kernel,
         [high, shape((length, width // HEAD_DIM * tile), BF16), shape((length, tile), F32)]
@@ -374,48 +388,48 @@
         backward_kernel, [high] * 3, [VMEM] * 8, 8 * unit, (query, key, value, grad_mixed, tier, probs, blend, inner)
     )
     top = span - 1
-    (near_mixed,) = call(
-        functools.partial(near_mixed_kernel, span),
-        [low],
+    (base,) = call(
+        functools.partial(base_kernel, span),
+        [high],
         [SMEM] + [VMEM] * (2 + top),
         top * unit,
         (spot, mixed, weighted, *got[:top]),
     )
-    near_other = lax.ppermute(near_mixed, "head", swap)
-    near_dq, part = call(
-        functools.partial(near_own_kernel, tiers, top),
-        [high, shape((length, half), F32)],
-        [SMEM] + [VMEM] * (5 + top),
+    base_other = lax.ppermute(base, "head", swap)
+    near_dq, part, far_dk, far_dv = call(
+        functools.partial(early_kernel, tiers, top),
+        [high, shape((length, half), F32), low, low],
+        [SMEM] + [VMEM] * (9 + top),
         project + top * unit,
-        (spot, dq, grad_mixed, tier, near_mixed, weight_own, *got[:top]),
-    )
-    (near_layer,) = call(
+        (spot, dq, dk, dv, key, value, grad_mixed, tier, base, weight_own, *got[:top]),
+    )
+    near_layer, near_query = call(
         functools.partial(near_layer_kernel, top),
-        [wide],
-        [SMEM] + [VMEM] * 3,
+        [wide, low],
+        [SMEM] + [VMEM] * 4,
         project,
-        (spot, part, near_other, weight_other),
-    )
-    (mixed,) = call(far_mixed_kernel, [low], [SMEM] + [VMEM] * (2 + span), span * unit, (spot, mixed, weighted, *got))
-    mixed_other = lax.ppermute(mixed, "head", swap)
-    *outs, part, dq_low, dk_low, dv_low = call(
+        (spot, part, base_other, weight_other, near_dq),
+    )
+    top_other = lax.ppermute(got[top], "head", swap)
+    layer_out, grad_query, grad_key, grad_value, part, dq_low = call(
         functools.partial(finish_kernel, tiers),
-        [wide, low, low, low, shape((length, half), F32), low, low, low],
-        [SMEM] + [VMEM] * (10 + span),
+        [wide, low, low, low, shape((length, half), F32), low],
+        [SMEM] + [VMEM] * (14 + span),
         project + 3 * unit,
-        (spot, dk, dv, key, value, near_dq, grad_mixed, tier, mixed, weight_own, near_layer, *got),
-        out_specs=[HBM] * 4 + [VMEM] * 4,
-        scratch=[low_buffer, dma((4,))],
-    )
-    layer_out, grad_query, grad_key, grad_value = call(
-        functools.partial(far_layer_kernel, top),
-        [wide, low, low, low],
-        [SMEM] + [VMEM] * 6 + [HBM] * 4,
-        project,
-        (spot, part, mixed_other, weight_other, dq_low, dk_low, dv_low, *outs),
-        out_specs=[HBM] * 4,
-        scratch=[pltpu.VMEM((length, half), BF16), dma((7,))],
-        aliases={7 + n: n for n in range(4)},
+        (spot, dk, dv, key, value, near_dq, grad_mixed, tier, base, weighted, weight_own)
+        + (near_layer, near_query, far_dk, far_dv, *got),
+        out_specs=[HBM] * 4 + [VMEM] * 2,
+        scratch=[low_buffer] * 2 + [dma((4,))],
+    )
+    layer_out, grad_query = call(
+        functools.partial(far_layer_kernel, span),
+        [wide, low],
+        [SMEM] + [VMEM] * 6 + [HBM] * 2,
+        project + unit,
+        (spot, part, base_other, weighted_other, top_other, weight_other, dq_low, layer_out, grad_query),
+        out_specs=[HBM] * 2,
+        scratch=[low_buffer, pltpu.VMEM((length, half), BF16), dma((5,))],
+        aliases={7: 0, 8: 1},
     )
     return tuple(x[None] for x in (layer_out, grad_query, grad_key, grad_value))
 

time: 27.4 us -> 30.7 us (1.12)
  waiting for transfers between devices: 6.71 us -> 8.56 us
  starting transfers between devices: 7.01 us -> 8.54 us
    ppermute x3, waiting for transfers between devices: 6.7 us -> 8.54 us  [swap_blocks(): lax.ppermute(x, 'seq', [(n, n ^ 1 << level) for n in range(lax.axis_size(...]
    ppermute x3, starting transfers between devices: 6.29 us -> 7.21 us  [swap_blocks(): lax.ppermute(x, 'seq', [(n, n ^ 1 << level) for n in range(lax.axis_size(...]
    ppermute x2 -> x3, starting transfers between devices: 0.07 us -> 0.57 us  [the longest x1 0.5 us: on_device(): weighted_other = lax.ppermute(weighted, 'head', swap)]
    pallas_call x11 -> x10, Pallas kernels: 12.8 us -> 12.7 us  [call(): pl.pallas_call(kernel, out_shape=outs, in_specs=in_specs, out_specs=out_s...]
  transfers between devices with their start and end apart: 7 -> 8, of which waited for: 2 -> 3; matrix products, arithmetic and copies ran while one was open for 0% -> 0% of each run, Pallas kernels for 47% -> 38%
where the time goes in v5:
time: 30.7 us; the launch traced here: 30.6 us
  Pallas kernels  12.7 us (41%)
  waiting for transfers between devices  8.56 us (28%)
  starting transfers between devices  8.54 us (28%)
  between operations  0.75 us (2%)
    pallas_call x10, Pallas kernels, call(): pl.pallas_call(kernel, out_shape=outs, in_specs=in_specs, out_specs=out_s...  12.7 us
    ppermute x3, waiting for transfers between devices, swap_blocks(): lax.ppermute(x, 'seq', [(n, n ^ 1 << level) for n in range(lax.axis_size(...  8.54 us
    ppermute x3, starting transfers between devices, swap_blocks(): lax.ppermute(x, 'seq', [(n, n ^ 1 << level) for n in range(lax.axis_size(...  7.21 us
  transfers between devices with their start and end apart: 8, of which 3 were waited for; matrix products, arithmetic and copies ran while one was open for 0% of the time, Pallas kernels for 38%

profile of v5, /device:TPU:0, one launch (start us, length us, event | category | flops | bytes accessed | tf_op | source)
XLA Modules:
  0.0 30.6 jit_solution(10004450736295923114)
XLA Ops:
  0.6 0.6 %collective-permute-start = (bf16[512,1024]{1,0:T(8,128)(2,1)}, bf16[512,1024]{1,0:T(8,128)(2,1)S(1)}, u32[]{:S(2)}, u32[]{:S(2)}) collective-permute-start(bf16[512,1024]{1,0:T(8,128)(2,1)} %bitcast.13), channel_id=1, source_target_pairs={{0,1},{1,0},{2,3},{3,2},{4,5},{5,4},{6,7},{7,6},{8,9},{9,8},{10,11... | collective-permute-start | bytes 3145736 | tf_op jit(solution)/shard_map/ppermute | solution.py:354
  1.2 3.1 %shard_map.93 = (bf16[512,128]{1,0:T(8,128)(2,1)S(1)}, f32[512,16]{1,0:T(8,128)S(1)}, bf16[512,512]{1,0:T(8,128)(2,1)S(1)}, bf16[512,512]{1,0:T(8,128)(2,1)S(1)}...) custom-call(s32[1]{0:T(128)} %bitcast.1.place_ref, ...), custom_call_target="tpu_custom_call" | custom-call | flops 603979776 | bytes 10682376 | tf_op jit(solution)/shard_map/pallas_call | solution.py:38
  4.3 0.0 collective-permute-done.grad_ref
  4.3 1.1 %shard_map.94 = (bf16[512,512]{1,0:T(8,128)(2,1)S(1)}, bf16[512,128]{1,0:T(8,128)(2,1)S(1)}, bf16[512,128]{1,0:T(8,128)(2,1)S(1)}) custom-call(s32[1]{0:T(128)} %bitcast.spot_ref, bf16[512,1024]{1,0:T(8,128)(2,1)S(1)} %collective-permute-done.grad_ref, bf16[512,1024]{1,0:T(8,128)(2,1)S(1)} %get-tuple-element.40.weight_ref, ...), custom_call_target="tpu_custom_call" | custom-call | flops 671088640 | bytes 5111812 | tf_op jit(solution)/shard_map/pallas_call | solution.py:38
  5.4 2.7 %collective-permute-start.1 = (bf16[512,128]{1,0:T(8,128)(2,1)S(1)}, bf16[512,128]{1,0:T(8,128)(2,1)S(1)}, u32[]{:S(2)}, u32[]{:S(2)}) collective-permute-start(bf16[512,128]{1,0:T(8,128)(2,1)S(1)} %get-tuple-element.53), channel_id=1, source_target_pairs={{0,4},{4,0},{8,12},{12,8},{1,5},{5,1},{9,13},{13,9},{2,6},{6,2},{1... | collective-permute-start | bytes 393224 | tf_op jit(solution)/shard_map/ppermute | solution.py:319
  8.1 0.2 collective-permute-start.3
  8.3 2.3 %shard_map.95 = (f32[512,512]{1,0:T(8,128)S(1)}, bf16[512,1024]{1,0:T(8,128)(2,1)S(1)}, f32[512,256]{1,0:T(8,128)S(1)}, bf16[1,512,128]{2,1,0:T(8,128)(2,1)S(1)}) custom-call(bf16[512,512]{1,0:T(8,128)(2,1)S(1)} %get-tuple-element.37.query_ref, bf16[512,512]{1,0:T(8,128)(2,1)S(1)} %get-tuple-element.38.key_ref, ...), custom_call_target="tpu_custom_call" | custom-call | flops 268435456 | bytes 4358144 | tf_op jit(solution)/shard_map/pallas_call | solution.py:38
  10.5 1.7 %collective-permute-done.1.refs_0_.refs_2_.refs_7_ = bf16[512,128]{1,0:T(8,128)(2,1)S(1)} collective-permute-done((bf16[512,128]{1,0:T(8,128)(2,1)S(1)}, bf16[512,128]{1,0:T(8,128)(2,1)S(1)}, u32[]{:S(2)}, u32[]{:S(2)}) %collective-permute-start.1) | collective-permute-done | bytes 131104 | tf_op jit(solution)/shard_map/ppermute | solution.py:319
  12.2 0.3 shard_map.97.refs_0_
  12.5 0.1 collective-permute-start.2
  12.6 0.5 %collective-permute-start.6 = (bf16[512,1024]{1,0:T(8,128)(2,1)S(1)}, bf16[512,1024]{1,0:T(8,128)(2,1)S(1)}, u32[]{:S(2)}, u32[]{:S(2)}) collective-permute-start(bf16[512,1024]{1,0:T(8,128)(2,1)S(1)} %get-tuple-element.42.weighted_ref.refs_1_), channel_id=1, source_target_pairs={{0,1},{1,0},{2,3},{3,2},{4,5},{5,4},{6,7},{7,6},{8,9},{9,8},{10,11... | collective-permute-start | bytes 3145736 | tf_op jit(solution)/shard_map/ppermute | solution.py:373
  13.1 1.7 %collective-permute-start.4 = (bf16[512,128]{1,0:T(8,128)(2,1)S(1)}, bf16[512,128]{1,0:T(8,128)(2,1)S(1)}, u32[]{:S(2)}, u32[]{:S(2)}) collective-permute-start(bf16[512,128]{1,0:T(8,128)(2,1)S(1)} %get-tuple-element.61.a_ref), channel_id=1, source_target_pairs={{0,4},{4,0},{8,12},{12,8},{1,5},{5,1},{9,13},{13,9},{2,6},{6,2},{1... | collective-permute-start | bytes 393224 | tf_op jit(solution)/shard_map/ppermute | solution.py:319
  14.8 3.7 %collective-permute-done.4.b_ref = bf16[512,128]{1,0:T(8,128)(2,1)S(1)} collective-permute-done((bf16[512,128]{1,0:T(8,128)(2,1)S(1)}, bf16[512,128]{1,0:T(8,128)(2,1)S(1)}, u32[]{:S(2)}, u32[]{:S(2)}) %collective-permute-start.4) | collective-permute-done | bytes 131104 | tf_op jit(solution)/shard_map/ppermute | solution.py:319
  18.6 2.8 %collective-permute-start.5 = (bf16[512,128]{1,0:T(8,128)(2,1)S(1)}, bf16[512,128]{1,0:T(8,128)(2,1)S(1)}, u32[]{:S(2)}, u32[]{:S(2)}) collective-permute-start(bf16[512,128]{1,0:T(8,128)(2,1)S(1)} %shard_map.100), channel_id=1, source_target_pairs={{0,8},{4,12},{8,0},{12,4},{1,9},{5,13},{9,1},{13,5},{2,10},{6,14},... | collective-permute-start | bytes 393224 | tf_op jit(solution)/shard_map/ppermute | solution.py:319
  21.4 2.5 %shard_map.96 = (f32[512,512]{1,0:T(8,128)S(1)}, f32[512,512]{1,0:T(8,128)S(1)}, f32[512,512]{1,0:T(8,128)S(1)}) custom-call(bf16[512,512]{1,0:T(8,128)(2,1)S(1)} %get-tuple-element.37.query_ref, bf16[512,512]{1,0:T(8,128)(2,1)S(1)} %get-tuple-element.38.key_ref, bf16[512,512]{1,0:T(8,128)(2,1)S(1)} %get-tuple-element.39.value_ref, ...), custom_call_target="tpu_custom_call" | custom-call | flops 536870912 | bytes 6979584 | tf_op jit(solution)/shard_map/pallas_call | solution.py:38
  23.9 3.1 %collective-permute-done.5.refs_8_ = bf16[512,128]{1,0:T(8,128)(2,1)S(1)} collective-permute-done((bf16[512,128]{1,0:T(8,128)(2,1)S(1)}, bf16[512,128]{1,0:T(8,128)(2,1)S(1)}, u32[]{:S(2)}, u32[]{:S(2)}) %collective-permute-start.5) | collective-permute-done | bytes 131104 | tf_op jit(solution)/shard_map/ppermute | solution.py:319
  27.1 0.0 collective-permute-start.7
  27.1 1.1 %shard_map.98 = (f32[512,512]{1,0:T(8,128)S(1)}, f32[512,1024]{1,0:T(8,128)S(1)}, bf16[512,512]{1,0:T(8,128)(2,1)S(1)}, bf16[512,512]{1,0:T(8,128)(2,1)S(1)}) custom-call(s32[1]{0:T(128)} %bitcast.spot_ref, f32[512,512]{1,0:T(8,128)S(1)} %get-tuple-element.51.dq_ref, f32[512,512]{1,0:T(8,128)S(1)} %get-tuple-element.49.dk_ref, ...), custom_call_target="tpu_custom_call" | custom-call | flops 603979776 | bytes 11173892 | tf_op jit(solution)/shard_map/pallas_call | solution.py:38
  28.2 0.0 collective-permute-done.3.weight_ref
  28.2 0.0 collective-permute-done.2.base_ref
  28.2 0.7 %shard_map.99 = (bf16[512,1024]{1,0:T(8,128)(2,1)S(1)}, bf16[512,512]{1,0:T(8,128)(2,1)S(1)}) custom-call(s32[1]{0:T(128)} %bitcast.spot_ref, f32[512,1024]{1,0:T(8,128)S(1)} %get-tuple-element.56.part_ref, f32[512,512]{1,0:T(8,128)S(1)} %collective-permute-done.2.base_ref, bf16[512,1024]{1,0:T(8,128)(2,1)S(1)} %collective-permute-done.3.weight_ref, ...), custom_call_target="tpu_custom_call" | custom-call | flops 536870912 | bytes 6815748 | tf_op jit(solution)/shard_map/pallas_call | solution.py:38
  29.0 1.5 %shard_map.101 = (bf16[512,1024]{1,0:T(8,128)(2,1)}, bf16[512,512]{1,0:T(8,128)(2,1)}, bf16[512,512]{1,0:T(8,128)(2,1)}, bf16[512,512]{1,0:T(8,128)(2,1)}, f32[5...) custom-call(s32[1]{0:T(128)} %bitcast.spot_ref, f32[512,512]{1,0:T(8,128)S(1)} %get-tuple-element.49.dk_ref, ...), custom_call_target="tpu_custom_call" | custom-call | flops 738197504 | bytes 16023556 | tf_op jit(solution)/shard_map/pallas_call | solution.py:38
  30.5 0.0 collective-permute-done.7.got_ref
  30.5 0.1 shard_map.102
  (2 shorter events, 0.0 us)
Async XLA Ops:
  0.6 3.7 %collective-permute-start = (bf16[512,1024]{1,0:T(8,128)(2,1)}, bf16[512,1024]{1,0:T(8,128)(2,1)S(1)}, u32[]{:S(2)}, u32[]{:S(2)}) collective-permute-start(bf16[512,1024]{1,0:T(8,128)(2,1)} %bitcast.13), channel_id=1, source_target_pairs={{0,1},{1,0},{2,3},{3,2},{4,5},{5,4},{6,7},{7,6},{8,9},{9,8},{10,11... | collective-permute-start | bytes 3145736 | tf_op jit(solution)/shard_map/ppermute | solution.py:354
  5.4 6.8 %collective-permute-start.1 = (bf16[512,128]{1,0:T(8,128)(2,1)S(1)}, bf16[512,128]{1,0:T(8,128)(2,1)S(1)}, u32[]{:S(2)}, u32[]{:S(2)}) collective-permute-start(bf16[512,128]{1,0:T(8,128)(2,1)S(1)} %get-tuple-element.53), channel_id=1, source_target_pairs={{0,4},{4,0},{8,12},{12,8},{1,5},{5,1},{9,13},{13,9},{2,6},{6,2},{1... | collective-permute-start | bytes 393224 | tf_op jit(solution)/shard_map/ppermute | solution.py:319
  8.1 20.2 %collective-permute-start.3 = (bf16[512,1024]{1,0:T(8,128)(2,1)S(1)}, bf16[512,1024]{1,0:T(8,128)(2,1)S(1)}, u32[]{:S(2)}, u32[]{:S(2)}) collective-permute-start(bf16[512,1024]{1,0:T(8,128)(2,1)S(1)} %get-tuple-element.40.weight_ref), channel_id=1, source_target_pairs={{0,1},{1,0},{2,3},{3,2},{4,5},{5,4},{6,7},{7,6},{8,9},{9,8},{10,11... | collective-permute-start | bytes 3145736 | tf_op jit(solution)/shard_map/ppermute | solution.py:372
  12.5 15.7 %collective-permute-start.2 = (f32[512,512]{1,0:T(8,128)S(1)}, f32[512,512]{1,0:T(8,128)S(1)}, u32[]{:S(2)}, u32[]{:S(2)}) collective-permute-start(f32[512,512]{1,0:T(8,128)S(1)} %shard_map.97.refs_0_), channel_id=1, source_target_pairs={{0,1},{1,0},{2,3},{3,2},{4,5},{5,4},{6,7},{7,6},{8,9},{9,8},{10,11... | collective-permute-start | bytes 3145736 | tf_op jit(solution)/shard_map/ppermute | solution.py:398
  12.6 17.9 %collective-permute-start.6 = (bf16[512,1024]{1,0:T(8,128)(2,1)S(1)}, bf16[512,1024]{1,0:T(8,128)(2,1)S(1)}, u32[]{:S(2)}, u32[]{:S(2)}) collective-permute-start(bf16[512,1024]{1,0:T(8,128)(2,1)S(1)} %get-tuple-element.42.weighted_ref.refs_1_), channel_id=1, source_target_pairs={{0,1},{1,0},{2,3},{3,2},{4,5},{5,4},{6,7},{7,6},{8,9},{9,8},{10,11... | collective-permute-start | bytes 3145736 | tf_op jit(solution)/shard_map/ppermute | solution.py:373
  13.1 5.5 %collective-permute-start.4 = (bf16[512,128]{1,0:T(8,128)(2,1)S(1)}, bf16[512,128]{1,0:T(8,128)(2,1)S(1)}, u32[]{:S(2)}, u32[]{:S(2)}) collective-permute-start(bf16[512,128]{1,0:T(8,128)(2,1)S(1)} %get-tuple-element.61.a_ref), channel_id=1, source_target_pairs={{0,4},{4,0},{8,12},{12,8},{1,5},{5,1},{9,13},{13,9},{2,6},{6,2},{1... | collective-permute-start | bytes 393224 | tf_op jit(solution)/shard_map/ppermute | solution.py:319
  18.6 8.5 %collective-permute-start.5 = (bf16[512,128]{1,0:T(8,128)(2,1)S(1)}, bf16[512,128]{1,0:T(8,128)(2,1)S(1)}, u32[]{:S(2)}, u32[]{:S(2)}) collective-permute-start(bf16[512,128]{1,0:T(8,128)(2,1)S(1)} %shard_map.100), channel_id=1, source_target_pairs={{0,8},{4,12},{8,0},{12,4},{1,9},{5,13},{9,1},{13,5},{2,10},{6,14},... | collective-permute-start | bytes 393224 | tf_op jit(solution)/shard_map/ppermute | solution.py:319
  27.1 3.4 %collective-permute-start.7 = (bf16[512,128]{1,0:T(8,128)(2,1)S(1)}, bf16[512,128]{1,0:T(8,128)(2,1)S(1)}, u32[]{:S(2)}, u32[]{:S(2)}) collective-permute-start(bf16[512,128]{1,0:T(8,128)(2,1)S(1)} %collective-permute-done.5.refs_8_), channel_id=1, source_target_pairs={{0,1},{1,0},{2,3},{3,2},{4,5},{5,4},{6,7},{7,6},{8,9},{9,8},{10,11... | collective-permute-start | bytes 393224 | tf_op jit(solution)/shard_map/ppermute | solution.py:413

commit v6 on v5

--- a/solution.py
+++ b/solution.py
@@ -70,27 +70,28 @@
 def prep_kernel(tiers, span, place_ref, spot_ref, mask_hbm, key_hbm, value_hbm, grad_hbm, weight_hbm, query_hbm, *refs):
     state_ref, tier_ref, key, value, weight, rest, query, part_ref, weighted_ref, mask, grad, sems = refs
     mine, other = column(weight_hbm, place_ref[0]), column(weight_hbm, 1 - place_ref[0])
-    sources = [mine, grad_hbm, key_hbm, value_hbm, mask_hbm, query_hbm, other]
-    copies = start_copies(zip(sources, [weight, grad, key, value, mask, query, rest]), sems)
+    sources = [mask_hbm, query_hbm, key_hbm, value_hbm, mine, grad_hbm, other]
+    copies = start_copies(zip(sources, [mask, query, key, value, weight, grad, rest]), sems)
     copies[0].wait()
-    copies[1].wait()
-    part_ref[...] = dot_nt(grad[...], weight[...])
-    copies[2].wait()
-    copies[3].wait()
-    cols = head_slices(key.shape[1])
-    for col in cols:
-        state_ref[col, :] = dot_tn(key[:, col], value[:, col]).astype(BF16)
-    copies[4].wait()
     levels = mask[...].astype(F32)
     rows = [levels[l : l + 1] * jnp.float32(level_scale(l)) for l in range(levels.shape[0])]
     tier = jnp.transpose(jnp.concatenate(rows, axis=0))
     tier_ref[...] = tier
+    copies[1].wait()
+    length, width = query.shape
+    cols = head_slices(width)
+    for j in range(span):
+        scale = jnp.broadcast_to(tier[:, tiers + j : tiers + j + 1], (length, HEAD_DIM))
+        for col in cols:
+            at = j * width + col.start
+            weighted_ref[:, at : at + HEAD_DIM] = (scale * query[:, col].astype(F32)).astype(BF16)
+    copies[2].wait()
+    copies[3].wait()
+    for col in cols:
+        state_ref[col, :] = dot_tn(key[:, col], value[:, col]).astype(BF16)
+    copies[4].wait()
     copies[5].wait()
-    for j in range(span):
-        scale = jnp.broadcast_to(tier[:, tiers + j : tiers + j + 1], (tier.shape[0], HEAD_DIM))
-        for i, col in enumerate(cols):
-            at = (i * span + j) * HEAD_DIM
-            weighted_ref[:, at : at + HEAD_DIM] = (scale * query[:, col].astype(F32)).astype(BF16)
+    part_ref[...] = dot_nt(grad[...], weight[...])
     copies[6].wait()
 
 
@@ -98,9 +99,10 @@
     grad_mixed_ref, send_refs = outs[0], outs[1:]
     grad_mixed = (part_ref[...] + dot_nt(grad_ref[...], weight_ref[...])).astype(BF16)
     grad_mixed_ref[...] = grad_mixed
-    step = span * HEAD_DIM
-    for i, col in enumerate(head_slices(grad_mixed.shape[1])):
-        reach = dot_tn(grad_mixed[:, col], weighted_ref[:, i * step : (i + 1) * step])
+    width = grad_mixed.shape[1]
+    for col in head_slices(width):
+        pieces = [weighted_ref[:, j * width + col.start : j * width + col.stop] for j in range(span)]
+        reach = dot_tn(grad_mixed[:, col], jnp.concatenate(pieces, axis=1))
         state = state_ref[col, :].astype(F32)
         for j in range(span):
             send = jnp.where(upper(spot_ref, j) > 0, reach[:, j * HEAD_DIM : (j + 1) * HEAD_DIM], state)
@@ -190,43 +192,56 @@
             dv_ref[rows, col] = dv[m]
 
 
-def low_states(state_refs, col, spot_ref):
-    kept = [(ref[col, :].astype(F32) * upper(spot_ref, j).astype(F32)).astype(BF16) for j, ref in enumerate(state_refs)]
-    return jnp.concatenate(kept, axis=0)
-
-
-def low_back(back_refs, col, spot_ref):
-    kept = [ref[col, :].astype(F32) * (1 - upper(spot_ref, j)).astype(F32) for j, ref in enumerate(back_refs)]
-    return functools.reduce(jnp.add, kept).astype(BF16)
+def head_pairs(width):
+    cols = head_slices(width)
+    pairs = [cols[i : i + 2] for i in range(0, len(cols), 2)]
+    return [(pair, slice(pair[0].start, pair[-1].stop)) for pair in pairs]
+
+
+def block_diagonal(blocks):
+    zero = jnp.zeros_like(blocks[0])
+    rows = [jnp.concatenate([x if i == j else zero for j in range(len(blocks))], axis=1) for i, x in enumerate(blocks)]
+    return jnp.concatenate(rows, axis=0)
 
 
 def far(spot_ref, top):
     return upper(spot_ref, top) > 0
 
 
-def base_kernel(span, spot_ref, mixed_ref, weighted_ref, *refs):
+def low_state(ref, pair, spot_ref, level):
+    keep = upper(spot_ref, level).astype(F32)
+    return block_diagonal([(ref[col, :].astype(F32) * keep).astype(BF16) for col in pair])
+
+
+def low_back(refs, pair, spot_ref):
+    blocks = []
+    for col in pair:
+        kept = [ref[col, :].astype(F32) * (1 - upper(spot_ref, j)).astype(F32) for j, ref in enumerate(refs)]
+        blocks.append(functools.reduce(jnp.add, kept).astype(BF16))
+    return block_diagonal(blocks)
+
+
+def base_kernel(spot_ref, mixed_ref, weighted_ref, *refs):
     got_refs, out_ref = refs[:-1], refs[-1]
-    for i, col in enumerate(head_slices(mixed_ref.shape[1])):
-        total = mixed_ref[:, col]
-        if got_refs:
-            at = i * span * HEAD_DIM
-            weighted = weighted_ref[:, at : at + len(got_refs) * HEAD_DIM]
-            total = total + dot(weighted, low_states(got_refs, col, spot_ref))
-        out_ref[:, col] = total
+    width = mixed_ref.shape[1]
+    for pair, cols in head_pairs(width):
+        total = mixed_ref[:, cols]
+        for j, ref in enumerate(got_refs):
+            weighted = weighted_ref[:, j * width + cols.start : j * width + cols.stop]
+            total = total + dot(weighted, low_state(ref, pair, spot_ref, j))
+        out_ref[:, cols] = total
 
 
 def early_kernel(tiers, top, spot_ref, dq_ref, dk_ref, dv_ref, key_ref, value_ref, grad_ref, tier_ref, *refs):
     base_ref, weight_ref = refs[:2]
     got_refs, (dq_out, part_ref, dk_low, dv_low) = refs[2:-4], refs[-4:]
-    cols = head_slices(dq_ref.shape[1])
-    for col in cols:
-        total = dq_ref[:, col]
-        if got_refs:
-            rest = dot_nt(grad_ref[:, col], low_states(got_refs, col, spot_ref))
-            for j in range(top):
-                scale = tier_ref[:, tiers + j : tiers + j + 1]
-                total = total + scale * rest[:, j * HEAD_DIM : (j + 1) * HEAD_DIM]
-        dq_out[:, col] = total
+    pairs = head_pairs(dq_ref.shape[1])
+    for pair, cols in pairs:
+        total = dq_ref[:, cols]
+        for j, ref in enumerate(got_refs):
+            rest = dot_nt(grad_ref[:, cols], low_state(ref, pair, spot_ref, j))
+            total = total + tier_ref[:, tiers + j : tiers + j + 1] * rest
+        dq_out[:, cols] = total
 
     @pl.when(jnp.logical_not(far(spot_ref, top)))
     def _():
@@ -234,14 +249,14 @@
 
     @pl.when(far(spot_ref, top))
     def _():
-        for col in cols:
-            dk, dv = dk_ref[:, col], dv_ref[:, col]
+        for pair, cols in pairs:
+            dk, dv = dk_ref[:, cols], dv_ref[:, cols]
             if got_refs:
-                back = low_back(got_refs, col, spot_ref)
-                dk = dk + dot(value_ref[:, col], back)
-                dv = dv + dot_nt(key_ref[:, col], back)
-            dk_low[:, col] = dk.astype(BF16)
-            dv_low[:, col] = dv.astype(BF16)
+                back = low_back(got_refs, pair, spot_ref)
+                dk = dk + dot(value_ref[:, cols], back)
+                dv = dv + dot_nt(key_ref[:, cols], back)
+            dk_low[:, cols] = dk.astype(BF16)
+            dv_low[:, cols] = dv.astype(BF16)
 
 
 def near_layer_kernel(top, spot_ref, part_ref, base_ref, weight_ref, dq_ref, out_ref, dq_low):
@@ -251,29 +266,33 @@
         dq_low[...] = dq_ref[...].astype(BF16)
 
 
-def top_columns(weighted_ref, i, span):
-    at = (i * span + span - 1) * HEAD_DIM
-    return weighted_ref[:, at : at + HEAD_DIM]
+def top_mixed(base_ref, weighted_ref, got_ref):
+    width = base_ref.shape[1]
+    mixed = []
+    for pair, cols in head_pairs(width):
+        weighted = weighted_ref[:, pl.ds(weighted_ref.shape[1] - width + cols.start, cols.stop - cols.start)]
+        state = block_diagonal([got_ref[col, :] for col in pair])
+        mixed.append((base_ref[:, cols] + dot(weighted, state)).astype(BF16))
+    return jnp.concatenate(mixed, axis=1)
 
 
 def finish_kernel(tiers, spot_ref, dk_ref, dv_ref, key_ref, value_ref, dq_ref, grad_ref, tier_ref, *refs):
     base_ref, weighted_ref, weight_ref, near_layer, near_dq, far_dk, far_dv = refs[:7]
     got_refs = refs[7:-9]
     out_hbm, dq_hbm, dk_hbm, dv_hbm, part_ref, dq_low, dk_low, dv_low, sems = refs[-9:]
-    span = len(got_refs)
-    top = span - 1
-    cols = head_slices(key_ref.shape[1])
+    top = len(got_refs) - 1
+    pairs = head_pairs(key_ref.shape[1])
 
     @pl.when(jnp.logical_not(far(spot_ref, top)))
     def _():
         copies = start_copies([(near_layer, out_hbm), (near_dq, dq_hbm)], sems)
-        backs = [low_back(got_refs, col, spot_ref) for col in cols]
-        for col, back in zip(cols, backs):
-            dk_low[:, col] = (dk_ref[:, col] + dot(value_ref[:, col], back)).astype(BF16)
+        backs = [low_back(got_refs, pair, spot_ref) for pair, _ in pairs]
+        for (_, cols), back in zip(pairs, backs):
+            dk_low[:, cols] = (dk_ref[:, cols] + dot(value_ref[:, cols], back)).astype(BF16)
         copies.append(pltpu.make_async_copy(dk_low, dk_hbm, sems.at[2]))
         copies[-1].start()
-        for col, back in zip(cols, backs):
-            dv_low[:, col] = (dv_ref[:, col] + dot_nt(key_ref[:, col], back)).astype(BF16)
+        for (_, cols), back in zip(pairs, backs):
+            dv_low[:, cols] = (dv_ref[:, cols] + dot_nt(key_ref[:, cols], back)).astype(BF16)
         copies.append(pltpu.make_async_copy(dv_low, dv_hbm, sems.at[3]))
         copies[-1].start()
         for copy in copies:
@@ -282,28 +301,22 @@
     @pl.when(far(spot_ref, top))
     def _():
         copies = start_copies([(far_dk, dk_hbm), (far_dv, dv_hbm)], sems)
-        mixed = []
-        for i, col in enumerate(cols):
-            total = base_ref[:, col] + dot(top_columns(weighted_ref, i, span), got_refs[top][col, :])
-            mixed.append(total.astype(BF16))
-        part_ref[...] = dot(jnp.concatenate(mixed, axis=1), weight_ref[...])
+        part_ref[...] = dot(top_mixed(base_ref, weighted_ref, got_refs[top]), weight_ref[...])
         scale = tier_ref[:, tiers + top : tiers + top + 1]
-        for col in cols:
-            rest = dot_nt(grad_ref[:, col], got_refs[top][col, :])
-            dq_low[:, col] = (dq_ref[:, col] + scale * rest).astype(BF16)
+        for pair, cols in pairs:
+            rest = dot_nt(grad_ref[:, cols], block_diagonal([got_refs[top][col, :] for col in pair]))
+            dq_low[:, cols] = (dq_ref[:, cols] + scale * rest).astype(BF16)
         for copy in copies:
             copy.wait()
 
 
-def far_layer_kernel(span, spot_ref, part_ref, base_ref, weighted_ref, got_ref, weight_ref, dq_ref, *refs):
+def far_layer_kernel(top, spot_ref, part_ref, base_ref, weighted_ref, got_ref, weight_ref, dq_ref, *refs):
     out_hbm, dq_hbm, mixed_low, out_low, sems = refs[2:]
 
-    @pl.when(far(spot_ref, span - 1))
+    @pl.when(far(spot_ref, top))
     def _():
         copies = start_copies([(dq_ref, dq_hbm)], sems)
-        for i, col in enumerate(head_slices(base_ref.shape[1])):
-            total = base_ref[:, col] + dot(top_columns(weighted_ref, i, span), got_ref[col, :])
-            mixed_low[:, col] = total.astype(BF16)
+        mixed_low[...] = top_mixed(base_ref, weighted_ref, got_ref)
         chunks = sems.shape[0] - 1
         rows = part_ref.shape[0] // chunks
         for n in range(chunks):
@@ -388,13 +401,7 @@
         backward_kernel, [high] * 3, [VMEM] * 8, 8 * unit, (query, key, value, grad_mixed, tier, probs, blend, inner)
     )
     top = span - 1
-    (base,) = call(
-        functools.partial(base_kernel, span),
-        [high],
-        [SMEM] + [VMEM] * (2 + top),
-        top * unit,
-        (spot, mixed, weighted, *got[:top]),
-    )
+    (base,) = call(base_kernel, [high], [SMEM] + [VMEM] * (2 + top), top * unit, (spot, mixed, weighted, *got[:top]))
     base_other = lax.ppermute(base, "head", swap)
     near_dq, part, far_dk, far_dv = call(
         functools.partial(early_kernel, tiers, top),
@@ -422,7 +429,7 @@
         scratch=[low_buffer] * 2 + [dma((4,))],
     )
     layer_out, grad_query = call(
-        functools.partial(far_layer_kernel, span),
+        functools.partial(far_layer_kernel, top),
         [wide, low],
         [SMEM] + [VMEM] * 6 + [HBM] * 2,
         project + unit,

time: 30.7 us -> 30.4 us (level)
    pallas_call x10, Pallas kernels: 12.7 us -> 12.4 us  [call(): pl.pallas_call(kernel, out_shape=outs, in_specs=in_specs, out_specs=out_s...]
  transfers between devices with their start and end apart: 8 -> 8, of which waited for: 3 -> 3; matrix products, arithmetic and copies ran while one was open for 0% -> 0% of each run, Pallas kernels for 38% -> 37%
where the time goes in v6:
time: 30.4 us; the launch traced here: 30.3 us
  Pallas kernels  12.4 us (41%)
  waiting for transfers between devices  8.57 us (28%)
  starting transfers between devices  8.52 us (28%)
  between operations  0.75 us (2%)
    pallas_call x10, Pallas kernels, call(): pl.pallas_call(kernel, out_shape=outs, in_specs=in_specs, out_specs=out_s...  12.4 us
    ppermute x3, waiting for transfers between devices, swap_blocks(): lax.ppermute(x, 'seq', [(n, n ^ 1 << level) for n in range(lax.axis_size(...  8.56 us
    ppermute x3, starting transfers between devices, swap_blocks(): lax.ppermute(x, 'seq', [(n, n ^ 1 << level) for n in range(lax.axis_size(...  7.19 us
  transfers between devices with their start and end apart: 8, of which 3 were waited for; matrix products, arithmetic and copies ran while one was open for 0% of the time, Pallas kernels for 37%

profile of v6, /device:TPU:0, one launch (start us, length us, event | category | flops | bytes accessed | tf_op | source)
XLA Modules:
  0.0 30.3 jit_solution(1176018744303898601)
XLA Ops:
  0.6 0.6 %collective-permute-start = (bf16[512,1024]{1,0:T(8,128)(2,1)}, bf16[512,1024]{1,0:T(8,128)(2,1)S(1)}, u32[]{:S(2)}, u32[]{:S(2)}) collective-permute-start(bf16[512,1024]{1,0:T(8,128)(2,1)} %bitcast.13), channel_id=1, source_target_pairs={{0,1},{1,0},{2,3},{3,2},{4,5},{5,4},{6,7},{7,6},{8,9},{9,8},{10,11... | collective-permute-start | bytes 3145736 | tf_op jit(solution)/shard_map/ppermute | solution.py:367
  1.2 2.8 %shard_map.93 = (bf16[512,128]{1,0:T(8,128)(2,1)S(1)}, f32[512,16]{1,0:T(8,128)S(1)}, bf16[512,512]{1,0:T(8,128)(2,1)S(1)}, bf16[512,512]{1,0:T(8,128)(2,1)S(1)}...) custom-call(s32[1]{0:T(128)} %bitcast.1.place_ref, ...), custom_call_target="tpu_custom_call" | custom-call | flops 603979776 | bytes 10682376 | tf_op jit(solution)/shard_map/pallas_call | solution.py:38
  4.0 0.0 collective-permute-done.grad_ref
  4.0 1.1 %shard_map.94 = (bf16[512,512]{1,0:T(8,128)(2,1)S(1)}, bf16[512,128]{1,0:T(8,128)(2,1)S(1)}, bf16[512,128]{1,0:T(8,128)(2,1)S(1)}) custom-call(s32[1]{0:T(128)} %bitcast.spot_ref, bf16[512,1024]{1,0:T(8,128)(2,1)S(1)} %collective-permute-done.grad_ref, bf16[512,1024]{1,0:T(8,128)(2,1)S(1)} %get-tuple-element.40.weight_ref, ...), custom_call_target="tpu_custom_call" | custom-call | flops 671088640 | bytes 5111812 | tf_op jit(solution)/shard_map/pallas_call | solution.py:38
  5.1 2.7 %collective-permute-start.1 = (bf16[512,128]{1,0:T(8,128)(2,1)S(1)}, bf16[512,128]{1,0:T(8,128)(2,1)S(1)}, u32[]{:S(2)}, u32[]{:S(2)}) collective-permute-start(bf16[512,128]{1,0:T(8,128)(2,1)S(1)} %get-tuple-element.53), channel_id=1, source_target_pairs={{0,4},{4,0},{8,12},{12,8},{1,5},{5,1},{9,13},{13,9},{2,6},{6,2},{1... | collective-permute-start | bytes 393224 | tf_op jit(solution)/shard_map/ppermute | solution.py:332
  7.8 0.2 collective-permute-start.3
  8.0 2.3 %shard_map.95 = (f32[512,512]{1,0:T(8,128)S(1)}, bf16[512,1024]{1,0:T(8,128)(2,1)S(1)}, f32[512,256]{1,0:T(8,128)S(1)}, bf16[1,512,128]{2,1,0:T(8,128)(2,1)S(1)}) custom-call(bf16[512,512]{1,0:T(8,128)(2,1)S(1)} %get-tuple-element.37.query_ref, bf16[512,512]{1,0:T(8,128)(2,1)S(1)} %get-tuple-element.38.key_ref, ...), custom_call_target="tpu_custom_call" | custom-call | flops 268435456 | bytes 4358144 | tf_op jit(solution)/shard_map/pallas_call | solution.py:38
  10.3 1.7 %collective-permute-done.1.refs_0_.refs_2_.refs_7_ = bf16[512,128]{1,0:T(8,128)(2,1)S(1)} collective-permute-done((bf16[512,128]{1,0:T(8,128)(2,1)S(1)}, bf16[512,128]{1,0:T(8,128)(2,1)S(1)}, u32[]{:S(2)}, u32[]{:S(2)}) %collective-permute-start.1) | collective-permute-done | bytes 131104 | tf_op jit(solution)/shard_map/ppermute | solution.py:332
  11.9 0.3 shard_map.97.refs_0_
  12.2 0.1 collective-permute-start.2
  12.3 0.5 %collective-permute-start.6 = (bf16[512,1024]{1,0:T(8,128)(2,1)S(1)}, bf16[512,1024]{1,0:T(8,128)(2,1)S(1)}, u32[]{:S(2)}, u32[]{:S(2)}) collective-permute-start(bf16[512,1024]{1,0:T(8,128)(2,1)S(1)} %get-tuple-element.42.weighted_ref.refs_1_), channel_id=1, source_target_pairs={{0,1},{1,0},{2,3},{3,2},{4,5},{5,4},{6,7},{7,6},{8,9},{9,8},{10,11... | collective-permute-start | bytes 3145736 | tf_op jit(solution)/shard_map/ppermute | solution.py:386
  12.8 1.7 %collective-permute-start.4 = (bf16[512,128]{1,0:T(8,128)(2,1)S(1)}, bf16[512,128]{1,0:T(8,128)(2,1)S(1)}, u32[]{:S(2)}, u32[]{:S(2)}) collective-permute-start(bf16[512,128]{1,0:T(8,128)(2,1)S(1)} %get-tuple-element.61.a_ref), channel_id=1, source_target_pairs={{0,4},{4,0},{8,12},{12,8},{1,5},{5,1},{9,13},{13,9},{2,6},{6,2},{1... | collective-permute-start | bytes 393224 | tf_op jit(solution)/shard_map/ppermute | solution.py:332
  14.5 3.8 %collective-permute-done.4.b_ref = bf16[512,128]{1,0:T(8,128)(2,1)S(1)} collective-permute-done((bf16[512,128]{1,0:T(8,128)(2,1)S(1)}, bf16[512,128]{1,0:T(8,128)(2,1)S(1)}, u32[]{:S(2)}, u32[]{:S(2)}) %collective-permute-start.4) | collective-permute-done | bytes 131104 | tf_op jit(solution)/shard_map/ppermute | solution.py:332
  18.3 2.8 %collective-permute-start.5 = (bf16[512,128]{1,0:T(8,128)(2,1)S(1)}, bf16[512,128]{1,0:T(8,128)(2,1)S(1)}, u32[]{:S(2)}, u32[]{:S(2)}) collective-permute-start(bf16[512,128]{1,0:T(8,128)(2,1)S(1)} %shard_map.100), channel_id=1, source_target_pairs={{0,8},{4,12},{8,0},{12,4},{1,9},{5,13},{9,1},{13,5},{2,10},{6,14},... | collective-permute-start | bytes 393224 | tf_op jit(solution)/shard_map/ppermute | solution.py:332
  21.1 2.5 %shard_map.96 = (f32[512,512]{1,0:T(8,128)S(1)}, f32[512,512]{1,0:T(8,128)S(1)}, f32[512,512]{1,0:T(8,128)S(1)}) custom-call(bf16[512,512]{1,0:T(8,128)(2,1)S(1)} %get-tuple-element.37.query_ref, bf16[512,512]{1,0:T(8,128)(2,1)S(1)} %get-tuple-element.38.key_ref, bf16[512,512]{1,0:T(8,128)(2,1)S(1)} %get-tuple-element.39.value_ref, ...), custom_call_target="tpu_custom_call" | custom-call | flops 536870912 | bytes 6979584 | tf_op jit(solution)/shard_map/pallas_call | solution.py:38
  23.7 3.2 %collective-permute-done.5.refs_8_ = bf16[512,128]{1,0:T(8,128)(2,1)S(1)} collective-permute-done((bf16[512,128]{1,0:T(8,128)(2,1)S(1)}, bf16[512,128]{1,0:T(8,128)(2,1)S(1)}, u32[]{:S(2)}, u32[]{:S(2)}) %collective-permute-start.5) | collective-permute-done | bytes 131104 | tf_op jit(solution)/shard_map/ppermute | solution.py:332
  26.8 0.0 collective-permute-start.7
  26.8 1.1 %shard_map.98 = (f32[512,512]{1,0:T(8,128)S(1)}, f32[512,1024]{1,0:T(8,128)S(1)}, bf16[512,512]{1,0:T(8,128)(2,1)S(1)}, bf16[512,512]{1,0:T(8,128)(2,1)S(1)}) custom-call(s32[1]{0:T(128)} %bitcast.spot_ref, f32[512,512]{1,0:T(8,128)S(1)} %get-tuple-element.51.dq_ref, f32[512,512]{1,0:T(8,128)S(1)} %get-tuple-element.49.dk_ref, ...), custom_call_target="tpu_custom_call" | custom-call | flops 603979776 | bytes 11173892 | tf_op jit(solution)/shard_map/pallas_call | solution.py:38
  27.9 0.0 collective-permute-done.2.base_ref
  27.9 0.7 %shard_map.99 = (bf16[512,1024]{1,0:T(8,128)(2,1)S(1)}, bf16[512,512]{1,0:T(8,128)(2,1)S(1)}) custom-call(s32[1]{0:T(128)} %bitcast.spot_ref, f32[512,1024]{1,0:T(8,128)S(1)} %get-tuple-element.56.part_ref, f32[512,512]{1,0:T(8,128)S(1)} %collective-permute-done.2.base_ref, bf16[512,1024]{1,0:T(8,128)(2,1)S(1)} %collective-permute-done.3.weight_ref, ...), custom_call_target="tpu_custom_call" | custom-call | flops 536870912 | bytes 6815748 | tf_op jit(solution)/shard_map/pallas_call | solution.py:38
  28.6 1.5 %shard_map.101 = (bf16[512,1024]{1,0:T(8,128)(2,1)}, bf16[512,512]{1,0:T(8,128)(2,1)}, bf16[512,512]{1,0:T(8,128)(2,1)}, bf16[512,512]{1,0:T(8,128)(2,1)}, f32[5...) custom-call(s32[1]{0:T(128)} %bitcast.spot_ref, f32[512,512]{1,0:T(8,128)S(1)} %get-tuple-element.49.dk_ref, ...), custom_call_target="tpu_custom_call" | custom-call | flops 738197504 | bytes 16023556 | tf_op jit(solution)/shard_map/pallas_call | solution.py:38
  30.2 0.0 collective-permute-done.6.weighted_ref
  30.2 0.0 collective-permute-done.7.got_ref
  30.2 0.1 shard_map.102
  (2 shorter events, 0.0 us)
Async XLA Ops:
  0.6 3.4 %collective-permute-start = (bf16[512,1024]{1,0:T(8,128)(2,1)}, bf16[512,1024]{1,0:T(8,128)(2,1)S(1)}, u32[]{:S(2)}, u32[]{:S(2)}) collective-permute-start(bf16[512,1024]{1,0:T(8,128)(2,1)} %bitcast.13), channel_id=1, source_target_pairs={{0,1},{1,0},{2,3},{3,2},{4,5},{5,4},{6,7},{7,6},{8,9},{9,8},{10,11... | collective-permute-start | bytes 3145736 | tf_op jit(solution)/shard_map/ppermute | solution.py:367
  5.1 6.8 %collective-permute-start.1 = (bf16[512,128]{1,0:T(8,128)(2,1)S(1)}, bf16[512,128]{1,0:T(8,128)(2,1)S(1)}, u32[]{:S(2)}, u32[]{:S(2)}) collective-permute-start(bf16[512,128]{1,0:T(8,128)(2,1)S(1)} %get-tuple-element.53), channel_id=1, source_target_pairs={{0,4},{4,0},{8,12},{12,8},{1,5},{5,1},{9,13},{13,9},{2,6},{6,2},{1... | collective-permute-start | bytes 393224 | tf_op jit(solution)/shard_map/ppermute | solution.py:332
  7.8 20.1 %collective-permute-start.3 = (bf16[512,1024]{1,0:T(8,128)(2,1)S(1)}, bf16[512,1024]{1,0:T(8,128)(2,1)S(1)}, u32[]{:S(2)}, u32[]{:S(2)}) collective-permute-start(bf16[512,1024]{1,0:T(8,128)(2,1)S(1)} %get-tuple-element.40.weight_ref), channel_id=1, source_target_pairs={{0,1},{1,0},{2,3},{3,2},{4,5},{5,4},{6,7},{7,6},{8,9},{9,8},{10,11... | collective-permute-start | bytes 3145736 | tf_op jit(solution)/shard_map/ppermute | solution.py:385
  12.2 15.7 %collective-permute-start.2 = (f32[512,512]{1,0:T(8,128)S(1)}, f32[512,512]{1,0:T(8,128)S(1)}, u32[]{:S(2)}, u32[]{:S(2)}) collective-permute-start(f32[512,512]{1,0:T(8,128)S(1)} %shard_map.97.refs_0_), channel_id=1, source_target_pairs={{0,1},{1,0},{2,3},{3,2},{4,5},{5,4},{6,7},{7,6},{8,9},{9,8},{10,11... | collective-permute-start | bytes 3145736 | tf_op jit(solution)/shard_map/ppermute | solution.py:405
  12.3 17.9 %collective-permute-start.6 = (bf16[512,1024]{1,0:T(8,128)(2,1)S(1)}, bf16[512,1024]{1,0:T(8,128)(2,1)S(1)}, u32[]{:S(2)}, u32[]{:S(2)}) collective-permute-start(bf16[512,1024]{1,0:T(8,128)(2,1)S(1)} %get-tuple-element.42.weighted_ref.refs_1_), channel_id=1, source_target_pairs={{0,1},{1,0},{2,3},{3,2},{4,5},{5,4},{6,7},{7,6},{8,9},{9,8},{10,11... | collective-permute-start | bytes 3145736 | tf_op jit(solution)/shard_map/ppermute | solution.py:386
  12.8 5.5 %collective-permute-start.4 = (bf16[512,128]{1,0:T(8,128)(2,1)S(1)}, bf16[512,128]{1,0:T(8,128)(2,1)S(1)}, u32[]{:S(2)}, u32[]{:S(2)}) collective-permute-start(bf16[512,128]{1,0:T(8,128)(2,1)S(1)} %get-tuple-element.61.a_ref), channel_id=1, source_target_pairs={{0,4},{4,0},{8,12},{12,8},{1,5},{5,1},{9,13},{13,9},{2,6},{6,2},{1... | collective-permute-start | bytes 393224 | tf_op jit(solution)/shard_map/ppermute | solution.py:332
  18.3 8.5 %collective-permute-start.5 = (bf16[512,128]{1,0:T(8,128)(2,1)S(1)}, bf16[512,128]{1,0:T(8,128)(2,1)S(1)}, u32[]{:S(2)}, u32[]{:S(2)}) collective-permute-start(bf16[512,128]{1,0:T(8,128)(2,1)S(1)} %shard_map.100), channel_id=1, source_target_pairs={{0,8},{4,12},{8,0},{12,4},{1,9},{5,13},{9,1},{13,5},{2,10},{6,14},... | collective-permute-start | bytes 393224 | tf_op jit(solution)/shard_map/ppermute | solution.py:332
  26.8 3.4 %collective-permute-start.7 = (bf16[512,128]{1,0:T(8,128)(2,1)S(1)}, bf16[512,128]{1,0:T(8,128)(2,1)S(1)}, u32[]{:S(2)}, u32[]{:S(2)}) collective-permute-start(bf16[512,128]{1,0:T(8,128)(2,1)S(1)} %collective-permute-done.5.refs_8_), channel_id=1, source_target_pairs={{0,1},{1,0},{2,3},{3,2},{4,5},{5,4},{6,7},{7,6},{8,9},{9,8},{10,11... | collective-permute-start | bytes 393224 | tf_op jit(solution)/shard_map/ppermute | solution.py:420

commit v7 on v6

--- a/solution.py
+++ b/solution.py
@@ -107,6 +107,21 @@
         for j in range(span):
             send = jnp.where(upper(spot_ref, j) > 0, reach[:, j * HEAD_DIM : (j + 1) * HEAD_DIM], state)
             send_refs[j][col, :] = send.astype(BF16)
+
+
+def half_kernel(spot_ref, sent_ref, keep_ref, give_ref):
+    half = keep_ref.shape[0]
+    odd = upper(spot_ref, 0) > 0
+    first, second = sent_ref[:half, :], sent_ref[half:, :]
+    keep_ref[...] = jnp.where(odd, second, first)
+    give_ref[...] = jnp.where(odd, first, second)
+
+
+def join_kernel(spot_ref, same_ref, cross_ref, out_ref):
+    half = same_ref.shape[0]
+    odd = upper(spot_ref, 0) > 0
+    out_ref[:half, :] = jnp.where(odd, cross_ref[...], same_ref[...])
+    out_ref[half:, :] = jnp.where(odd, same_ref[...], cross_ref[...])
 
 
 def add_kernel(a_ref, b_ref, out_ref):
@@ -336,6 +351,16 @@
     return call(add_kernel, [jax.ShapeDtypeStruct(a.shape, BF16)], [VMEM] * 2, a.size, (a, b), limit=4)[0]
 
 
+def exchange_halves(spot, sent):
+    half = jax.ShapeDtypeStruct((sent.shape[0] // 2, HEAD_DIM), BF16)
+    keep, give = call(half_kernel, [half] * 2, [SMEM, VMEM], sent.size, (spot, sent), limit=4)
+    total = add_low(keep, swap_blocks(give, 0))
+    same = swap_blocks(total, 1)
+    cross = lax.ppermute(total, "seq", [(n, n ^ 3) for n in range(lax.axis_size("seq"))])
+    whole = jax.ShapeDtypeStruct(sent.shape, BF16)
+    return call(join_kernel, [whole], [SMEM] + [VMEM] * 2, sent.size, (spot, same, cross), limit=4)[0]
+
+
 def hbm(*arrays):
     return [pltpu.with_memory_space_constraint(x, pltpu.HBM) for x in arrays]
 
@@ -394,6 +419,9 @@
     )
     got = []
     for level, total in enumerate(sends):
+        if span == 2 and level == 1:
+            got.append(exchange_halves(spot, total))
+            continue
         for step in range(level):
             total = add_low(total, swap_blocks(total, step))
         got.append(swap_blocks(total, level))

time: 30.4 us -> 29.8 us (0.980)
  waiting for transfers between devices: 8.57 us -> 6.37 us
  starting transfers between devices: 8.52 us -> 10 us
    ppermute x3, waiting for transfers between devices: 8.56 us -> 4.19 us  [swap_blocks(): lax.ppermute(x, 'seq', [(n, n ^ 1 << level) for n in range(lax.axis_size(...]
    ppermute x0 -> x1, waiting for transfers between devices: none -> 2.17 us  [exchange_halves(): lax.ppermute(total, 'seq', [(n, n ^ 3) for n in range(lax.axis_size('seq'...]
    ppermute x0 -> x1, starting transfers between devices: none -> 1.35 us  [exchange_halves(): lax.ppermute(total, 'seq', [(n, n ^ 3) for n in range(lax.axis_size('seq'...]
    pallas_call x10 -> x12, Pallas kernels: 12.4 us -> 12.5 us  [call(): pl.pallas_call(kernel, out_shape=outs, in_specs=in_specs, out_specs=out_s...]
  transfers between devices with their start and end apart: 8 -> 9, of which waited for: 3 -> 3; matrix products, arithmetic and copies ran while one was open for 0% -> 0% of each run, Pallas kernels for 37% -> 38%
where the time goes in v7:
time: 29.8 us; the launch traced here: 29.6 us
  Pallas kernels  12.5 us (42%)
  starting transfers between devices  10 us (34%)
  waiting for transfers between devices  6.37 us (21%)
  between operations  0.77 us (3%)
    pallas_call x12, Pallas kernels, call(): pl.pallas_call(kernel, out_shape=outs, in_specs=in_specs, out_specs=out_s...  12.5 us
    ppermute x3, starting transfers between devices, swap_blocks(): lax.ppermute(x, 'seq', [(n, n ^ 1 << level) for n in range(lax.axis_size(...  7.25 us
    ppermute x3, waiting for transfers between devices, swap_blocks(): lax.ppermute(x, 'seq', [(n, n ^ 1 << level) for n in range(lax.axis_size(...  4.19 us
    ppermute x1, waiting for transfers between devices, exchange_halves(): lax.ppermute(total, 'seq', [(n, n ^ 3) for n in range(lax.axis_size('seq'...  2.17 us
    ppermute x1, starting transfers between devices, exchange_halves(): lax.ppermute(total, 'seq', [(n, n ^ 3) for n in range(lax.axis_size('seq'...  1.35 us
  transfers between devices with their start and end apart: 9, of which 3 were waited for; matrix products, arithmetic and copies ran while one was open for 0% of the time, Pallas kernels for 38%

profile of v7, /device:TPU:0, one launch (start us, length us, event | category | flops | bytes accessed | tf_op | source)
XLA Modules:
  0.0 29.6 jit_solution(14699264680276152592)
XLA Ops:
  0.6 0.6 %collective-permute-start = (bf16[512,1024]{1,0:T(8,128)(2,1)}, bf16[512,1024]{1,0:T(8,128)(2,1)S(1)}, u32[]{:S(2)}, u32[]{:S(2)}) collective-permute-start(bf16[512,1024]{1,0:T(8,128)(2,1)} %bitcast.13), channel_id=1, source_target_pairs={{0,1},{1,0},{2,3},{3,2},{4,5},{5,4},{6,7},{7,6},{8,9},{9,8},{10,11... | collective-permute-start | bytes 3145736 | tf_op jit(solution)/shard_map/ppermute | solution.py:392
  1.2 2.8 %shard_map.93 = (bf16[512,128]{1,0:T(8,128)(2,1)S(1)}, f32[512,16]{1,0:T(8,128)S(1)}, bf16[512,512]{1,0:T(8,128)(2,1)S(1)}, bf16[512,512]{1,0:T(8,128)(2,1)S(1)}...) custom-call(s32[1]{0:T(128)} %bitcast.1.place_ref, ...), custom_call_target="tpu_custom_call" | custom-call | flops 603979776 | bytes 10682376 | tf_op jit(solution)/shard_map/pallas_call | solution.py:38
  4.0 1.1 %shard_map.94 = (bf16[512,512]{1,0:T(8,128)(2,1)S(1)}, bf16[512,128]{1,0:T(8,128)(2,1)S(1)}, bf16[512,128]{1,0:T(8,128)(2,1)S(1)}) custom-call(s32[1]{0:T(128)} %bitcast.spot_ref, bf16[512,1024]{1,0:T(8,128)(2,1)S(1)} %collective-permute-done.grad_ref, bf16[512,1024]{1,0:T(8,128)(2,1)S(1)} %get-tuple-element.42.weight_ref, ...), custom_call_target="tpu_custom_call" | custom-call | flops 671088640 | bytes 5111812 | tf_op jit(solution)/shard_map/pallas_call | solution.py:38
  5.1 2.7 %collective-permute-start.1 = (bf16[512,128]{1,0:T(8,128)(2,1)S(1)}, bf16[512,128]{1,0:T(8,128)(2,1)S(1)}, u32[]{:S(2)}, u32[]{:S(2)}) collective-permute-start(bf16[512,128]{1,0:T(8,128)(2,1)S(1)} %get-tuple-element.55), channel_id=1, source_target_pairs={{0,4},{4,0},{8,12},{12,8},{1,5},{5,1},{9,13},{13,9},{2,6},{6,2},{1... | collective-permute-start | bytes 393224 | tf_op jit(solution)/shard_map/ppermute | solution.py:347
  7.8 0.2 collective-permute-start.3
  8.0 2.3 %shard_map.95 = (f32[512,512]{1,0:T(8,128)S(1)}, bf16[512,1024]{1,0:T(8,128)(2,1)S(1)}, f32[512,256]{1,0:T(8,128)S(1)}, bf16[1,512,128]{2,1,0:T(8,128)(2,1)S(1)}) custom-call(bf16[512,512]{1,0:T(8,128)(2,1)S(1)} %get-tuple-element.39.query_ref, bf16[512,512]{1,0:T(8,128)(2,1)S(1)} %get-tuple-element.40.key_ref, ...), custom_call_target="tpu_custom_call" | custom-call | flops 268435456 | bytes 4358144 | tf_op jit(solution)/shard_map/pallas_call | solution.py:38
  10.3 1.7 %collective-permute-done.1.refs_0_.refs_2_.refs_7_ = bf16[512,128]{1,0:T(8,128)(2,1)S(1)} collective-permute-done((bf16[512,128]{1,0:T(8,128)(2,1)S(1)}, bf16[512,128]{1,0:T(8,128)(2,1)S(1)}, u32[]{:S(2)}, u32[]{:S(2)}) %collective-permute-start.1) | collective-permute-done | bytes 131104 | tf_op jit(solution)/shard_map/ppermute | solution.py:347
  11.9 0.3 %shard_map.97.refs_0_ = f32[512,512]{1,0:T(8,128)S(1)} custom-call(s32[1]{0:T(128)} %bitcast.spot_ref, f32[512,512]{1,0:T(8,128)S(1)} %get-tuple-element.54.mixed_ref, bf16[512,1024]{1,0:T(8,128)(2,1)S(1)} %get-tuple-element.44.weighted_ref.refs_1_, bf16[512,128]{1,0:T(8,128)(2,1)S(1)} %collective-permute-done.1.refs_0_.refs_2_.refs_7_), custom_call_target="tpu_custom_call" | custom-call | flops 67108864 | bytes 3276804 | tf_op jit(solution)/shard_map/pallas_call | solution.py:38
  12.2 0.1 collective-permute-start.2
  12.3 0.5 %collective-permute-start.7 = (bf16[512,1024]{1,0:T(8,128)(2,1)S(1)}, bf16[512,1024]{1,0:T(8,128)(2,1)S(1)}, u32[]{:S(2)}, u32[]{:S(2)}) collective-permute-start(bf16[512,1024]{1,0:T(8,128)(2,1)S(1)} %get-tuple-element.44.weighted_ref.refs_1_), channel_id=1, source_target_pairs={{0,1},{1,0},{2,3},{3,2},{4,5},{5,4},{6,7},{7,6},{8,9},{9,8},{10,11... | collective-permute-start | bytes 3145736 | tf_op jit(solution)/shard_map/ppermute | solution.py:411
  12.8 1.8 %collective-permute-start.4 = (bf16[256,128]{1,0:T(8,128)(2,1)S(1)}, bf16[256,128]{1,0:T(8,128)(2,1)S(1)}, u32[]{:S(2)}, u32[]{:S(2)}) collective-permute-start(bf16[256,128]{1,0:T(8,128)(2,1)S(1)} %get-tuple-element.65), channel_id=1, source_target_pairs={{0,4},{4,0},{8,12},{12,8},{1,5},{5,1},{9,13},{13,9},{2,6},{6,2},{1... | collective-permute-start | bytes 196616 | tf_op jit(solution)/shard_map/ppermute | solution.py:347
  14.6 2.5 %collective-permute-done.4.b_ref = bf16[256,128]{1,0:T(8,128)(2,1)S(1)} collective-permute-done((bf16[256,128]{1,0:T(8,128)(2,1)S(1)}, bf16[256,128]{1,0:T(8,128)(2,1)S(1)}, u32[]{:S(2)}, u32[]{:S(2)}) %collective-permute-start.4) | collective-permute-done | bytes 65568 | tf_op jit(solution)/shard_map/ppermute | solution.py:347
  17.2 2.8 %collective-permute-start.5 = (bf16[256,128]{1,0:T(8,128)(2,1)S(1)}, bf16[256,128]{1,0:T(8,128)(2,1)S(1)}, u32[]{:S(2)}, u32[]{:S(2)}) collective-permute-start(bf16[256,128]{1,0:T(8,128)(2,1)S(1)} %shard_map.101), channel_id=1, source_target_pairs={{0,8},{4,12},{8,0},{12,4},{1,9},{5,13},{9,1},{13,5},{2,10},{6,14},... | collective-permute-start | bytes 196616 | tf_op jit(solution)/shard_map/ppermute | solution.py:347
  20.0 1.3 %collective-permute-start.6 = (bf16[256,128]{1,0:T(8,128)(2,1)S(1)}, bf16[256,128]{1,0:T(8,128)(2,1)S(1)}, u32[]{:S(2)}, u32[]{:S(2)}) collective-permute-start(bf16[256,128]{1,0:T(8,128)(2,1)S(1)} %shard_map.101), channel_id=1, source_target_pairs={{0,12},{4,8},{8,4},{12,0},{1,13},{5,9},{9,5},{13,1},{2,14},{6,10},... | collective-permute-start | bytes 196616 | tf_op jit(solution)/shard_map/ppermute | solution.py:359
  21.3 2.5 %shard_map.96 = (f32[512,512]{1,0:T(8,128)S(1)}, f32[512,512]{1,0:T(8,128)S(1)}, f32[512,512]{1,0:T(8,128)S(1)}) custom-call(bf16[512,512]{1,0:T(8,128)(2,1)S(1)} %get-tuple-element.39.query_ref, bf16[512,512]{1,0:T(8,128)(2,1)S(1)} %get-tuple-element.40.key_ref, bf16[512,512]{1,0:T(8,128)(2,1)S(1)} %get-tuple-element.41.value_ref, ...), custom_call_target="tpu_custom_call" | custom-call | flops 536870912 | bytes 6979584 | tf_op jit(solution)/shard_map/pallas_call | solution.py:38
  23.9 0.0 collective-permute-done.5.same_ref
  23.9 2.2 %collective-permute-done.6.cross_ref = bf16[256,128]{1,0:T(8,128)(2,1)S(1)} collective-permute-done((bf16[256,128]{1,0:T(8,128)(2,1)S(1)}, bf16[256,128]{1,0:T(8,128)(2,1)S(1)}, u32[]{:S(2)}, u32[]{:S(2)}) %collective-permute-start.6) | collective-permute-done | bytes 65568 | tf_op jit(solution)/shard_map/ppermute | solution.py:359
  26.1 0.1 collective-permute-start.8
  26.2 1.1 %shard_map.98 = (f32[512,512]{1,0:T(8,128)S(1)}, f32[512,1024]{1,0:T(8,128)S(1)}, bf16[512,512]{1,0:T(8,128)(2,1)S(1)}, bf16[512,512]{1,0:T(8,128)(2,1)S(1)}) custom-call(s32[1]{0:T(128)} %bitcast.spot_ref, f32[512,512]{1,0:T(8,128)S(1)} %get-tuple-element.53.dq_ref, f32[512,512]{1,0:T(8,128)S(1)} %get-tuple-element.51.dk_ref, ...), custom_call_target="tpu_custom_call" | custom-call | flops 603979776 | bytes 11173892 | tf_op jit(solution)/shard_map/pallas_call | solution.py:38
  27.2 0.0 collective-permute-done.2.base_ref
  27.3 0.7 %shard_map.99 = (bf16[512,1024]{1,0:T(8,128)(2,1)S(1)}, bf16[512,512]{1,0:T(8,128)(2,1)S(1)}) custom-call(s32[1]{0:T(128)} %bitcast.spot_ref, f32[512,1024]{1,0:T(8,128)S(1)} %get-tuple-element.58.part_ref, f32[512,512]{1,0:T(8,128)S(1)} %collective-permute-done.2.base_ref, bf16[512,1024]{1,0:T(8,128)(2,1)S(1)} %collective-permute-done.3.weight_ref, ...), custom_call_target="tpu_custom_call" | custom-call | flops 536870912 | bytes 6815748 | tf_op jit(solution)/shard_map/pallas_call | solution.py:38
  28.0 1.5 %shard_map.103 = (bf16[512,1024]{1,0:T(8,128)(2,1)}, bf16[512,512]{1,0:T(8,128)(2,1)}, bf16[512,512]{1,0:T(8,128)(2,1)}, bf16[512,512]{1,0:T(8,128)(2,1)}, f32[5...) custom-call(s32[1]{0:T(128)} %bitcast.spot_ref, f32[512,512]{1,0:T(8,128)S(1)} %get-tuple-element.51.dk_ref, ...), custom_call_target="tpu_custom_call" | custom-call | flops 738197504 | bytes 16023556 | tf_op jit(solution)/shard_map/pallas_call | solution.py:38
  29.5 0.0 collective-permute-done.7.weighted_ref
  29.6 0.1 shard_map.104
  (6 shorter events, 0.1 us)
Async XLA Ops:
  0.6 3.4 %collective-permute-start = (bf16[512,1024]{1,0:T(8,128)(2,1)}, bf16[512,1024]{1,0:T(8,128)(2,1)S(1)}, u32[]{:S(2)}, u32[]{:S(2)}) collective-permute-start(bf16[512,1024]{1,0:T(8,128)(2,1)} %bitcast.13), channel_id=1, source_target_pairs={{0,1},{1,0},{2,3},{3,2},{4,5},{5,4},{6,7},{7,6},{8,9},{9,8},{10,11... | collective-permute-start | bytes 3145736 | tf_op jit(solution)/shard_map/ppermute | solution.py:392
  5.1 6.8 %collective-permute-start.1 = (bf16[512,128]{1,0:T(8,128)(2,1)S(1)}, bf16[512,128]{1,0:T(8,128)(2,1)S(1)}, u32[]{:S(2)}, u32[]{:S(2)}) collective-permute-start(bf16[512,128]{1,0:T(8,128)(2,1)S(1)} %get-tuple-element.55), channel_id=1, source_target_pairs={{0,4},{4,0},{8,12},{12,8},{1,5},{5,1},{9,13},{13,9},{2,6},{6,2},{1... | collective-permute-start | bytes 393224 | tf_op jit(solution)/shard_map/ppermute | solution.py:347
  7.8 19.5 %collective-permute-start.3 = (bf16[512,1024]{1,0:T(8,128)(2,1)S(1)}, bf16[512,1024]{1,0:T(8,128)(2,1)S(1)}, u32[]{:S(2)}, u32[]{:S(2)}) collective-permute-start(bf16[512,1024]{1,0:T(8,128)(2,1)S(1)} %get-tuple-element.42.weight_ref), channel_id=1, source_target_pairs={{0,1},{1,0},{2,3},{3,2},{4,5},{5,4},{6,7},{7,6},{8,9},{9,8},{10,11... | collective-permute-start | bytes 3145736 | tf_op jit(solution)/shard_map/ppermute | solution.py:410
  12.2 15.0 %collective-permute-start.2 = (f32[512,512]{1,0:T(8,128)S(1)}, f32[512,512]{1,0:T(8,128)S(1)}, u32[]{:S(2)}, u32[]{:S(2)}) collective-permute-start(f32[512,512]{1,0:T(8,128)S(1)} %shard_map.97.refs_0_), channel_id=1, source_target_pairs={{0,1},{1,0},{2,3},{3,2},{4,5},{5,4},{6,7},{7,6},{8,9},{9,8},{10,11... | collective-permute-start | bytes 3145736 | tf_op jit(solution)/shard_map/ppermute | solution.py:433
  12.3 17.2 %collective-permute-start.7 = (bf16[512,1024]{1,0:T(8,128)(2,1)S(1)}, bf16[512,1024]{1,0:T(8,128)(2,1)S(1)}, u32[]{:S(2)}, u32[]{:S(2)}) collective-permute-start(bf16[512,1024]{1,0:T(8,128)(2,1)S(1)} %get-tuple-element.44.weighted_ref.refs_1_), channel_id=1, source_target_pairs={{0,1},{1,0},{2,3},{3,2},{4,5},{5,4},{6,7},{7,6},{8,9},{9,8},{10,11... | collective-permute-start | bytes 3145736 | tf_op jit(solution)/shard_map/ppermute | solution.py:411
  12.8 4.3 %collective-permute-start.4 = (bf16[256,128]{1,0:T(8,128)(2,1)S(1)}, bf16[256,128]{1,0:T(8,128)(2,1)S(1)}, u32[]{:S(2)}, u32[]{:S(2)}) collective-permute-start(bf16[256,128]{1,0:T(8,128)(2,1)S(1)} %get-tuple-element.65), channel_id=1, source_target_pairs={{0,4},{4,0},{8,12},{12,8},{1,5},{5,1},{9,13},{13,9},{2,6},{6,2},{1... | collective-permute-start | bytes 196616 | tf_op jit(solution)/shard_map/ppermute | solution.py:347
  17.2 6.7 %collective-permute-start.5 = (bf16[256,128]{1,0:T(8,128)(2,1)S(1)}, bf16[256,128]{1,0:T(8,128)(2,1)S(1)}, u32[]{:S(2)}, u32[]{:S(2)}) collective-permute-start(bf16[256,128]{1,0:T(8,128)(2,1)S(1)} %shard_map.101), channel_id=1, source_target_pairs={{0,8},{4,12},{8,0},{12,4},{1,9},{5,13},{9,1},{13,5},{2,10},{6,14},... | collective-permute-start | bytes 196616 | tf_op jit(solution)/shard_map/ppermute | solution.py:347
  20.0 6.1 %collective-permute-start.6 = (bf16[256,128]{1,0:T(8,128)(2,1)S(1)}, bf16[256,128]{1,0:T(8,128)(2,1)S(1)}, u32[]{:S(2)}, u32[]{:S(2)}) collective-permute-start(bf16[256,128]{1,0:T(8,128)(2,1)S(1)} %shard_map.101), channel_id=1, source_target_pairs={{0,12},{4,8},{8,4},{12,0},{1,13},{5,9},{9,5},{13,1},{2,14},{6,10},... | collective-permute-start | bytes 196616 | tf_op jit(solution)/shard_map/ppermute | solution.py:359
  26.1 3.5 %collective-permute-start.8 = (bf16[512,128]{1,0:T(8,128)(2,1)S(1)}, bf16[512,128]{1,0:T(8,128)(2,1)S(1)}, u32[]{:S(2)}, u32[]{:S(2)}) collective-permute-start(bf16[512,128]{1,0:T(8,128)(2,1)S(1)} %shard_map.102.refs_8_), channel_id=1, source_target_pairs={{0,1},{1,0},{2,3},{3,2},{4,5},{5,4},{6,7},{7,6},{8,9},{9,8},{10,11... | collective-permute-start | bytes 393224 | tf_op jit(solution)/shard_map/ppermute | solution.py:448
